TPU v7x, 32 devices: a whole 2x2x4 slice. The times are simulated.
32 devices in a mesh: dom: 16 (over z, y, x), segment: 2 (over core).
Axes of the slice: x: 2, y: 2, z: 4, core: 2. Of those that a mesh axis runs over, the one named last changes fastest.
Arguments:
- feats: bfloat16 [4096, 512], P('dom'), may hold values from -6 to 6
- adj_local: bfloat16 [4096, 256], P('dom'), as said below
- couple: bfloat16 [4096, 256], P('dom'), as said below
- send_rows: int32 [16, 256], P('dom'), may hold values from 0 to 255, as said below
- weights: bfloat16 [1024, 512], P('segment'), may hold values from -0.25 to 0.25
- cotangent: bfloat16 [4096, 512], P('dom'), may hold values from -1.5 to 1.5
Outputs:
- acts: bfloat16 [2, 4096, 512], P('segment', 'dom')
- grad_weights: float32 [2, 512, 512], P('segment', 'dom')
- grad_feats: float32 [4096, 512], P('dom', 'segment')
Inputs may be any that keep to these rules, and one draw needn't show every extreme that they name: `adj_local`: entries are non-negative. `couple`: entries are non-negative. `send_rows`: the 128 local indices that a partition sends in one round are distinct.
All inputs are finite; a program needn't handle non-finite values.
Results may differ from a plain program's by a relative error of at most 0.013.
Values may be sent and summed in bfloat16 or wider, within the bound.
No kernel may reach another device: no remote copies, remote signals or barrier semaphores. Data moves between devices by JAX's collectives and lax.ppermute only.
A program may use at most 64 MiB of HBM per device.

v0:
```python
import jax
import jax.numpy as jnp
from jax import lax
from jax.sharding import PartitionSpec as P

RESIDUAL_SHARE = 0.1
BETA_SCALE = 0.5


def partner(x, axis, bit):
    return lax.ppermute(x, axis, [(i, i ^ 1 << bit) for i in range(lax.axis_size(axis))])


def passed_along(block, axis, distance):
    devices = range(lax.axis_size(axis))
    route = [(i - distance, i) for i in devices if i - distance in devices]
    return lax.ppermute(block, axis, route)


def far_bit_of():
    return lax.axis_size("dom").bit_length() - 2


def forward_layer(inputs, first_acts, weight, beta_coef, adjacency, coupling, sending):
    half_rows = sending.shape[0] // 2
    outgoing = inputs[sending]
    near_in = partner(outgoing[:half_rows], "dom", 0)
    far_in = partner(outgoing[half_rows:], "dom", far_bit_of())
    incoming = jnp.concatenate([near_in, far_in], axis=0)
    aggregate = jnp.dot(adjacency, inputs, preferred_element_type=jnp.float32)
    aggregate = aggregate + jnp.dot(coupling, incoming, preferred_element_type=jnp.float32)
    share = RESIDUAL_SHARE
    mixed = ((1.0 - share) * aggregate + share * first_acts.astype(jnp.float32)).astype(
        jnp.bfloat16
    )
    preact = (1.0 - beta_coef) * mixed.astype(jnp.float32) + beta_coef * jnp.dot(
        mixed, weight, preferred_element_type=jnp.float32
    )
    return (jax.nn.silu(preact).astype(jnp.bfloat16), mixed, preact)


def backward_layer(upstream, preact, weight, beta_coef, adjacency, coupling, sending):
    half_rows = sending.shape[0] // 2
    share = RESIDUAL_SHARE
    sigmoid_z = jax.nn.sigmoid(preact)
    slope = sigmoid_z * (1.0 + preact * (1.0 - sigmoid_z))
    grad_pre = (upstream.astype(jnp.float32) * slope).astype(jnp.bfloat16)
    through = lax.dot_general(
        grad_pre, weight, (((1,), (1,)), ((), ())), preferred_element_type=jnp.float32
    )
    grad_mix = ((1.0 - beta_coef) * grad_pre.astype(jnp.float32) + beta_coef * through).astype(
        jnp.bfloat16
    )
    backward_rows = (
        (1.0 - share)
        * jnp.einsum("ik,ih->kh", coupling, grad_mix, preferred_element_type=jnp.float32)
    ).astype(jnp.bfloat16)
    near_back = partner(backward_rows[:half_rows], "dom", 0)
    far_back = partner(backward_rows[half_rows:], "dom", far_bit_of())
    returned = jnp.concatenate([near_back, far_back], axis=0)
    row_ids = jnp.arange(adjacency.shape[0], dtype=jnp.int32)
    placing = (row_ids[:, None] == sending[None, :]).astype(jnp.bfloat16)
    grad_full = (1.0 - share) * jnp.einsum(
        "ji,jh->ih", adjacency, grad_mix, preferred_element_type=jnp.float32
    )
    grad_full = grad_full + jnp.dot(placing, returned, preferred_element_type=jnp.float32)
    return (grad_full, grad_pre, grad_mix)


def on_device(feats, adj_local, couple, send_rows, weights, cotangent):
    segment_index = lax.axis_index("segment")
    segments = lax.axis_size("segment")
    sending = send_rows[0]
    share = RESIDUAL_SHARE
    beta_own = jnp.log(BETA_SCALE / (segment_index.astype(jnp.float32) + 1.0) + 1.0)
    zero_acts = jnp.zeros_like(feats)

    def forward_turn(turn_no, state):
        current, kept_mix, kept_pre, kept_out = state
        output, mixed, preact = forward_layer(
            current, feats, weights, beta_own, adj_local, couple, sending
        )
        is_active = turn_no == segment_index
        kept = (
            jnp.where(is_active, mixed, kept_mix),
            jnp.where(is_active, preact, kept_pre),
            jnp.where(is_active, output, kept_out),
        )
        return (output, kept)

    def forward_loop(turn_no, state):
        output, kept = forward_turn(turn_no, state)
        return (passed_along(output, "segment", 1),) + kept

    start_fwd = (
        jnp.where(segment_index == 0, feats, zero_acts),
        zero_acts,
        jnp.zeros(feats.shape, jnp.float32),
        zero_acts,
    )
    state_fwd = lax.fori_loop(0, segments - 1, forward_loop, start_fwd)
    unused_out, (kept_mix, kept_pre, acts) = forward_turn(segments - 1, state_fwd)

    def backward_turn(turn_no, state):
        upstream, kept_pre_grad, kept_mix_grad, kept_full = state
        grad_full, grad_pre, grad_mix = backward_layer(
            upstream, kept_pre, weights, beta_own, adj_local, couple, sending
        )
        is_active = segments - 1 - turn_no == segment_index
        kept = (
            jnp.where(is_active, grad_pre, kept_pre_grad),
            jnp.where(is_active, grad_mix, kept_mix_grad),
            jnp.where(is_active, grad_full, kept_full),
        )
        return (grad_full, kept)

    def backward_loop(turn_no, state):
        grad_full, kept = backward_turn(turn_no, state)
        return (passed_along(grad_full.astype(jnp.bfloat16), "segment", -1),) + kept

    start_bwd = (
        jnp.where(segment_index == segments - 1, cotangent, zero_acts),
        zero_acts,
        zero_acts,
        jnp.zeros(feats.shape, jnp.float32),
    )
    state_bwd = lax.fori_loop(0, segments - 1, backward_loop, start_bwd)
    unused_grad, (own_grad_pre, own_grad_mix, own_full) = backward_turn(segments - 1, state_bwd)
    feat_term = share * own_grad_mix.astype(jnp.float32) + jnp.where(
        segment_index == 0, own_full, jnp.zeros_like(own_full)
    )
    feat_grads = lax.psum_scatter(
        feat_term.astype(jnp.bfloat16), "segment", scatter_dimension=1, tiled=True
    ).astype(jnp.float32)
    weight_grads = lax.psum_scatter(
        beta_own
        * jnp.einsum("nh,nk->hk", kept_mix, own_grad_pre, preferred_element_type=jnp.float32),
        "dom",
        scatter_dimension=0,
        tiled=True,
    )
    return (acts[None], weight_grads[None], feat_grads)


def solution(mesh):
    in_specs = (
        P("dom", None),
        P("dom", None),
        P("dom", None),
        P("dom", None),
        P("segment", None),
        P("dom", None),
    )
    out_specs = (P("segment", "dom", None), P("segment", "dom", None), P("dom", "segment"))
    return jax.shard_map(
        on_device, mesh=mesh, in_specs=in_specs, out_specs=out_specs, check_vma=False
    )
```

profile of v0, /device:TPU:0, one launch (start us, length us, event | category | flops | bytes accessed | tf_op | source)
XLA Modules:
  0.0 158.8 jit_solution(11724324333304337583)
XLA Ops:
  7.2 0.7 copy-done.5
  8.0 1.1 copy.22
  9.2 1.2 gather_fusion
  10.4 3.0 %collective-permute-start = (bf16[128,512]{1,0:T(8,128)(2,1)S(1)}, bf16[128,512]{1,0:T(8,128)(2,1)S(1)}, u32[]{:S(2)}, u32[]{:S(2)}) collective-permute-start(bf16[128,512]{1,0:T(8,128)(2,1)S(1)} %get-tuple-element.80), channel_id=1, source_target_pairs={{0,2},{2,0},{4,6},{6,4},{8,10},{10,8},{12,14},{14,12},{16,18},{18,... | collective-permute-start | bytes 393224 | tf_op jit(solution)/shard_map/while/body/eval_jaxpr/ppermute | solution.py:11
  13.5 2.6 %collective-permute-start.1 = (bf16[128,512]{1,0:T(8,128)(2,1)S(1)}, bf16[128,512]{1,0:T(8,128)(2,1)S(1)}, u32[]{:S(2)}, u32[]{:S(2)}) collective-permute-start(bf16[128,512]{1,0:T(8,128)(2,1)S(1)} %get-tuple-element.81), channel_id=1, source_target_pairs={{0,16},{2,18},{4,20},{6,22},{8,24},{10,26},{12,28},{14,30},{16,0},... | collective-permute-start | bytes 393224 | tf_op jit(solution)/shard_map/while/body/eval_jaxpr/ppermute | solution.py:11
  16.4 0.5 collective-permute-done
  17.0 5.2 %collective-permute-done.1 = bf16[128,512]{1,0:T(8,128)(2,1)S(1)} collective-permute-done((bf16[128,512]{1,0:T(8,128)(2,1)S(1)}, bf16[128,512]{1,0:T(8,128)(2,1)S(1)}, u32[]{:S(2)}, u32[]{:S(2)}) %collective-permute-start.1) | collective-permute-done | bytes 131104 | tf_op jit(solution)/shard_map/while/body/eval_jaxpr/ppermute | solution.py:11
  22.4 0.4 multiply_convert_fusion.3
  22.8 1.3 collective-permute-start.2
  24.1 1.1 collective-permute-done.2
  25.4 1.2 gather_fusion.1
  26.6 0.5 collective-permute-start.3
  27.2 0.4 copy-done.4
  27.7 4.8 %collective-permute-done.3 = bf16[128,512]{1,0:T(8,128)(2,1)S(1)} collective-permute-done((bf16[128,512]{1,0:T(8,128)(2,1)S(1)}, bf16[128,512]{1,0:T(8,128)(2,1)S(1)}, u32[]{:S(2)}, u32[]{:S(2)}) %collective-permute-start.3) | collective-permute-done | bytes 131104 | tf_op jit(solution)/shard_map/ppermute | solution.py:11
  32.4 3.9 %collective-permute-done.4 = bf16[128,512]{1,0:T(8,128)(2,1)S(1)} collective-permute-done((bf16[128,512]{1,0:T(8,128)(2,1)S(1)}, bf16[128,512]{1,0:T(8,128)(2,1)S(1)}, u32[]{:S(2)}, u32[]{:S(2)}) %collective-permute-start.4) | collective-permute-done | bytes 131104 | tf_op jit(solution)/shard_map/ppermute | solution.py:11
  36.9 0.5 add_multiply_fusion
  37.4 0.3 fusion.13
  38.0 1.6 %collective-permute-start.5 = (bf16[128,512]{0,1:T(8,128)(2,1)S(1)}, bf16[128,512]{0,1:T(8,128)(2,1)S(1)}, u32[]{:S(2)}, u32[]{:S(2)}) collective-permute-start(bf16[128,512]{0,1:T(8,128)(2,1)S(1)} %get-tuple-element.63), channel_id=1, source_target_pairs={{0,2},{2,0},{4,6},{6,4},{8,10},{10,8},{12,14},{14,12},{16,18},{18,... | collective-permute-start | bytes 393224 | tf_op jit(solution)/shard_map/while/body/eval_jaxpr/ppermute | solution.py:11
  39.8 3.2 %collective-permute-done.5 = bf16[128,512]{0,1:T(8,128)(2,1)S(1)} collective-permute-done((bf16[128,512]{0,1:T(8,128)(2,1)S(1)}, bf16[128,512]{0,1:T(8,128)(2,1)S(1)}, u32[]{:S(2)}, u32[]{:S(2)}) %collective-permute-start.5) | collective-permute-done | bytes 131104 | tf_op jit(solution)/shard_map/while/body/eval_jaxpr/ppermute | solution.py:11
  43.0 3.6 %collective-permute-done.6 = bf16[128,512]{0,1:T(8,128)(2,1)S(1)} collective-permute-done((bf16[128,512]{0,1:T(8,128)(2,1)S(1)}, bf16[128,512]{0,1:T(8,128)(2,1)S(1)}, u32[]{:S(2)}, u32[]{:S(2)}) %collective-permute-start.6) | collective-permute-done | bytes 131104 | tf_op jit(solution)/shard_map/while/body/eval_jaxpr/ppermute | solution.py:11
  46.6 1.1 fusion.54
  47.8 1.3 collective-permute-start.7
  49.1 2.3 %collective-permute-done.7 = bf16[256,512]{0,1:T(8,128)(2,1)S(1)} collective-permute-done((bf16[256,512]{0,1:T(8,128)(2,1)}, bf16[256,512]{0,1:T(8,128)(2,1)S(1)}, u32[]{:S(2)}, u32[]{:S(2)}) %collective-permute-start.7) | collective-permute-done | bytes 262176 | tf_op jit(solution)/shard_map/while/body/eval_jaxpr/ppermute | solution.py:17
  52.0 0.6 collective-permute-start.8
  52.8 4.8 %collective-permute-done.8 = bf16[128,512]{0,1:T(8,128)(2,1)S(1)} collective-permute-done((bf16[128,512]{0,1:T(8,128)(2,1)S(1)}, bf16[128,512]{0,1:T(8,128)(2,1)S(1)}, u32[]{:S(2)}, u32[]{:S(2)}) %collective-permute-start.8) | collective-permute-done | bytes 131104 | tf_op jit(solution)/shard_map/ppermute | solution.py:11
  57.6 3.4 %collective-permute-done.9 = bf16[128,512]{0,1:T(8,128)(2,1)S(1)} collective-permute-done((bf16[128,512]{0,1:T(8,128)(2,1)S(1)}, bf16[128,512]{0,1:T(8,128)(2,1)S(1)}, u32[]{:S(2)}, u32[]{:S(2)}) %collective-permute-start.9) | collective-permute-done | bytes 131104 | tf_op jit(solution)/shard_map/ppermute | solution.py:11
  61.1 1.0 fusion.16
  62.2 1.4 convolution_multiply_fusion
  63.8 0.8 copy.33
  64.6 4.7 %reduce-scatter.5.cloned.1.call-done = bf16[256,256]{0,1:T(8,128)(2,1)} async-done(((bf16[256,512]{0,1:T(8,128)(2,1)}), bf16[256,256]{0,1:T(8,128)(2,1)}) %reduce-scatter.5.cloned.1.call-update) | async-done | bytes 131088 | tf_op jit(solution)/shard_map/reduce_scatter | solution.py:132
  69.4 1.7 %copy.34 = f32[256,256]{1,0:T(8,128)} copy(bf16[256,256]{0,1:T(8,128)(2,1)} %reduce-scatter.5.cloned.1.call-done) | data formatting | bytes 393216
  71.1 80.9 %reduce-scatter.3.cloned.1.call-done = f32[32,512]{1,0:T(8,128)} async-done(((f32[512,512]{1,0:T(8,128)}), f32[32,512]{1,0:T(8,128)}) %reduce-scatter.3.cloned.1.call-update) | async-done | bytes 65552 | tf_op jit(solution)/shard_map/reduce_scatter | solution.py:135
  (37 shorter events, 3.1 us)
Async XLA Ops:
  7.2 15.3 %copy-start = (bf16[512,512]{1,0:T(8,128)(2,1)S(1)}, bf16[512,512]{1,0:T(8,128)(2,1)}, u32[]{:S(2)}) copy-start(bf16[512,512]{1,0:T(8,128)(2,1)} %param.10) | copy-start | bytes 1572868
  7.2 62.2 %reduce-scatter.5.cloned.1.call-start = ((), (), s32[]{:S(2)}) async-start(), calls=%async_computation.3 | async-start | bytes 393216 | tf_op jit(solution)/shard_map/reduce_scatter | solution.py:132
  7.2 0.7 copy-start.5
  10.4 5.8 %copy-start.2 = (bf16[256,256]{1,0:T(8,128)(2,1)S(1)}, bf16[256,256]{1,0:T(8,128)(2,1)}, u32[]{:S(2)}) copy-start(bf16[256,256]{1,0:T(8,128)(2,1)} %param.7) | copy-start | bytes 393220
  10.4 6.5 %collective-permute-start = (bf16[128,512]{1,0:T(8,128)(2,1)S(1)}, bf16[128,512]{1,0:T(8,128)(2,1)S(1)}, u32[]{:S(2)}, u32[]{:S(2)}) collective-permute-start(bf16[128,512]{1,0:T(8,128)(2,1)S(1)} %get-tuple-element.80), channel_id=1, source_target_pairs={{0,2},{2,0},{4,6},{6,4},{8,10},{10,8},{12,14},{14,12},{16,18},{18,... | collective-permute-start | bytes 393224 | tf_op jit(solution)/shard_map/while/body/eval_jaxpr/ppermute | solution.py:11
  13.5 8.7 %collective-permute-start.1 = (bf16[128,512]{1,0:T(8,128)(2,1)S(1)}, bf16[128,512]{1,0:T(8,128)(2,1)S(1)}, u32[]{:S(2)}, u32[]{:S(2)}) collective-permute-start(bf16[128,512]{1,0:T(8,128)(2,1)S(1)} %get-tuple-element.81), channel_id=1, source_target_pairs={{0,16},{2,18},{4,20},{6,22},{8,24},{10,26},{12,28},{14,30},{16,0},... | collective-permute-start | bytes 393224 | tf_op jit(solution)/shard_map/while/body/eval_jaxpr/ppermute | solution.py:11
  16.2 6.0 %copy-start.1 = (bf16[256,256]{1,0:T(8,128)(2,1)S(1)}, bf16[256,256]{1,0:T(8,128)(2,1)}, u32[]{:S(2)}) copy-start(bf16[256,256]{1,0:T(8,128)(2,1)} %param.8) | copy-start | bytes 393220
  22.8 2.4 %collective-permute-start.2 = (bf16[256,512]{0,1:T(8,128)(2,1)S(1)}, bf16[256,512]{0,1:T(8,128)(2,1)S(1)}, u32[]{:S(2)}, u32[]{:S(2)}) collective-permute-start(bf16[256,512]{0,1:T(8,128)(2,1)S(1)} %get-tuple-element.82), channel_id=1, source_target_pairs={{0,1},{2,3},{4,5},{6,7},{8,9},{10,11},{12,13},{14,15},{16,17},{18,... | collective-permute-start | bytes 786440 | tf_op jit(solution)/shard_map/while/body/eval_jaxpr/ppermute | solution.py:17
  26.6 1.0 copy-start.4
  26.6 5.8 %collective-permute-start.3 = (bf16[128,512]{1,0:T(8,128)(2,1)S(1)}, bf16[128,512]{1,0:T(8,128)(2,1)S(1)}, u32[]{:S(2)}, u32[]{:S(2)}) collective-permute-start(bf16[128,512]{1,0:T(8,128)(2,1)S(1)} %get-tuple-element.78), channel_id=1, source_target_pairs={{0,2},{2,0},{4,6},{6,4},{8,10},{10,8},{12,14},{14,12},{16,18},{18,... | collective-permute-start | bytes 393224 | tf_op jit(solution)/shard_map/ppermute | solution.py:11
  27.1 9.2 %collective-permute-start.4 = (bf16[128,512]{1,0:T(8,128)(2,1)S(1)}, bf16[128,512]{1,0:T(8,128)(2,1)S(1)}, u32[]{:S(2)}, u32[]{:S(2)}) collective-permute-start(bf16[128,512]{1,0:T(8,128)(2,1)S(1)} %get-tuple-element.79), channel_id=1, source_target_pairs={{0,16},{2,18},{4,20},{6,22},{8,24},{10,26},{12,28},{14,30},{16,0},... | collective-permute-start | bytes 393224 | tf_op jit(solution)/shard_map/ppermute | solution.py:11
  38.0 5.0 %collective-permute-start.5 = (bf16[128,512]{0,1:T(8,128)(2,1)S(1)}, bf16[128,512]{0,1:T(8,128)(2,1)S(1)}, u32[]{:S(2)}, u32[]{:S(2)}) collective-permute-start(bf16[128,512]{0,1:T(8,128)(2,1)S(1)} %get-tuple-element.63), channel_id=1, source_target_pairs={{0,2},{2,0},{4,6},{6,4},{8,10},{10,8},{12,14},{14,12},{16,18},{18,... | collective-permute-start | bytes 393224 | tf_op jit(solution)/shard_map/while/body/eval_jaxpr/ppermute | solution.py:11
  39.6 7.1 %collective-permute-start.6 = (bf16[128,512]{0,1:T(8,128)(2,1)S(1)}, bf16[128,512]{0,1:T(8,128)(2,1)S(1)}, u32[]{:S(2)}, u32[]{:S(2)}) collective-permute-start(bf16[128,512]{0,1:T(8,128)(2,1)S(1)} %get-tuple-element.64), channel_id=1, source_target_pairs={{0,16},{2,18},{4,20},{6,22},{8,24},{10,26},{12,28},{14,30},{16,0},... | collective-permute-start | bytes 393224 | tf_op jit(solution)/shard_map/while/body/eval_jaxpr/ppermute | solution.py:11
  47.8 3.6 %collective-permute-start.7 = (bf16[256,512]{0,1:T(8,128)(2,1)}, bf16[256,512]{0,1:T(8,128)(2,1)S(1)}, u32[]{:S(2)}, u32[]{:S(2)}) collective-permute-start(bf16[256,512]{0,1:T(8,128)(2,1)} %get-tuple-element.86), channel_id=1, source_target_pairs={{1,0},{3,2},{5,4},{7,6},{9,8},{11,10},{13,12},{15,14},{17,16},{19,... | collective-permute-start | bytes 786440 | tf_op jit(solution)/shard_map/while/body/eval_jaxpr/ppermute | solution.py:17
  52.0 9.1 %copy-start.3 = (f32[256,512]{0,1:T(8,128)S(1)}, f32[256,512]{0,1:T(8,128)}, u32[]{:S(2)}) copy-start(f32[256,512]{0,1:T(8,128)} %get-tuple-element.87) | copy-start | bytes 1572868
  52.0 5.6 %collective-permute-start.8 = (bf16[128,512]{0,1:T(8,128)(2,1)S(1)}, bf16[128,512]{0,1:T(8,128)(2,1)S(1)}, u32[]{:S(2)}, u32[]{:S(2)}) collective-permute-start(bf16[128,512]{0,1:T(8,128)(2,1)S(1)} %get-tuple-element.61), channel_id=1, source_target_pairs={{0,2},{2,0},{4,6},{6,4},{8,10},{10,8},{12,14},{14,12},{16,18},{18,... | collective-permute-start | bytes 393224 | tf_op jit(solution)/shard_map/ppermute | solution.py:11
  52.6 8.5 %collective-permute-start.9 = (bf16[128,512]{0,1:T(8,128)(2,1)S(1)}, bf16[128,512]{0,1:T(8,128)(2,1)S(1)}, u32[]{:S(2)}, u32[]{:S(2)}) collective-permute-start(bf16[128,512]{0,1:T(8,128)(2,1)S(1)} %get-tuple-element.62), channel_id=1, source_target_pairs={{0,16},{2,18},{4,20},{6,22},{8,24},{10,26},{12,28},{14,30},{16,0},... | collective-permute-start | bytes 393224 | tf_op jit(solution)/shard_map/ppermute | solution.py:11
  62.1 89.9 %reduce-scatter.3.cloned.1.call-start = ((), (), s32[]{:S(2)}) async-start(), calls=%async_computation.2 | async-start | bytes 1114112 | tf_op jit(solution)/shard_map/reduce_scatter | solution.py:135
Sparse Core Ops, SparseCore 0:
  62.2 7.0 reduce-scatter.4
  72.2 79.7 reduce-scatter.2
where the time goes:
time: 159 us
  waiting for transfers between devices  119 us (75%)
  between operations  14.4 us (9%)
  starting transfers between devices  11 us (7%)
  local copies, waits for them, and re-layouts  7.55 us (5%)
  matrix products  7.03 us (4%)
    reduce_scatter x1, waiting for transfers between devices, on_device(): lax.psum_scatter(beta_own * jnp.einsum('nh,nk->hk', kept_mix, own_grad_pr...  80.9 us
    ppermute x8, waiting for transfers between devices, partner(): lax.ppermute(x, axis, [(i, i ^ 1 << bit) for i in range(lax.axis_size(axi...  29.5 us
    ppermute x8, starting transfers between devices, partner(): lax.ppermute(x, axis, [(i, i ^ 1 << bit) for i in range(lax.axis_size(axi...  8.37 us
    unnamed x16, local copies, waits for them, and re-layouts  4.88 us
    reduce_scatter x1, waiting for transfers between devices, on_device(): lax.psum_scatter(feat_term.astype(jnp.bfloat16), 'segment', scatter_dimen...  4.71 us
    ppermute x2, waiting for transfers between devices, passed_along(): return lax.ppermute(block, axis, route)  3.47 us
  transfers between devices with their start and end apart: 12, of which 12 were waited for; matrix products, arithmetic and copies ran while one was open for 3% of the time, Pallas kernels for 0%

commit v1 on v0

v1 whole, which is shorter than its diff:
```python
import jax
import jax.numpy as jnp
from jax import lax
from jax.sharding import PartitionSpec as P

SHARE = 0.1
BETA_SCALE = 0.5
BF16 = jnp.bfloat16
F32 = jnp.float32


def swapped(x, mask):
    return lax.ppermute(x, "dom", [(i, i ^ mask) for i in range(lax.axis_size("dom"))])


def across(x, shift):
    n = lax.axis_size("segment")
    return lax.ppermute(x, "segment", [(i, (i + shift) % n) for i in range(n)])


def gathered(piece, seg):
    n = lax.axis_size("segment")
    if n == 1:
        return piece
    if n == 2:
        other = across(piece, 1)
        first = seg == 0
        return jnp.concatenate([jnp.where(first, piece, other), jnp.where(first, other, piece)], axis=0)
    parts = jnp.stack([piece] + [across(piece, n - k) for k in range(1, n)])
    order = (jnp.arange(n, dtype=jnp.int32) - seg) % n
    return parts[order].reshape((-1,) + piece.shape[1:])


def chosen(items, seg):
    out = items[0]
    for k in range(1, len(items)):
        out = jnp.where(seg == k, items[k], out)
    return out


def mm(a, b):
    return jnp.dot(a, b, preferred_element_type=F32)


def mm_t(a, b):
    return lax.dot_general(a, b, (((0,), (0,)), ((), ())), preferred_element_type=F32)


def on_device(feats, adj, couple, send_rows, weights, cot):
    seg = lax.axis_index("segment")
    layers = lax.axis_size("segment")
    n_dom = lax.axis_size("dom")
    top = n_dom // 2
    rows, width = feats.shape
    piece = rows // layers
    bound = couple.shape[1] // 2

    ac = jnp.concatenate([adj, couple], axis=1)
    sr_row = jnp.zeros((16, ac.shape[1]), BF16).at[0, : send_rows.shape[1]].set(send_rows[0].astype(BF16))
    ac_mine = jnp.concatenate([lax.dynamic_slice_in_dim(ac, seg * piece, piece, 0), sr_row], axis=0)
    f_mine = lax.dynamic_slice_in_dim(feats, seg * piece, piece, 0)
    c_mine = lax.dynamic_slice_in_dim(cot, seg * piece, piece, 0)

    fwd_mine = jnp.concatenate([f_mine, ac_mine], axis=0)
    far_fwd = swapped(fwd_mine, top)
    near_fwd = swapped(fwd_mine, 1)
    far_cot = swapped(c_mine, top)
    near_cot = swapped(c_mine, 1)
    diag_fwd = swapped(far_fwd, 1)
    diag_cot = swapped(far_cot, 1)

    all_w = gathered(weights, seg).reshape(layers, width, width)

    def spread(got):
        both = gathered(got[None], seg)
        f = both[:, :piece].reshape(rows, width)
        a = both[:, piece : 2 * piece].reshape(rows, -1)
        s = both[0, 2 * piece, : 2 * bound]
        return f, a, s

    own = (feats, ac, send_rows[0].astype(BF16))
    groups = [own] + [spread(g) for g in (near_fwd, far_fwd, diag_fwd)]
    x0 = [g[0] for g in groups]
    ids = lax.broadcasted_iota(jnp.int32, (2 * bound, rows), 1).astype(F32)
    picks = [(g[2].astype(F32)[:, None] == ids).astype(BF16) for g in groups]
    blocks = []
    for r in range(4):
        a = groups[r][1]
        near_blk = mm(a[:, rows : rows + bound], picks[r ^ 1][:bound]).astype(BF16)
        far_blk = mm(a[:, rows + bound :], picks[r ^ 2][bound:]).astype(BF16)
        blocks.append((a[:, :rows], near_blk, far_blk))

    betas = [jnp.log(BETA_SCALE / (jnp.float32(k) + 1.0) + 1.0) for k in range(layers)]
    xs = x0
    mixes, pres, outs = [], [], []
    for k in range(layers):
        mixed = []
        for r in range(4):
            own_b, near_b, far_b = blocks[r]
            agg = mm(own_b, xs[r]) + mm(near_b, xs[r ^ 1]) + mm(far_b, xs[r ^ 2])
            mixed.append(((1.0 - SHARE) * agg + SHARE * x0[r].astype(F32)).astype(BF16))
        pre = [(1.0 - betas[k]) * m.astype(F32) + betas[k] * mm(m, all_w[k]) for m in mixed]
        xs = [jax.nn.silu(p).astype(BF16) for p in pre]
        mixes.append(mixed)
        pres.append(pre)
        outs.append(xs[0])

    acts = chosen(outs, seg)

    ups = [cot] + [gathered(g, seg) for g in (near_cot, far_cot, diag_cot)]
    ups = [u.astype(BF16) for u in ups]
    others = n_dom // 4
    out_rows = width // n_dom
    dom = lax.axis_index("dom")
    low = dom & 1
    high = dom // top
    grads = []
    carried = jnp.zeros((rows, width), F32)
    full = None
    for k in range(layers - 1, -1, -1):
        dpre = []
        for r in range(4):
            sg = jax.nn.sigmoid(pres[k][r])
            slope = sg * (1.0 + pres[k][r] * (1.0 - sg))
            dpre.append((ups[r].astype(F32) * slope).astype(BF16))
        mix_all = jnp.concatenate(mixes[k], axis=0)
        cols = mix_all.reshape(4 * rows, 2, others, 2, out_rows)
        cols = lax.dynamic_index_in_dim(cols, high, 1, keepdims=False)
        cols = lax.dynamic_index_in_dim(cols, low, 2, keepdims=False)
        grads.append(betas[k] * mm_t(cols.reshape(4 * rows, others * out_rows), jnp.concatenate(dpre, axis=0)))
        dmix = [
            (
                (1.0 - betas[k]) * d.astype(F32)
                + betas[k] * lax.dot_general(d, all_w[k], (((1,), (1,)), ((), ())), preferred_element_type=F32)
            ).astype(BF16)
            for d in dpre
        ]
        carried = carried + SHARE * dmix[0].astype(F32)
        wanted = range(4) if k else range(1)
        full = [
            (1.0 - SHARE)
            * (mm_t(blocks[r][0], dmix[r]) + mm_t(blocks[r ^ 1][1], dmix[r ^ 1]) + mm_t(blocks[r ^ 2][2], dmix[r ^ 2]))
            for r in wanted
        ]
        ups = [f.astype(BF16) for f in full]

    total = full[0] + carried
    feat_grads = lax.dynamic_slice_in_dim(total, seg * (width // layers), width // layers, 1)

    part = chosen(grads[::-1], seg).reshape(others, out_rows, width)
    place = (dom // 2) % others
    wgrad = lax.dynamic_index_in_dim(part, place, 0, keepdims=False)
    for m in range(1, others):
        block = lax.dynamic_index_in_dim(part, place ^ m, 0, keepdims=False).astype(BF16)
        wgrad = wgrad + swapped(block, 2 * m).astype(F32)
    return (acts[None], wgrad[None], feat_grads)


def solution(mesh):
    in_specs = (
        P("dom", None),
        P("dom", None),
        P("dom", None),
        P("dom", None),
        P("segment", None),
        P("dom", None),
    )
    out_specs = (P("segment", "dom", None), P("segment", "dom", None), P("dom", "segment"))
    return jax.shard_map(on_device, mesh=mesh, in_specs=in_specs, out_specs=out_specs, check_vma=False)
```

time: 159 us -> 87.3 us (0.55)
  waiting for transfers between devices: 119 us -> 22.3 us
  matrix products: 7.03 us -> 32.9 us
  between operations: 14.4 us -> 1.64 us
  other arithmetic: 0.24 us -> 5.57 us
  starting transfers between devices: 11 us -> 15.1 us
  local copies, waits for them, and re-layouts: 7.55 us -> 9.27 us
    reduce_scatter x2 -> x0, waiting for transfers between devices: 85.6 us -> none  [the longest x1 80.9 us: on_device(): lax.psum_scatter(beta_own * jnp.einsum('nh,nk->hk', kept_mix, own_grad_pr...]
    dot_general x15 -> x62, matrix products: 7.03 us -> 32.9 us  [the longest x40 15.2 us: mm(): return jnp.dot(a, b, preferred_element_type=F32)]
    ppermute x10 -> x16, waiting for transfers between devices: 32.9 us -> 22.3 us  [the longest x9 20.2 us: swapped(): lax.ppermute(x, 'dom', [(i, i ^ mask) for i in range(lax.axis_size('dom'))])]
    ppermute x10 -> x16, starting transfers between devices: 11 us -> 15.1 us  [the longest x9 13.5 us: swapped(): lax.ppermute(x, 'dom', [(i, i ^ mask) for i in range(lax.axis_size('dom'))])]
    dynamic_slice x0 -> x3, local copies, waits for them, and re-layouts: none -> 2.68 us  [the longest x2 1.72 us: on_device(): cols = lax.dynamic_index_in_dim(cols, low, 2, keepdims=False)]
    gather x2 -> x0, local copies, waits for them, and re-layouts: 2.31 us -> none  [forward_layer(): outgoing = inputs[sending]]
    concatenate x0 -> x2, local copies, waits for them, and re-layouts: none -> 2.06 us  [on_device(): mix_all = jnp.concatenate(mixes[k], axis=0)]
    unnamed x16 -> x96, local copies, waits for them, and re-layouts: 4.88 us -> 4.51 us
  transfers between devices with their start and end apart: 12 -> 16, of which waited for: 12 -> 8; matrix products, arithmetic and copies ran while one was open for 3% -> 5% of each run, Pallas kernels for 0% -> 0%
where the time goes in v1:
time: 87.3 us; the launch traced here: 86.8 us
  matrix products  32.9 us (38%)
  waiting for transfers between devices  22.3 us (26%)
  starting transfers between devices  15.1 us (17%)
  local copies, waits for them, and re-layouts  9.27 us (11%)
  other arithmetic  5.57 us (6%)
  between operations  1.64 us (2%)
    ppermute x9, waiting for transfers between devices, swapped(): lax.ppermute(x, 'dom', [(i, i ^ mask) for i in range(lax.axis_size('dom'))])  20.2 us
    dot_general x40, matrix products, mm(): return jnp.dot(a, b, preferred_element_type=F32)  15.2 us
    dot_general x17, matrix products, mm_t(): lax.dot_general(a, b, (((0,), (0,)), ((), ())), preferred_element_type=F32)  14.6 us
    ppermute x9, starting transfers between devices, swapped(): lax.ppermute(x, 'dom', [(i, i ^ mask) for i in range(lax.axis_size('dom'))])  13.5 us
    unnamed x96, local copies, waits for them, and re-layouts  4.51 us
    dot_general x5, matrix products, on_device(): lax.dot_general(d, all_w[k], (((1,), (1,)), ((), ())), preferred_element_...  3.08 us
    ppermute x7, waiting for transfers between devices, across(): return lax.ppermute(x, 'segment', [(i, (i + shift) % n) for i in range(n)])  2.14 us
    concatenate x2, local copies, waits for them, and re-layouts, on_device(): mix_all = jnp.concatenate(mixes[k], axis=0)  2.06 us
  transfers between devices with their start and end apart: 16, of which 8 were waited for; matrix products, arithmetic and copies ran while one was open for 5% of the time, Pallas kernels for 0%

profile of v1, /device:TPU:0, one launch (start us, length us, event | category | flops | bytes accessed | tf_op | source)
XLA Modules:
  0.0 86.8 jit_solution(11604651688608125952)
XLA Ops:
  0.7 1.0 %constant_dynamic-slice_fusion.1 = bf16[128,512]{1,0:T(8,128)(2,1)S(1)} fusion(bf16[256,512]{1,0:T(8,128)(2,1)} %param.13, s32[]{:T(128)S(6)} %select_n.135), kind=kLoop, calls=%fused_computation.237 | loop fusion | bytes 262148 | tf_op jit(solution)/shard_map/dynamic_slice | solution.py:62
  1.6 4.1 %collective-permute-start.9 = (bf16[128,512]{1,0:T(8,128)(2,1)S(1)}, bf16[128,512]{1,0:T(8,128)(2,1)S(1)}, u32[]{:S(2)}, u32[]{:S(2)}) collective-permute-start(bf16[128,512]{1,0:T(8,128)(2,1)S(1)} %constant_dynamic-slice_fusion.1), channel_id=1, source_target_pairs={{0,16},{2,18},{4,20},{6,22},{8,24},{10,26},{12,28},{14,30},{16,0},... | collective-permute-start | bytes 393224 | tf_op jit(solution)/shard_map/ppermute | solution.py:13
  6.4 1.0 %fusion.93 = (bf16[128,512]{1,0:T(8,128)(2,1)S(1)}, bf16[128,512]{1,0:T(8,128)(2,1)S(1)}) fusion(s32[]{:T(128)S(6)} %select_n.135, bf16[256,256]{1,0:T(8,128)(2,1)} %param.9, bf16[256,256]{1,0:T(8,128)(2,1)} %param.10, bf16[256,512]{1,0:T(8,128)(2,1)} %param.8), kind=kLoop, calls=%fused_computation.184 | loop fusion | flops 262144 | bytes 655364 | tf_op jit(solution)/shard_map/concatenate | solution.py:58
  7.6 1.8 %collective-permute-start = (bf16[272,512]{1,0:T(8,128)(2,1)S(1)}, bf16[272,512]{1,0:T(8,128)(2,1)S(1)}, u32[]{:S(2)}, u32[]{:S(2)}) collective-permute-start(bf16[272,512]{1,0:T(8,128)(2,1)S(1)} %fusion.84), channel_id=1, source_target_pairs={{0,2},{2,0},{4,6},{6,4},{8,10},{10,8},{12,14},{14,12},{16,18},{18,... | collective-permute-start | bytes 835592 | tf_op jit(solution)/shard_map/ppermute | solution.py:13
  9.7 9.2 %collective-permute-done.9 = bf16[128,512]{1,0:T(8,128)(2,1)S(1)} collective-permute-done((bf16[128,512]{1,0:T(8,128)(2,1)S(1)}, bf16[128,512]{1,0:T(8,128)(2,1)S(1)}, u32[]{:S(2)}, u32[]{:S(2)}) %collective-permute-start.9) | collective-permute-done | bytes 131104 | tf_op jit(solution)/shard_map/ppermute | solution.py:13
  18.9 1.8 %collective-permute-start.11 = (bf16[128,512]{1,0:T(8,128)(2,1)S(1)}, bf16[128,512]{1,0:T(8,128)(2,1)S(1)}, u32[]{:S(2)}, u32[]{:S(2)}) collective-permute-start(bf16[128,512]{1,0:T(8,128)(2,1)S(1)} %collective-permute-done.9), channel_id=1, source_target_pairs={{0,2},{2,0},{4,6},{6,4},{8,10},{10,8},{12,14},{14,12},{16,18},{18,... | collective-permute-start | bytes 393224 | tf_op jit(solution)/shard_map/ppermute | solution.py:13
  21.6 2.3 %collective-permute-done.11 = bf16[128,512]{1,0:T(8,128)(2,1)S(1)} collective-permute-done((bf16[128,512]{1,0:T(8,128)(2,1)S(1)}, bf16[128,512]{1,0:T(8,128)(2,1)S(1)}, u32[]{:S(2)}, u32[]{:S(2)}) %collective-permute-start.11) | collective-permute-done | bytes 131104 | tf_op jit(solution)/shard_map/ppermute | solution.py:13
  25.8 1.8 %collective-permute-start.5 = (bf16[272,512]{1,0:T(8,128)(2,1)S(1)}, bf16[272,512]{1,0:T(8,128)(2,1)S(1)}, u32[]{:S(2)}, u32[]{:S(2)}) collective-permute-start(bf16[272,512]{1,0:T(8,128)(2,1)S(1)} %collective-permute-done.2), channel_id=1, source_target_pairs={{0,2},{2,0},{4,6},{6,4},{8,10},{10,8},{12,14},{14,12},{16,18},{18,... | collective-permute-start | bytes 835592 | tf_op jit(solution)/shard_map/ppermute | solution.py:13
  28.4 6.2 %collective-permute-done.5 = bf16[272,512]{1,0:T(8,128)(2,1)S(1)} collective-permute-done((bf16[272,512]{1,0:T(8,128)(2,1)S(1)}, bf16[272,512]{1,0:T(8,128)(2,1)S(1)}, u32[]{:S(2)}, u32[]{:S(2)}) %collective-permute-start.5) | collective-permute-done | bytes 278560 | tf_op jit(solution)/shard_map/ppermute | solution.py:13
  34.8 1.3 %collective-permute-done.6 = bf16[1,272,512]{2,1,0:T(8,128)(2,1)S(1)} collective-permute-done((bf16[1,272,512]{2,1,0:T(8,128)(2,1)S(1)}, bf16[1,272,512]{2,1,0:T(8,128)(2,1)S(1)}, u32[]{:S(2)}, u32[]{:S(2)}) %collective-permute-start.6) | collective-permute-done | bytes 278560 | tf_op jit(solution)/shard_map/ppermute | solution.py:18
  38.9 1.2 %multiply_convert_fusion.11 = (bf16[256,512]{1,0:T(8,128)(2,1)S(1)}, f32[256,512]{1,0:T(8,128)}) fusion(bf16[256,512]{1,0:T(8,128)(2,1)S(1)} %fusion.47, bf16[512,512]{1,0:T(8,128)(2,1)S(1)} %get-tuple-element.16), kind=kOutput, calls=%fused_computation.151 | convolution fusion | flops 135397376 | bytes 1572864 | tf_op jit(solution)/shard_map/dot_general | solution.py:42
  41.5 1.2 %multiply_convert_fusion.10 = (bf16[256,512]{1,0:T(8,128)(2,1)S(1)}, f32[256,512]{1,0:T(8,128)}) fusion(bf16[256,512]{1,0:T(8,128)(2,1)S(1)} %fusion.48, bf16[512,512]{1,0:T(8,128)(2,1)S(1)} %get-tuple-element.16), kind=kOutput, calls=%fused_computation.148 | convolution fusion | flops 135397376 | bytes 1572864 | tf_op jit(solution)/shard_map/dot_general | solution.py:42
  43.5 1.2 %multiply_convert_fusion.12 = (bf16[256,512]{1,0:T(8,128)(2,1)S(1)}, f32[256,512]{1,0:T(8,128)}) fusion(bf16[256,512]{1,0:T(8,128)(2,1)S(1)} %fusion.46, bf16[512,512]{1,0:T(8,128)(2,1)S(1)} %get-tuple-element.16), kind=kOutput, calls=%fused_computation.154 | convolution fusion | flops 135397376 | bytes 1572864 | tf_op jit(solution)/shard_map/dot_general | solution.py:42
  47.6 1.1 %fusion.105 = f32[256,512]{1,0:T(8,128)} fusion(bf16[256,512]{1,0:T(8,128)(2,1)S(1)} %fusion.41, bf16[256,512]{1,0:T(8,128)(2,1)S(1)} %bitcast.185), kind=kOutput, calls=%fused_computation.208 | convolution fusion | flops 67108864 | bytes 917504 | tf_op jit(solution)/shard_map/dot_general | solution.py:46
  48.6 1.1 %fusion.142 = f32[256,512]{1,0:T(8,128)} fusion(bf16[256,256]{1,0:T(8,128)(2,1)S(1)} %convolution_convert_fusion.4, bf16[256,512]{1,0:T(8,128)(2,1)S(1)} %fusion.41), kind=kOutput, calls=%fused_computation.258 | convolution fusion | flops 67108864 | bytes 917504 | tf_op jit(solution)/shard_map/dot_general | solution.py:46
  51.2 1.0 %fusion.110 = f32[256,512]{1,0:T(8,128)} fusion(bf16[256,512]{1,0:T(8,128)(2,1)S(1)} %fusion.40, bf16[256,512]{1,0:T(8,128)(2,1)S(1)} %bitcast.190), kind=kOutput, calls=%fused_computation.213 | convolution fusion | flops 67108864 | bytes 917504 | tf_op jit(solution)/shard_map/dot_general | solution.py:46
  52.2 1.0 %fusion.141 = f32[256,512]{1,0:T(8,128)} fusion(bf16[256,256]{1,0:T(8,128)(2,1)S(1)} %convolution_convert_fusion.7, bf16[256,512]{1,0:T(8,128)(2,1)S(1)} %fusion.40), kind=kOutput, calls=%fused_computation.257 | convolution fusion | flops 67108864 | bytes 917504 | tf_op jit(solution)/shard_map/dot_general | solution.py:46
  54.2 1.3 %multiply_convert_fusion.7 = (bf16[256,512]{1,0:T(8,128)(2,1)}, f32[256,512]{1,0:T(8,128)}) fusion(bf16[256,512]{1,0:T(8,128)(2,1)S(1)} %copy-done.37, bf16[256,512]{1,0:T(8,128)(2,1)S(1)} %fusion.61, bf16[512,512]{1,0:T(8,128)(2,1)S(1)} %get-tuple-element.15), kind=kOutput, calls=%fused_computation.142 | convolution fusion | flops 136052736 | bytes 1835008 | tf_op jit(solution)/shard_map/dot_general | solution.py:42
  56.1 1.5 %copy.10 = bf16[1024,512]{0,1:T(8,128)(2,1)} copy(bf16[1024,512]{1,0:T(8,128)(2,1)S(1)} %pad_maximum_fusion) | data formatting | bytes 2097152 | tf_op jit(solution)/shard_map/concatenate | solution.py:126
  57.7 1.6 %multiply_convert_fusion.4 = bf16[256,512]{1,0:T(8,128)(2,1)S(1)} fusion(bf16[128,512]{1,0:T(8,128)(2,1)} %get-tuple-element.37, bf16[128,512]{1,0:T(8,128)(2,1)} %get-tuple-element.36, bf16[256,512]{1,0:T(8,128)(2,1)S(1)} %fusion.52, bf16[512,512]{1,0:T(8,128)(2,1)} %copy-done.25), kind=kOutput, calls=%fused_computation.139 | convolution fusion | flops 136445952 | bytes 1310720 | tf_op jit(solution)/shard_map/dot_general | solution.py:42
  59.3 1.0 %fusion.42 = bf16[256,512]{1,0:T(8,128)(2,1)} fusion(bf16[256,512]{1,0:T(8,128)(2,1)S(1)} %multiply_convert_fusion.4, bf16[512,512]{1,0:T(8,128)(2,1)S(1)} %copy-done.26), kind=kOutput, calls=%fused_computation.80 | convolution fusion | flops 134873088 | bytes 1048576 | tf_op jit(solution)/shard_map/dot_general | solution.py:134
  60.4 1.0 %fusion.39 = bf16[256,512]{1,0:T(8,128)(2,1)} fusion(bf16[256,512]{1,0:T(8,128)(2,1)S(1)} %copy-done.43, bf16[512,512]{1,0:T(8,128)(2,1)S(1)} %copy-done.26), kind=kOutput, calls=%fused_computation.77 | convolution fusion | flops 134873088 | bytes 1048576 | tf_op jit(solution)/shard_map/dot_general | solution.py:134
  61.4 1.0 %constant_dynamic-slice_fusion.2 = bf16[1024,1,4,1,32]{0,4,3,2,1:T(8,128)(2,1)S(1)} fusion(bf16[1024,2,4,2,32]{0,4,3,2,1:T(8,128)(2,1)} %bitcast.191, s32[]{:T(128)S(6)} %select_n.149, s32[]{:T(128)S(6)} %select_n.151), kind=kLoop, calls=%fused_computation.238 | loop fusion | bytes 524296 | tf_op jit(solution)/shard_map/jit(dynamic_index_in_dim)/dynamic_slice | solution.py:129
  62.4 1.0 %convolution_multiply_fusion.16 = f32[128,512]{1,0:T(8,128)} fusion(bf16[1024,128]{0,1:T(8,128)(2,1)S(1)} %bitcast.202, bf16[256,512]{1,0:T(8,128)(2,1)S(1)} %multiply_convert_fusion.4, bf16[256,512]{1,0:T(8,128)(2,1)S(1)} %copy-done.40, bf16[256,512]{1,0:T(8,128)(2,1)S(1)} %copy-done.42, bf16[256,512]{1,0:T(8,128)(2,1)S(1)} %copy-done.43), kind=kOutput, calls=%fused_computation.104 | convolution fusion | flops 138477568 | bytes 1572864 | tf_op jit(solution)/shard_map/dot_general | solution.py:46
  64.7 1.3 %fusion.100 = f32[256,512]{1,0:T(8,128)S(1)} fusion(bf16[256,512]{1,0:T(8,128)(2,1)} %fusion.42, bf16[256,512]{1,0:T(8,128)(2,1)S(1)} %bitcast.197), kind=kOutput, calls=%fused_computation.203 | convolution fusion | flops 67108864 | bytes 917504 | tf_op jit(solution)/shard_map/dot_general | solution.py:46
  66.3 1.0 %multiply_convert_fusion = bf16[256,512]{1,0:T(8,128)(2,1)} fusion(f32[256,512]{1,0:T(8,128)S(1)} %copy-done.30, f32[256,512]{1,0:T(8,128)S(1)} %convolution_add_fusion.1, bf16[256,256]{1,0:T(8,128)(2,1)S(1)} %copy-done.34, bf16[256,512]{1,0:T(8,128)(2,1)S(1)} %copy-done.21), kind=kOutput, calls=%fused_computation.135 | convolution fusion | flops 68812800 | bytes 1703936 | tf_op jit(solution)/shard_map/dot_general | solution.py:46
  71.7 1.0 %multiply_convert_fusion.2 = bf16[256,512]{1,0:T(8,128)(2,1)} fusion(f32[256,512]{1,0:T(8,128)S(1)} %copy-done.45, f32[256,512]{1,0:T(8,128)S(1)} %convolution_add_fusion.5, bf16[256,256]{1,0:T(8,128)(2,1)S(1)} %copy-done.19, bf16[256,512]{1,0:T(8,128)(2,1)S(1)} %copy-done.22), kind=kOutput, calls=%fused_computation.137 | convolution fusion | flops 68812800 | bytes 1703936 | tf_op jit(solution)/shard_map/dot_general | solution.py:46
  72.8 2.5 %fusion.63 = f32[256,512]{1,0:T(8,128)} fusion(bf16[256,256]{1,0:T(8,128)(2,1)S(1)} %convolution_convert_fusion.7, bf16[256,512]{1,0:T(8,128)(2,1)} %multiply_convert_fusion.2, bf16[512,512]{1,0:T(8,128)(2,1)S(1)} %get-tuple-element.16), kind=kOutput, calls=%fused_computation.101 | convolution fusion | flops 201981952 | bytes 1441792 | tf_op jit(solution)/shard_map/dot_general | solution.py:46
  75.2 1.4 %multiply_convert_fusion.3 = bf16[256,512]{1,0:T(8,128)(2,1)S(1)} fusion(f32[256,512]{1,0:T(8,128)} %get-tuple-element.45, f32[256,512]{1,0:T(8,128)S(1)} %copy-done.27, f32[256,512]{1,0:T(8,128)S(1)} %copy-done.28, bf16[256,512]{1,0:T(8,128)(2,1)S(1)} %copy-done.23, bf16[256,256]{1,0:T(8,128)(2,1)S(1)} %copy-done.11), kind=kOutput, calls=%fused_computation.138 | convolution fusion | flops 68943872 | bytes 2228224 | tf_op jit(solution)/shard_map/dot_general | solution.py:46
  78.9 1.3 %collective-permute-start.15 = (bf16[32,512]{1,0:T(8,128)(2,1)S(1)}, bf16[32,512]{1,0:T(8,128)(2,1)S(1)}, u32[]{:S(2)}, u32[]{:S(2)}) collective-permute-start(bf16[32,512]{1,0:T(8,128)(2,1)S(1)} %get-tuple-element.30), channel_id=1, source_target_pairs={{0,12},{2,14},{4,8},{6,10},{8,4},{10,6},{12,0},{14,2},{16,28},{18,... | collective-permute-start | bytes 98312 | tf_op jit(solution)/shard_map/ppermute | solution.py:13
  80.2 2.0 %collective-permute-start.14 = (bf16[32,512]{1,0:T(8,128)(2,1)S(1)}, bf16[32,512]{1,0:T(8,128)(2,1)S(1)}, u32[]{:S(2)}, u32[]{:S(2)}) collective-permute-start(bf16[32,512]{1,0:T(8,128)(2,1)S(1)} %get-tuple-element.31), channel_id=1, source_target_pairs={{0,8},{2,10},{4,12},{6,14},{8,0},{10,2},{12,4},{14,6},{16,24},{18,... | collective-permute-start | bytes 98312 | tf_op jit(solution)/shard_map/ppermute | solution.py:13
  84.5 1.7 %collective-permute-done.13 = bf16[32,512]{1,0:T(8,128)(2,1)S(1)} collective-permute-done((bf16[32,512]{1,0:T(8,128)(2,1)S(1)}, bf16[32,512]{1,0:T(8,128)(2,1)S(1)}, u32[]{:S(2)}, u32[]{:S(2)}) %collective-permute-start.13) | collective-permute-done | bytes 32800 | tf_op jit(solution)/shard_map/ppermute | solution.py:13
  (187 shorter events, 26.1 us)
Async XLA Ops:
  0.6 20.1 %copy-start.9 = (bf16[256,256]{1,0:T(8,128)(2,1)S(1)}, bf16[256,256]{1,0:T(8,128)(2,1)}, u32[]{:S(2)}) copy-start(bf16[256,256]{1,0:T(8,128)(2,1)} %param.9) | copy-start | bytes 393220
  0.6 20.0 %copy-start = (bf16[256,512]{1,0:T(8,128)(2,1)S(1)}, bf16[256,512]{1,0:T(8,128)(2,1)}, u32[]{:S(2)}) copy-start(bf16[256,512]{1,0:T(8,128)(2,1)} %param.8) | copy-start | bytes 786436
  1.6 17.3 %collective-permute-start.9 = (bf16[128,512]{1,0:T(8,128)(2,1)S(1)}, bf16[128,512]{1,0:T(8,128)(2,1)S(1)}, u32[]{:S(2)}, u32[]{:S(2)}) collective-permute-start(bf16[128,512]{1,0:T(8,128)(2,1)S(1)} %constant_dynamic-slice_fusion.1), channel_id=1, source_target_pairs={{0,16},{2,18},{4,20},{6,22},{8,24},{10,26},{12,28},{14,30},{16,0},... | collective-permute-start | bytes 393224 | tf_op jit(solution)/shard_map/ppermute | solution.py:13
  6.4 14.6 %copy-start.24 = (bf16[512,512]{1,0:T(8,128)(2,1)S(1)}, bf16[512,512]{1,0:T(8,128)(2,1)}, u32[]{:S(2)}) copy-start(bf16[512,512]{1,0:T(8,128)(2,1)} %param.12) | copy-start | bytes 1572868
  7.5 17.7 %collective-permute-start.2 = (bf16[272,512]{1,0:T(8,128)(2,1)S(1)}, bf16[272,512]{1,0:T(8,128)(2,1)S(1)}, u32[]{:S(2)}, u32[]{:S(2)}) collective-permute-start(bf16[272,512]{1,0:T(8,128)(2,1)S(1)} %fusion.84), channel_id=1, source_target_pairs={{0,16},{2,18},{4,20},{6,22},{8,24},{10,26},{12,28},{14,30},{16,0},... | collective-permute-start | bytes 835592 | tf_op jit(solution)/shard_map/ppermute | solution.py:13
  7.6 17.9 %collective-permute-start = (bf16[272,512]{1,0:T(8,128)(2,1)S(1)}, bf16[272,512]{1,0:T(8,128)(2,1)S(1)}, u32[]{:S(2)}, u32[]{:S(2)}) collective-permute-start(bf16[272,512]{1,0:T(8,128)(2,1)S(1)} %fusion.84), channel_id=1, source_target_pairs={{0,2},{2,0},{4,6},{6,4},{8,10},{10,8},{12,14},{14,12},{16,18},{18,... | collective-permute-start | bytes 835592 | tf_op jit(solution)/shard_map/ppermute | solution.py:13
  9.4 11.6 %collective-permute-start.7 = (bf16[128,512]{1,0:T(8,128)(2,1)S(1)}, bf16[128,512]{1,0:T(8,128)(2,1)S(1)}, u32[]{:S(2)}, u32[]{:S(2)}) collective-permute-start(bf16[128,512]{1,0:T(8,128)(2,1)S(1)} %constant_dynamic-slice_fusion.1), channel_id=1, source_target_pairs={{0,2},{2,0},{4,6},{6,4},{8,10},{10,8},{12,14},{14,12},{16,18},{18,... | collective-permute-start | bytes 393224 | tf_op jit(solution)/shard_map/ppermute | solution.py:13
  18.9 5.0 %collective-permute-start.11 = (bf16[128,512]{1,0:T(8,128)(2,1)S(1)}, bf16[128,512]{1,0:T(8,128)(2,1)S(1)}, u32[]{:S(2)}, u32[]{:S(2)}) collective-permute-start(bf16[128,512]{1,0:T(8,128)(2,1)S(1)} %collective-permute-done.9), channel_id=1, source_target_pairs={{0,2},{2,0},{4,6},{6,4},{8,10},{10,8},{12,14},{14,12},{16,18},{18,... | collective-permute-start | bytes 393224 | tf_op jit(solution)/shard_map/ppermute | solution.py:13
  20.7 3.2 %collective-permute-start.10 = (bf16[128,512]{1,0:T(8,128)(2,1)S(1)}, bf16[128,512]{1,0:T(8,128)(2,1)S(1)}, u32[]{:S(2)}, u32[]{:S(2)}) collective-permute-start(bf16[128,512]{1,0:T(8,128)(2,1)S(1)} %collective-permute-done.9), channel_id=1, source_target_pairs={{0,1},{1,0},{2,3},{3,2},{4,5},{5,4},{6,7},{7,6},{8,9},{9,8},{10,11... | collective-permute-start | bytes 393224 | tf_op jit(solution)/shard_map/ppermute | solution.py:18
  21.0 7.3 %collective-permute-start.4 = (bf16[512,512]{1,0:T(8,128)(2,1)S(1)}, bf16[512,512]{1,0:T(8,128)(2,1)S(1)}, u32[]{:S(2)}, u32[]{:S(2)}) collective-permute-start(bf16[512,512]{1,0:T(8,128)(2,1)S(1)} %copy-done.24), channel_id=1, source_target_pairs={{0,1},{1,0},{2,3},{3,2},{4,5},{5,4},{6,7},{7,6},{8,9},{9,8},{10,11... | collective-permute-start | bytes 1572872 | tf_op jit(solution)/shard_map/ppermute | solution.py:18
  23.9 1.3 %collective-permute-start.8 = (bf16[128,512]{1,0:T(8,128)(2,1)S(1)}, bf16[128,512]{1,0:T(8,128)(2,1)S(1)}, u32[]{:S(2)}, u32[]{:S(2)}) collective-permute-start(bf16[128,512]{1,0:T(8,128)(2,1)S(1)} %collective-permute-done.7), channel_id=1, source_target_pairs={{0,1},{1,0},{2,3},{3,2},{4,5},{5,4},{6,7},{7,6},{8,9},{9,8},{10,11... | collective-permute-start | bytes 393224 | tf_op jit(solution)/shard_map/ppermute | solution.py:18
  23.9 3.8 %collective-permute-start.12 = (bf16[128,512]{1,0:T(8,128)(2,1)S(1)}, bf16[128,512]{1,0:T(8,128)(2,1)S(1)}, u32[]{:S(2)}, u32[]{:S(2)}) collective-permute-start(bf16[128,512]{1,0:T(8,128)(2,1)S(1)} %collective-permute-done.11), channel_id=1, source_target_pairs={{0,1},{1,0},{2,3},{3,2},{4,5},{5,4},{6,7},{7,6},{8,9},{9,8},{10,11... | collective-permute-start | bytes 393224 | tf_op jit(solution)/shard_map/ppermute | solution.py:18
  25.2 9.4 %collective-permute-start.3 = (bf16[1,272,512]{2,1,0:T(8,128)(2,1)S(1)}, bf16[1,272,512]{2,1,0:T(8,128)(2,1)S(1)}, u32[]{:S(2)}, u32[]{:S(2)}) collective-permute-start(bf16[1,272,512]{2,1,0:T(8,128)(2,1)S(1)} %bitcast.199), channel_id=1, source_target_pairs={{0,1},{1,0},{2,3},{3,2},{4,5},{5,4},{6,7},{7,6},{8,9},{9,8},{10,11... | collective-permute-start | bytes 835592 | tf_op jit(solution)/shard_map/ppermute | solution.py:18
  25.5 9.2 %collective-permute-start.1 = (bf16[1,272,512]{2,1,0:T(8,128)(2,1)S(1)}, bf16[1,272,512]{2,1,0:T(8,128)(2,1)S(1)}, u32[]{:S(2)}, u32[]{:S(2)}) collective-permute-start(bf16[1,272,512]{2,1,0:T(8,128)(2,1)S(1)} %bitcast.198), channel_id=1, source_target_pairs={{0,1},{1,0},{2,3},{3,2},{4,5},{5,4},{6,7},{7,6},{8,9},{9,8},{10,11... | collective-permute-start | bytes 835592 | tf_op jit(solution)/shard_map/ppermute | solution.py:18
  25.8 8.8 %collective-permute-start.5 = (bf16[272,512]{1,0:T(8,128)(2,1)S(1)}, bf16[272,512]{1,0:T(8,128)(2,1)S(1)}, u32[]{:S(2)}, u32[]{:S(2)}) collective-permute-start(bf16[272,512]{1,0:T(8,128)(2,1)S(1)} %collective-permute-done.2), channel_id=1, source_target_pairs={{0,2},{2,0},{4,6},{6,4},{8,10},{10,8},{12,14},{14,12},{16,18},{18,... | collective-permute-start | bytes 835592 | tf_op jit(solution)/shard_map/ppermute | solution.py:13
  28.4 25.1 %copy-start.25 = (bf16[512,512]{1,0:T(8,128)(2,1)}, bf16[512,512]{1,0:T(8,128)(2,1)S(1)}, u32[]{:S(2)}) copy-start(bf16[512,512]{1,0:T(8,128)(2,1)S(1)} %get-tuple-element.15) | copy-start | bytes 1572868
  34.6 1.6 %collective-permute-start.6 = (bf16[1,272,512]{2,1,0:T(8,128)(2,1)S(1)}, bf16[1,272,512]{2,1,0:T(8,128)(2,1)S(1)}, u32[]{:S(2)}, u32[]{:S(2)}) collective-permute-start(bf16[1,272,512]{2,1,0:T(8,128)(2,1)S(1)} %bitcast.200), channel_id=1, source_target_pairs={{0,1},{1,0},{2,3},{3,2},{4,5},{5,4},{6,7},{7,6},{8,9},{9,8},{10,11... | collective-permute-start | bytes 835592 | tf_op jit(solution)/shard_map/ppermute | solution.py:18
  36.6 9.5 %copy-start.16 = (bf16[256,256]{1,0:T(8,128)(2,1)}, bf16[256,256]{1,0:T(8,128)(2,1)S(1)}, u32[]{:S(2)}) copy-start(bf16[256,256]{1,0:T(8,128)(2,1)S(1)} %convolution_convert_fusion.5) | copy-start | bytes 393220
  36.8 11.8 %copy-start.3 = (bf16[256,256]{1,0:T(8,128)(2,1)}, bf16[256,256]{1,0:T(8,128)(2,1)S(1)}, u32[]{:S(2)}) copy-start(bf16[256,256]{1,0:T(8,128)(2,1)S(1)} %convolution_convert_fusion.4) | copy-start | bytes 393220
  37.2 12.7 %copy-start.33 = (bf16[256,256]{1,0:T(8,128)(2,1)}, bf16[256,256]{1,0:T(8,128)(2,1)S(1)}, u32[]{:S(2)}) copy-start(bf16[256,256]{1,0:T(8,128)(2,1)S(1)} %convolution_convert_fusion.6) | copy-start | bytes 393220
  37.5 3.1 %copy-start.5 = (bf16[256,256]{1,0:T(8,128)(2,1)}, bf16[256,256]{1,0:T(8,128)(2,1)S(1)}, u32[]{:S(2)}) copy-start(bf16[256,256]{1,0:T(8,128)(2,1)S(1)} %convolution_convert_fusion.1) | copy-start | bytes 393220
  37.7 5.5 %copy-start.14 = (bf16[256,256]{1,0:T(8,128)(2,1)}, bf16[256,256]{1,0:T(8,128)(2,1)S(1)}, u32[]{:S(2)}) copy-start(bf16[256,256]{1,0:T(8,128)(2,1)S(1)} %convolution_convert_fusion) | copy-start | bytes 393220
  37.8 8.0 %copy-start.12 = (bf16[2,128,512]{2,1,0:T(8,128)(2,1)}, bf16[2,128,512]{2,1,0:T(8,128)(2,1)S(1)}, u32[]{:S(2)}) copy-start(bf16[2,128,512]{2,1,0:T(8,128)(2,1)S(1)} %get-tuple-element.17) | copy-start | bytes 786436
  38.0 17.6 %copy-start.7 = (bf16[256,256]{1,0:T(8,128)(2,1)}, bf16[256,256]{1,0:T(8,128)(2,1)S(1)}, u32[]{:S(2)}) copy-start(bf16[256,256]{1,0:T(8,128)(2,1)S(1)} %convolution_convert_fusion.3) | copy-start | bytes 393220
  38.2 17.6 %copy-start.18 = (bf16[256,256]{1,0:T(8,128)(2,1)}, bf16[256,256]{1,0:T(8,128)(2,1)S(1)}, u32[]{:S(2)}) copy-start(bf16[256,256]{1,0:T(8,128)(2,1)S(1)} %convolution_convert_fusion.2) | copy-start | bytes 393220
  45.7 4.3 %copy-start.29 = (f32[256,512]{1,0:T(8,128)}, f32[256,512]{1,0:T(8,128)S(1)}, u32[]{:S(2)}) copy-start(f32[256,512]{1,0:T(8,128)S(1)} %fusion.34) | copy-start | bytes 1572868
  72.8 2.5 %copy-start.27 = (f32[256,512]{1,0:T(8,128)S(1)}, f32[256,512]{1,0:T(8,128)}, u32[]{:S(2)}) copy-start(f32[256,512]{1,0:T(8,128)} %fusion.142) | copy-start | bytes 1572868
  72.8 2.5 %copy-start.28 = (f32[256,512]{1,0:T(8,128)S(1)}, f32[256,512]{1,0:T(8,128)}, u32[]{:S(2)}) copy-start(f32[256,512]{1,0:T(8,128)} %fusion.141) | copy-start | bytes 1572868
  78.9 3.9 %copy-start.36 = (f32[256,512]{1,0:T(8,128)S(1)}, f32[256,512]{1,0:T(8,128)}, u32[]{:S(2)}) copy-start(f32[256,512]{1,0:T(8,128)} %fusion.63) | copy-start | bytes 1572868
  78.9 4.9 %collective-permute-start.15 = (bf16[32,512]{1,0:T(8,128)(2,1)S(1)}, bf16[32,512]{1,0:T(8,128)(2,1)S(1)}, u32[]{:S(2)}, u32[]{:S(2)}) collective-permute-start(bf16[32,512]{1,0:T(8,128)(2,1)S(1)} %get-tuple-element.30), channel_id=1, source_target_pairs={{0,12},{2,14},{4,8},{6,10},{8,4},{10,6},{12,0},{14,2},{16,28},{18,... | collective-permute-start | bytes 98312 | tf_op jit(solution)/shard_map/ppermute | solution.py:13
  80.2 4.2 %collective-permute-start.14 = (bf16[32,512]{1,0:T(8,128)(2,1)S(1)}, bf16[32,512]{1,0:T(8,128)(2,1)S(1)}, u32[]{:S(2)}, u32[]{:S(2)}) collective-permute-start(bf16[32,512]{1,0:T(8,128)(2,1)S(1)} %get-tuple-element.31), channel_id=1, source_target_pairs={{0,8},{2,10},{4,12},{6,14},{8,0},{10,2},{12,4},{14,6},{16,24},{18,... | collective-permute-start | bytes 98312 | tf_op jit(solution)/shard_map/ppermute | solution.py:13
  82.2 3.9 %collective-permute-start.13 = (bf16[32,512]{1,0:T(8,128)(2,1)S(1)}, bf16[32,512]{1,0:T(8,128)(2,1)S(1)}, u32[]{:S(2)}, u32[]{:S(2)}) collective-permute-start(bf16[32,512]{1,0:T(8,128)(2,1)S(1)} %get-tuple-element.29), channel_id=1, source_target_pairs={{0,4},{2,6},{4,0},{6,2},{8,12},{10,14},{12,8},{14,10},{16,20},{18,... | collective-permute-start | bytes 98312 | tf_op jit(solution)/shard_map/ppermute | solution.py:13
  (32 other events, 48.1 us)

commit v2 on v1

v2 whole, which is shorter than its diff:
```python
import math

import jax
import jax.numpy as jnp
from jax import lax
from jax.experimental import pallas as pl
from jax.experimental.pallas import tpu as pltpu
from jax.sharding import PartitionSpec as P

SHARE = 0.1
BETA_SCALE = 0.5
BF16 = jnp.bfloat16
F32 = jnp.float32


def swapped(x, mask):
    return lax.ppermute(x, "dom", [(i, i ^ mask) for i in range(lax.axis_size("dom"))])


def every_piece(x):
    n = lax.axis_size("segment")
    return [x] + [lax.ppermute(x, "segment", [(i, (i + k) % n) for i in range(n)]) for k in range(1, n)]


def beta_of(k):
    return math.log(BETA_SCALE / (k + 1.0) + 1.0)


def mm(a, b):
    return jnp.dot(a, b, preferred_element_type=F32)


def mm_nt(a, b):
    return lax.dot_general(a, b, (((1,), (1,)), ((), ())), preferred_element_type=F32)


def mm_tn(a, b):
    return lax.dot_general(a, b, (((0,), (0,)), ((), ())), preferred_element_type=F32)


def place_of(seg, k, n):
    return lax.rem(seg - k + n, n)


def forward_call(scalars, feats, adj, couple, send_rows, got, w_pieces):
    layers = len(w_pieces)
    rows, width = feats.shape
    piece = rows // layers
    bound = couple.shape[1] // 2

    def body(sc, feats_r, adj_r, couple_r, sr_r, *refs):
        got_r = [refs[g * layers : (g + 1) * layers] for g in range(3)]
        w_r = refs[3 * layers : 4 * layers]
        acts_o, mix_o, slope_o, blocks_o, w_o, x_s, ac_s = refs[4 * layers :]
        seg = sc[0]
        x_s[0] = feats_r[...]
        for g in range(3):
            for k in range(layers):
                at = pl.multiple_of(place_of(seg, k, layers) * piece, piece)
                x_s[g + 1, pl.ds(at, piece), :] = got_r[g][k][:piece, :]
                ac_s[g, pl.ds(at, piece), :] = got_r[g][k][piece : 2 * piece, :]
        for k in range(layers):
            w_o[place_of(seg, k, layers)] = w_r[k][...]
        ids = lax.broadcasted_iota(jnp.int32, (rows, 2 * bound), 0)
        picks = []
        for g in range(4):
            sr = sr_r[...] if g == 0 else got_r[g - 1][0][2 * piece : 2 * piece + 1, : 2 * bound].astype(F32).astype(jnp.int32)
            picks.append((ids == sr).astype(F32).astype(BF16))
        for g in range(4):
            own = adj_r[...] if g == 0 else ac_s[g - 1, :, :rows]
            cp = couple_r[...] if g == 0 else ac_s[g - 1, :, rows:]
            blocks_o[g, :, :rows] = own
            blocks_o[g, :, rows : 2 * rows] = mm_nt(cp[:, :bound], picks[g ^ 1][:, :bound]).astype(BF16)
            blocks_o[g, :, 2 * rows :] = mm_nt(cp[:, bound:], picks[g ^ 2][:, bound:]).astype(BF16)
        for k in range(layers):
            beta = beta_of(k)
            src = 0 if k == 0 else 4 + 4 * (k % 2)
            dst = 4 + 4 * ((k + 1) % 2)
            for g in range(4):
                agg = (
                    mm(blocks_o[g, :, :rows], x_s[src + g])
                    + mm(blocks_o[g, :, rows : 2 * rows], x_s[src + (g ^ 1)])
                    + mm(blocks_o[g, :, 2 * rows :], x_s[src + (g ^ 2)])
                )
                mixed = ((1.0 - SHARE) * agg + SHARE * x_s[g].astype(F32)).astype(BF16)
                mix_o[k, g] = mixed
                pre = (1.0 - beta) * mixed.astype(F32) + beta * mm(mixed, w_o[k])
                sig = 1.0 / (1.0 + jnp.exp(-pre))
                slope_o[k, g] = sig * (1.0 + pre * (1.0 - sig))
                out = (pre * sig).astype(BF16)
                if k + 1 < layers:
                    x_s[dst + g] = out
                if g == 0:

                    @pl.when(seg == k)
                    def _():
                        acts_o[...] = out

    n_in = 4 + 4 * layers
    vm = pl.BlockSpec(memory_space=pltpu.VMEM)
    return pl.pallas_call(
        body,
        out_shape=(
            jax.ShapeDtypeStruct((rows, width), BF16),
            jax.ShapeDtypeStruct((layers, 4, rows, width), BF16),
            jax.ShapeDtypeStruct((layers, 4, rows, width), F32),
            jax.ShapeDtypeStruct((4, rows, 3 * rows), BF16),
            jax.ShapeDtypeStruct((layers, width, width), BF16),
        ),
        in_specs=[pl.BlockSpec(memory_space=pltpu.SMEM)] + [vm] * n_in,
        out_specs=(vm,) * 5,
        scratch_shapes=[pltpu.VMEM((12, rows, width), BF16), pltpu.VMEM((3, rows, 2 * rows), BF16)],
        name="forward",
    )(scalars, feats, adj, couple, send_rows, *[p for g in got for p in g], *w_pieces)


def backward_call(scalars, cot, got, mix, slope, blocks, w):
    layers = w.shape[0]
    rows, width = cot.shape
    piece = rows // layers
    n_dom = lax.axis_size("dom")
    others = n_dom // 4
    out_rows = width // n_dom
    half = width // 2
    cols = width // layers

    def body(sc, cot_r, *refs):
        got_r = [refs[g * layers : (g + 1) * layers] for g in range(3)]
        mix_r, slope_r, blocks_r, w_r = refs[3 * layers : 3 * layers + 4]
        outs = refs[3 * layers + 4 :]
        feat_o, own_o = outs[:2]
        send_o = outs[2 : 1 + others]
        up_s, dpre_s, dmix_s, carry_s, part_s = outs[1 + others :]
        seg, low, high, place = sc[0], sc[1], sc[2], sc[3]
        for g in range(3):
            for k in range(layers):
                at = pl.multiple_of(place_of(seg, k, layers) * piece, piece)
                up_s[g + 1, pl.ds(at, piece), :] = got_r[g][k][...].astype(F32)
        up_s[0] = cot_r[...].astype(F32)
        for k in range(layers - 1, -1, -1):
            beta = beta_of(k)
            for g in range(4):
                up = up_s[g]
                if k + 1 < layers:
                    up = up.astype(BF16).astype(F32)
                dpre = (up * slope_r[k, g]).astype(BF16)
                dpre_s[pl.ds(g * rows, rows), :] = dpre
                if k or g < 3:
                    dmix = ((1.0 - beta) * dpre.astype(F32) + beta * mm_nt(dpre, w_r[k])).astype(BF16)
                    dmix_s[g] = dmix
                if g == 0:
                    carry_s[...] = SHARE * dmix.astype(F32) + (carry_s[...] if k + 1 < layers else 0.0)

            @pl.when(seg == k)
            def _():
                part = jnp.zeros((half, width), F32)
                for g in range(4):
                    chosen = mix_r[k, g, :, pl.ds(pl.multiple_of(high * half, half), half)]
                    part = part + mm_tn(chosen, dpre_s[pl.ds(g * rows, rows), :])
                part_s[...] = beta * part

            if k:
                for g in range(4):
                    up_s[g] = (1.0 - SHARE) * (
                        mm_tn(blocks_r[g, :, :rows], dmix_s[g])
                        + mm_tn(blocks_r[g ^ 1, :, rows : 2 * rows], dmix_s[g ^ 1])
                        + mm_tn(blocks_r[g ^ 2, :, 2 * rows :], dmix_s[g ^ 2])
                    )

        def block(m):
            at = (place ^ m) * (2 * out_rows) + low * out_rows
            return part_s[pl.ds(pl.multiple_of(at, out_rows), out_rows), :]

        own_o[...] = block(0)
        for m in range(1, others):
            send_o[m - 1][...] = block(m).astype(BF16)
        if cols % 128 == 0:
            at = pl.ds(pl.multiple_of(seg * cols, cols), cols)
            feat_o[...] = (
                (1.0 - SHARE)
                * (
                    mm_tn(blocks_r[0, :, :rows], dmix_s[0, :, at])
                    + mm_tn(blocks_r[1, :, rows : 2 * rows], dmix_s[1, :, at])
                    + mm_tn(blocks_r[2, :, 2 * rows :], dmix_s[2, :, at])
                )
                + carry_s[:, at]
            )
        else:
            feat_o[...] = (1.0 - SHARE) * (
                mm_tn(blocks_r[0, :, :rows], dmix_s[0])
                + mm_tn(blocks_r[1, :, rows : 2 * rows], dmix_s[1])
                + mm_tn(blocks_r[2, :, 2 * rows :], dmix_s[2])
            ) + carry_s[...]

    n_in = 1 + 3 * layers + 4
    vm = pl.BlockSpec(memory_space=pltpu.VMEM)
    feat_cols = cols if cols % 128 == 0 else width
    got_out = pl.pallas_call(
        body,
        out_shape=(jax.ShapeDtypeStruct((rows, feat_cols), F32), jax.ShapeDtypeStruct((out_rows, width), F32))
        + tuple(jax.ShapeDtypeStruct((out_rows, width), BF16) for _ in range(1, others)),
        in_specs=[pl.BlockSpec(memory_space=pltpu.SMEM)] + [vm] * n_in,
        out_specs=(vm,) * (1 + others),
        scratch_shapes=[
            pltpu.VMEM((4, rows, width), F32),
            pltpu.VMEM((4 * rows, width), BF16),
            pltpu.VMEM((4, rows, width), BF16),
            pltpu.VMEM((rows, width), F32),
            pltpu.VMEM((half, width), F32),
        ],
        name="backward",
    )(scalars, cot, *[p for g in got for p in g], mix, slope, blocks, w)
    feat, own = got_out[:2]
    if cols % 128:
        feat = lax.dynamic_slice_in_dim(feat, scalars[0] * cols, cols, 1)
    return feat, own, got_out[2:]


def on_device(feats, adj, couple, send_rows, weights, cot):
    seg = lax.axis_index("segment")
    dom = lax.axis_index("dom")
    layers = lax.axis_size("segment")
    n_dom = lax.axis_size("dom")
    top = n_dom // 2
    others = n_dom // 4
    rows, width = feats.shape
    piece = rows // layers
    place = (dom // 2) % others
    scalars = jnp.stack([seg, dom & 1, dom // top, place]).astype(jnp.int32)

    ac = jnp.concatenate([adj, couple], axis=1)
    sr_row = jnp.zeros((16, width), BF16).at[0, : send_rows.shape[1]].set(send_rows[0].astype(BF16))

    def mine(x):
        return lax.dynamic_slice_in_dim(x, seg * piece, piece, 0)

    fwd_mine = jnp.concatenate([mine(feats), mine(ac), sr_row], axis=0)
    cot_mine = mine(cot)
    far_fwd = swapped(fwd_mine, top)
    near_fwd = swapped(fwd_mine, 1)
    far_cot = swapped(cot_mine, top)
    near_cot = swapped(cot_mine, 1)
    diag_fwd = swapped(far_fwd, 1)
    diag_cot = swapped(far_cot, 1)
    w_pieces = every_piece(weights)

    acts, mix, slope, blocks, w = forward_call(
        scalars, feats, adj, couple, send_rows, [every_piece(x) for x in (near_fwd, far_fwd, diag_fwd)], w_pieces
    )
    feat, wgrad, sends = backward_call(
        scalars, cot, [every_piece(x) for x in (near_cot, far_cot, diag_cot)], mix, slope, blocks, w
    )
    for m in range(1, others):
        wgrad = wgrad + swapped(sends[m - 1], 2 * m).astype(F32)
    return (acts[None], wgrad[None], feat)


def solution(mesh):
    in_specs = (
        P("dom", None),
        P("dom", None),
        P("dom", None),
        P("dom", None),
        P("segment", None),
        P("dom", None),
    )
    out_specs = (P("segment", "dom", None), P("segment", "dom", None), P("dom", "segment"))
    return jax.shard_map(on_device, mesh=mesh, in_specs=in_specs, out_specs=out_specs, check_vma=False)
```

time: 87.3 us -> 70.3 us (0.81)
  matrix products: 32.9 us -> 0 us
  Pallas kernels: 0 us -> 17.4 us
  waiting for transfers between devices: 22.3 us -> 32.5 us
  local copies, waits for them, and re-layouts: 9.27 us -> 2.97 us
  starting transfers between devices: 15.1 us -> 12.4 us
  other arithmetic: 5.57 us -> 3.85 us
    dot_general x62 -> x0, matrix products: 32.9 us -> none  [the longest x40 15.2 us: mm(): return jnp.dot(a, b, preferred_element_type=F32)]
    pallas_call x0 -> x2, Pallas kernels: none -> 17.4 us  [the longest x1 9.45 us: forward_call(): pl.pallas_call(body, out_shape=(jax.ShapeDtypeStruct((rows, width), BF16)...]
    ppermute x9, waiting for transfers between devices: 20.2 us -> 32.5 us  [swapped(): lax.ppermute(x, 'dom', [(i, i ^ mask) for i in range(lax.axis_size('dom'))])]
    unnamed x96 -> x26, local copies, waits for them, and re-layouts: 4.51 us -> 2.06 us
    ppermute x9, starting transfers between devices: 13.5 us -> 11.3 us  [swapped(): lax.ppermute(x, 'dom', [(i, i ^ mask) for i in range(lax.axis_size('dom'))])]
    ppermute x7, waiting for transfers between devices: 2.14 us -> 0.02 us  [every_piece(): lax.ppermute(x, 'segment', [(i, (i + k) % n) for i in range(n)])]
    concatenate x2 -> x0, local copies, waits for them, and re-layouts: 2.06 us -> none  [on_device(): mix_all = jnp.concatenate(mixes[k], axis=0)]
    dynamic_slice x3 -> x1, local copies, waits for them, and re-layouts: 2.68 us -> 0.91 us  [mine(): return lax.dynamic_slice_in_dim(x, seg * piece, piece, 0)]
  transfers between devices with their start and end apart: 16 -> 16, of which waited for: 8 -> 7; matrix products, arithmetic and copies ran while one was open for 5% -> 2% of each run, Pallas kernels for 0% -> 14%
where the time goes in v2:
time: 70.3 us; the launch traced here: 70 us
  waiting for transfers between devices  32.5 us (46%)
  Pallas kernels  17.4 us (25%)
  starting transfers between devices  12.4 us (18%)
  other arithmetic  3.85 us (5%)
  local copies, waits for them, and re-layouts  2.97 us (4%)
  between operations  0.83 us (1%)
    ppermute x9, waiting for transfers between devices, swapped(): lax.ppermute(x, 'dom', [(i, i ^ mask) for i in range(lax.axis_size('dom'))])  32.5 us
    ppermute x9, starting transfers between devices, swapped(): lax.ppermute(x, 'dom', [(i, i ^ mask) for i in range(lax.axis_size('dom'))])  11.3 us
    pallas_call x1, Pallas kernels, forward_call(): pl.pallas_call(body, out_shape=(jax.ShapeDtypeStruct((rows, width), BF16)...  9.45 us
    pallas_call x1, Pallas kernels, backward_call(): pl.pallas_call(body, out_shape=(jax.ShapeDtypeStruct((rows, feat_cols), F...  7.98 us
    unnamed x26, local copies, waits for them, and re-layouts  2.06 us
    broadcast_in_dim x1, other arithmetic, on_device(): return (acts[None], wgrad[None], feat)  1.49 us
  transfers between devices with their start and end apart: 16, of which 7 were waited for; matrix products, arithmetic and copies ran while one was open for 2% of the time, Pallas kernels for 14%

profile of v2, /device:TPU:0, one launch (start us, length us, event | category | flops | bytes accessed | tf_op | source)
XLA Modules:
  0.0 70.0 jit_solution(219587943690599936)
XLA Ops:
  0.6 0.7 convert_element_type.13
  1.3 1.0 %fusion.2 = (bf16[128,512]{1,0:T(8,128)(2,1)S(1)}, bf16[128,512]{1,0:T(8,128)(2,1)S(1)}) fusion(s32[]{:T(128)S(6)} %select_n.22, bf16[256,256]{1,0:T(8,128)(2,1)} %adj_r.1, bf16[256,256]{1,0:T(8,128)(2,1)} %couple_r.1, bf16[256,512]{1,0:T(8,128)(2,1)} %feats_r.1), kind=kLoop, calls=%fused_computation.5 | loop fusion | flops 262144 | bytes 655364 | tf_op jit(solution)/shard_map/concatenate | solution.py:231
  2.3 4.1 %collective-permute-start.2 = (bf16[272,512]{1,0:T(8,128)(2,1)S(1)}, bf16[272,512]{1,0:T(8,128)(2,1)S(1)}, u32[]{:S(2)}, u32[]{:S(2)}) collective-permute-start(bf16[272,512]{1,0:T(8,128)(2,1)S(1)} %fusion.1), channel_id=1, source_target_pairs={{0,16},{2,18},{4,20},{6,22},{8,24},{10,26},{12,28},{14,30},{16,0},... | collective-permute-start | bytes 835592 | tf_op jit(solution)/shard_map/ppermute | solution.py:17
  6.5 0.0 collective-permute-start.6
  6.5 1.5 %collective-permute-start = (bf16[272,512]{1,0:T(8,128)(2,1)S(1)}, bf16[272,512]{1,0:T(8,128)(2,1)S(1)}, u32[]{:S(2)}, u32[]{:S(2)}) collective-permute-start(bf16[272,512]{1,0:T(8,128)(2,1)S(1)} %fusion.1), channel_id=1, source_target_pairs={{0,2},{2,0},{4,6},{6,4},{8,10},{10,8},{12,14},{14,12},{16,18},{18,... | collective-permute-start | bytes 835592 | tf_op jit(solution)/shard_map/ppermute | solution.py:17
  8.0 11.1 %collective-permute-done.2.refs_2_ = bf16[272,512]{1,0:T(8,128)(2,1)S(1)} collective-permute-done((bf16[272,512]{1,0:T(8,128)(2,1)S(1)}, bf16[272,512]{1,0:T(8,128)(2,1)S(1)}, u32[]{:S(2)}, u32[]{:S(2)}) %collective-permute-start.2) | collective-permute-done | bytes 278560 | tf_op jit(solution)/shard_map/ppermute | solution.py:17
  19.1 1.5 %collective-permute-start.4 = (bf16[272,512]{1,0:T(8,128)(2,1)S(1)}, bf16[272,512]{1,0:T(8,128)(2,1)S(1)}, u32[]{:S(2)}, u32[]{:S(2)}) collective-permute-start(bf16[272,512]{1,0:T(8,128)(2,1)S(1)} %collective-permute-done.2.refs_2_), channel_id=1, source_target_pairs={{0,2},{2,0},{4,6},{6,4},{8,10},{10,8},{12,14},{14,12},{16,18},{18,... | collective-permute-start | bytes 835592 | tf_op jit(solution)/shard_map/ppermute | solution.py:17
  20.6 0.9 %constant_dynamic-slice_fusion = bf16[128,512]{1,0:T(8,128)(2,1)S(1)} fusion(bf16[256,512]{1,0:T(8,128)(2,1)} %cot_r.1, s32[]{:T(128)S(6)} %select_n.22), kind=kLoop, calls=%fused_computation.7 | loop fusion | bytes 262148 | tf_op jit(solution)/shard_map/dynamic_slice | solution.py:235
  21.6 0.1 collective-permute-start.9
  21.6 0.1 collective-permute-start.3
  21.7 8.2 %collective-permute-done.9.refs_2_ = bf16[128,512]{1,0:T(8,128)(2,1)S(1)} collective-permute-done((bf16[128,512]{1,0:T(8,128)(2,1)S(1)}, bf16[128,512]{1,0:T(8,128)(2,1)S(1)}, u32[]{:S(2)}, u32[]{:S(2)}) %collective-permute-start.9) | collective-permute-done | bytes 131104 | tf_op jit(solution)/shard_map/ppermute | solution.py:17
  29.9 0.5 collective-permute-start.7
  30.5 0.0 collective-permute-done.refs_0_
  30.5 0.5 collective-permute-start.5
  31.0 5.1 %collective-permute-done.7.refs_0_ = bf16[128,512]{1,0:T(8,128)(2,1)S(1)} collective-permute-done((bf16[128,512]{1,0:T(8,128)(2,1)S(1)}, bf16[128,512]{1,0:T(8,128)(2,1)S(1)}, u32[]{:S(2)}, u32[]{:S(2)}) %collective-permute-start.7) | collective-permute-done | bytes 131104 | tf_op jit(solution)/shard_map/ppermute | solution.py:17
  36.1 5.0 %collective-permute-done.11.refs_4_ = bf16[128,512]{1,0:T(8,128)(2,1)S(1)} collective-permute-done((bf16[128,512]{1,0:T(8,128)(2,1)S(1)}, bf16[128,512]{1,0:T(8,128)(2,1)S(1)}, u32[]{:S(2)}, u32[]{:S(2)}) %collective-permute-start.11) | collective-permute-done | bytes 131104 | tf_op jit(solution)/shard_map/ppermute | solution.py:17
  41.1 0.5 collective-permute-start.8
  41.6 0.1 collective-permute-start.12
  41.7 0.7 pad_add_fusion.sc
  42.4 0.7 copy-done.5
  43.1 0.7 %copy-done.6 = bf16[272,512]{1,0:T(8,128)(2,1)} copy-done((bf16[272,512]{1,0:T(8,128)(2,1)}, bf16[272,512]{1,0:T(8,128)(2,1)S(1)}, u32[]{:S(2)}) %copy-start.6) | copy-done | bytes 278552
  43.8 9.5 %forward.1 = (bf16[256,512]{1,0:T(8,128)(2,1)}, bf16[2,4,256,512]{3,2,1,0:T(8,128)(2,1)}, f32[2,4,256,512]{3,2,1,0:T(8,128)}, bf16[4,256,768]{2,1,0:T(8,128)(2,1)}, bf16[2,512,512]{2,1,0:T(8,128)(2,1)}) custom-call(s32[4]{0:T(128)} %pad_add_fusion.sc, bf16[256,512]{1,0:T(8,128)(2,1)} %feats_r.1, bf16[256,256]{1,0:T(8,128)(2,1)} %adj_r.1, ...), custom_call_target="tpu_custom_call" | custom-call | tf_op jit(solution)/shard_map/forward/pallas_call | solution.py:101
  53.3 0.6 copy-done.10
  53.9 0.1 copy-done.11
  54.0 0.0 copy-done.12
  54.0 8.0 %backward.1 = (f32[256,256]{1,0:T(8,128)}, f32[32,512]{1,0:T(8,128)}, bf16[32,512]{1,0:T(8,128)(2,1)}, bf16[32,512]{1,0:T(8,128)(2,1)}, bf16[32,512]{1,0:T(8,128)(2,1)}) custom-call(s32[4]{0:T(128)} %pad_add_fusion.sc, bf16[256,512]{1,0:T(8,128)(2,1)} %cot_r.1, bf16[128,512]{1,0:T(8,128)(2,1)} %copy-done.8, bf16[128,512]{1,0:T(8,128)(2,1)} %copy-done.11, ...), custom_call_target="tpu_custom_call" | custom-call | tf_op jit(solution)/shard_map/backward/pallas_call | solution.py:198
  62.0 1.6 %collective-permute-start.13 = (bf16[32,512]{1,0:T(8,128)(2,1)}, bf16[32,512]{1,0:T(8,128)(2,1)S(1)}, u32[]{:S(2)}, u32[]{:S(2)}) collective-permute-start(bf16[32,512]{1,0:T(8,128)(2,1)} %get-tuple-element.31), channel_id=1, source_target_pairs={{0,4},{2,6},{4,0},{6,2},{8,12},{10,14},{12,8},{14,10},{16,20},{18,... | collective-permute-start | bytes 98312 | tf_op jit(solution)/shard_map/ppermute | solution.py:17
  63.5 1.9 %collective-permute-start.15 = (bf16[32,512]{1,0:T(8,128)(2,1)}, bf16[32,512]{1,0:T(8,128)(2,1)S(1)}, u32[]{:S(2)}, u32[]{:S(2)}) collective-permute-start(bf16[32,512]{1,0:T(8,128)(2,1)} %get-tuple-element.33), channel_id=1, source_target_pairs={{0,12},{2,14},{4,8},{6,10},{8,4},{10,6},{12,0},{14,2},{16,28},{18,... | collective-permute-start | bytes 98312 | tf_op jit(solution)/shard_map/ppermute | solution.py:17
  65.5 0.6 collective-permute-done.13
  66.1 1.6 %collective-permute-done.14 = bf16[32,512]{1,0:T(8,128)(2,1)S(1)} collective-permute-done((bf16[32,512]{1,0:T(8,128)(2,1)}, bf16[32,512]{1,0:T(8,128)(2,1)S(1)}, u32[]{:S(2)}, u32[]{:S(2)}) %collective-permute-start.14) | collective-permute-done | bytes 32800 | tf_op jit(solution)/shard_map/ppermute | solution.py:17
  67.7 0.9 %collective-permute-done.15 = bf16[32,512]{1,0:T(8,128)(2,1)S(1)} collective-permute-done((bf16[32,512]{1,0:T(8,128)(2,1)}, bf16[32,512]{1,0:T(8,128)(2,1)S(1)}, u32[]{:S(2)}, u32[]{:S(2)}) %collective-permute-start.15) | collective-permute-done | bytes 32800 | tf_op jit(solution)/shard_map/ppermute | solution.py:17
  68.6 1.5 %add_bitcast_fusion = f32[1,32,512]{2,1,0:T(8,128)} fusion(bf16[32,512]{1,0:T(8,128)(2,1)S(1)} %collective-permute-done.15, bf16[32,512]{1,0:T(8,128)(2,1)S(1)} %collective-permute-done.14, f32[32,512]{1,0:T(8,128)} %get-tuple-element.30, bf16[32,512]{1,0:T(8,128)(2,1)S(1)} %collective-permute-done.13), kind=kLoop, calls=%fused_computation.6 | loop fusion | flops 98304 | bytes 229376 | tf_op jit(solution)/shard_map/broadcast_in_dim | solution.py:255
  (34 shorter events, 0.1 us)
Async XLA Ops:
  2.3 16.8 %collective-permute-start.2 = (bf16[272,512]{1,0:T(8,128)(2,1)S(1)}, bf16[272,512]{1,0:T(8,128)(2,1)S(1)}, u32[]{:S(2)}, u32[]{:S(2)}) collective-permute-start(bf16[272,512]{1,0:T(8,128)(2,1)S(1)} %fusion.1), channel_id=1, source_target_pairs={{0,16},{2,18},{4,20},{6,22},{8,24},{10,26},{12,28},{14,30},{16,0},... | collective-permute-start | bytes 835592 | tf_op jit(solution)/shard_map/ppermute | solution.py:17
  6.5 34.6 %collective-permute-start.6 = (bf16[512,512]{1,0:T(8,128)(2,1)}, bf16[512,512]{1,0:T(8,128)(2,1)S(1)}, u32[]{:S(2)}, u32[]{:S(2)}) collective-permute-start(bf16[512,512]{1,0:T(8,128)(2,1)} %refs_6_.1), channel_id=1, source_target_pairs={{0,1},{1,0},{2,3},{3,2},{4,5},{5,4},{6,7},{7,6},{8,9},{9,8},{10,11... | collective-permute-start | bytes 1572872 | tf_op jit(solution)/shard_map/ppermute | solution.py:22
  6.5 24.0 %collective-permute-start = (bf16[272,512]{1,0:T(8,128)(2,1)S(1)}, bf16[272,512]{1,0:T(8,128)(2,1)S(1)}, u32[]{:S(2)}, u32[]{:S(2)}) collective-permute-start(bf16[272,512]{1,0:T(8,128)(2,1)S(1)} %fusion.1), channel_id=1, source_target_pairs={{0,2},{2,0},{4,6},{6,4},{8,10},{10,8},{12,14},{14,12},{16,18},{18,... | collective-permute-start | bytes 835592 | tf_op jit(solution)/shard_map/ppermute | solution.py:17
  19.1 23.3 %copy-start.1 = (bf16[272,512]{1,0:T(8,128)(2,1)}, bf16[272,512]{1,0:T(8,128)(2,1)S(1)}, u32[]{:S(2)}) copy-start(bf16[272,512]{1,0:T(8,128)(2,1)S(1)} %collective-permute-done.2.refs_2_) | copy-start | bytes 835588
  19.1 11.4 %collective-permute-start.4 = (bf16[272,512]{1,0:T(8,128)(2,1)S(1)}, bf16[272,512]{1,0:T(8,128)(2,1)S(1)}, u32[]{:S(2)}, u32[]{:S(2)}) collective-permute-start(bf16[272,512]{1,0:T(8,128)(2,1)S(1)} %collective-permute-done.2.refs_2_), channel_id=1, source_target_pairs={{0,2},{2,0},{4,6},{6,4},{8,10},{10,8},{12,14},{14,12},{16,18},{18,... | collective-permute-start | bytes 835592 | tf_op jit(solution)/shard_map/ppermute | solution.py:17
  21.6 8.4 %collective-permute-start.9 = (bf16[128,512]{1,0:T(8,128)(2,1)S(1)}, bf16[128,512]{1,0:T(8,128)(2,1)S(1)}, u32[]{:S(2)}, u32[]{:S(2)}) collective-permute-start(bf16[128,512]{1,0:T(8,128)(2,1)S(1)} %constant_dynamic-slice_fusion), channel_id=1, source_target_pairs={{0,16},{2,18},{4,20},{6,22},{8,24},{10,26},{12,28},{14,30},{16,0},... | collective-permute-start | bytes 393224 | tf_op jit(solution)/shard_map/ppermute | solution.py:17
  21.6 20.0 %collective-permute-start.3 = (bf16[272,512]{1,0:T(8,128)(2,1)S(1)}, bf16[272,512]{1,0:T(8,128)(2,1)S(1)}, u32[]{:S(2)}, u32[]{:S(2)}) collective-permute-start(bf16[272,512]{1,0:T(8,128)(2,1)S(1)} %collective-permute-done.2.refs_2_), channel_id=1, source_target_pairs={{0,1},{1,0},{2,3},{3,2},{4,5},{5,4},{6,7},{7,6},{8,9},{9,8},{10,11... | collective-permute-start | bytes 835592 | tf_op jit(solution)/shard_map/ppermute | solution.py:22
  29.9 23.4 %copy-start.7 = (bf16[128,512]{1,0:T(8,128)(2,1)}, bf16[128,512]{1,0:T(8,128)(2,1)S(1)}, u32[]{:S(2)}) copy-start(bf16[128,512]{1,0:T(8,128)(2,1)S(1)} %collective-permute-done.9.refs_2_) | copy-start | bytes 393220
  29.9 6.2 %collective-permute-start.7 = (bf16[128,512]{1,0:T(8,128)(2,1)S(1)}, bf16[128,512]{1,0:T(8,128)(2,1)S(1)}, u32[]{:S(2)}, u32[]{:S(2)}) collective-permute-start(bf16[128,512]{1,0:T(8,128)(2,1)S(1)} %constant_dynamic-slice_fusion), channel_id=1, source_target_pairs={{0,2},{2,0},{4,6},{6,4},{8,10},{10,8},{12,14},{14,12},{16,18},{18,... | collective-permute-start | bytes 393224 | tf_op jit(solution)/shard_map/ppermute | solution.py:17
  30.5 11.9 %copy-start.2 = (bf16[272,512]{1,0:T(8,128)(2,1)}, bf16[272,512]{1,0:T(8,128)(2,1)S(1)}, u32[]{:S(2)}) copy-start(bf16[272,512]{1,0:T(8,128)(2,1)S(1)} %collective-permute-done.refs_0_) | copy-start | bytes 835588
  30.5 11.9 %collective-permute-start.1 = (bf16[272,512]{1,0:T(8,128)(2,1)S(1)}, bf16[272,512]{1,0:T(8,128)(2,1)S(1)}, u32[]{:S(2)}, u32[]{:S(2)}) collective-permute-start(bf16[272,512]{1,0:T(8,128)(2,1)S(1)} %collective-permute-done.refs_0_), channel_id=1, source_target_pairs={{0,1},{1,0},{2,3},{3,2},{4,5},{5,4},{6,7},{7,6},{8,9},{9,8},{10,11... | collective-permute-start | bytes 835592 | tf_op jit(solution)/shard_map/ppermute | solution.py:22
  30.5 11.9 %copy-start.3 = (bf16[272,512]{1,0:T(8,128)(2,1)}, bf16[272,512]{1,0:T(8,128)(2,1)S(1)}, u32[]{:S(2)}) copy-start(bf16[272,512]{1,0:T(8,128)(2,1)S(1)} %collective-permute-done.4.refs_4_) | copy-start | bytes 835588
  30.5 11.9 %collective-permute-start.5 = (bf16[272,512]{1,0:T(8,128)(2,1)S(1)}, bf16[272,512]{1,0:T(8,128)(2,1)S(1)}, u32[]{:S(2)}, u32[]{:S(2)}) collective-permute-start(bf16[272,512]{1,0:T(8,128)(2,1)S(1)} %collective-permute-done.4.refs_4_), channel_id=1, source_target_pairs={{0,1},{1,0},{2,3},{3,2},{4,5},{5,4},{6,7},{7,6},{8,9},{9,8},{10,11... | collective-permute-start | bytes 835592 | tf_op jit(solution)/shard_map/ppermute | solution.py:22
  36.1 17.2 %copy-start.8 = (bf16[128,512]{1,0:T(8,128)(2,1)}, bf16[128,512]{1,0:T(8,128)(2,1)S(1)}, u32[]{:S(2)}) copy-start(bf16[128,512]{1,0:T(8,128)(2,1)S(1)} %collective-permute-done.7.refs_0_) | copy-start | bytes 393220
  36.1 5.0 %collective-permute-start.11 = (bf16[128,512]{1,0:T(8,128)(2,1)S(1)}, bf16[128,512]{1,0:T(8,128)(2,1)S(1)}, u32[]{:S(2)}, u32[]{:S(2)}) collective-permute-start(bf16[128,512]{1,0:T(8,128)(2,1)S(1)} %collective-permute-done.9.refs_2_), channel_id=1, source_target_pairs={{0,2},{2,0},{4,6},{6,4},{8,10},{10,8},{12,14},{14,12},{16,18},{18,... | collective-permute-start | bytes 393224 | tf_op jit(solution)/shard_map/ppermute | solution.py:17
  41.1 12.2 %copy-start.9 = (bf16[128,512]{1,0:T(8,128)(2,1)}, bf16[128,512]{1,0:T(8,128)(2,1)S(1)}, u32[]{:S(2)}) copy-start(bf16[128,512]{1,0:T(8,128)(2,1)S(1)} %collective-permute-done.11.refs_4_) | copy-start | bytes 393220
  41.1 12.2 %collective-permute-start.10 = (bf16[128,512]{1,0:T(8,128)(2,1)S(1)}, bf16[128,512]{1,0:T(8,128)(2,1)S(1)}, u32[]{:S(2)}, u32[]{:S(2)}) collective-permute-start(bf16[128,512]{1,0:T(8,128)(2,1)S(1)} %collective-permute-done.9.refs_2_), channel_id=1, source_target_pairs={{0,1},{1,0},{2,3},{3,2},{4,5},{5,4},{6,7},{7,6},{8,9},{9,8},{10,11... | collective-permute-start | bytes 393224 | tf_op jit(solution)/shard_map/ppermute | solution.py:22
  41.1 1.3 %copy-start = (bf16[512,512]{1,0:T(8,128)(2,1)}, bf16[512,512]{1,0:T(8,128)(2,1)S(1)}, u32[]{:S(2)}) copy-start(bf16[512,512]{1,0:T(8,128)(2,1)S(1)} %collective-permute-done.6.refs_7_) | copy-start | bytes 1572868
  41.1 12.2 %collective-permute-start.8 = (bf16[128,512]{1,0:T(8,128)(2,1)S(1)}, bf16[128,512]{1,0:T(8,128)(2,1)S(1)}, u32[]{:S(2)}, u32[]{:S(2)}) collective-permute-start(bf16[128,512]{1,0:T(8,128)(2,1)S(1)} %collective-permute-done.7.refs_0_), channel_id=1, source_target_pairs={{0,1},{1,0},{2,3},{3,2},{4,5},{5,4},{6,7},{7,6},{8,9},{9,8},{10,11... | collective-permute-start | bytes 393224 | tf_op jit(solution)/shard_map/ppermute | solution.py:22
  41.6 0.8 %copy-start.4 = (bf16[272,512]{1,0:T(8,128)(2,1)}, bf16[272,512]{1,0:T(8,128)(2,1)S(1)}, u32[]{:S(2)}) copy-start(bf16[272,512]{1,0:T(8,128)(2,1)S(1)} %collective-permute-done.3.refs_3_) | copy-start | bytes 835588
  41.6 11.7 %collective-permute-start.12 = (bf16[128,512]{1,0:T(8,128)(2,1)S(1)}, bf16[128,512]{1,0:T(8,128)(2,1)S(1)}, u32[]{:S(2)}, u32[]{:S(2)}) collective-permute-start(bf16[128,512]{1,0:T(8,128)(2,1)S(1)} %collective-permute-done.11.refs_4_), channel_id=1, source_target_pairs={{0,1},{1,0},{2,3},{3,2},{4,5},{5,4},{6,7},{7,6},{8,9},{9,8},{10,11... | collective-permute-start | bytes 393224 | tf_op jit(solution)/shard_map/ppermute | solution.py:22
  42.4 0.7 %copy-start.5 = (bf16[272,512]{1,0:T(8,128)(2,1)}, bf16[272,512]{1,0:T(8,128)(2,1)S(1)}, u32[]{:S(2)}) copy-start(bf16[272,512]{1,0:T(8,128)(2,1)S(1)} %collective-permute-done.1.refs_1_) | copy-start | bytes 835588
  43.1 0.7 %copy-start.6 = (bf16[272,512]{1,0:T(8,128)(2,1)}, bf16[272,512]{1,0:T(8,128)(2,1)S(1)}, u32[]{:S(2)}) copy-start(bf16[272,512]{1,0:T(8,128)(2,1)S(1)} %collective-permute-done.5.refs_5_) | copy-start | bytes 835588
  53.2 0.6 copy-start.10
  53.3 0.7 copy-start.11
  53.3 0.7 %copy-start.12 = (bf16[128,512]{1,0:T(8,128)(2,1)}, bf16[128,512]{1,0:T(8,128)(2,1)S(1)}, u32[]{:S(2)}) copy-start(bf16[128,512]{1,0:T(8,128)(2,1)S(1)} %collective-permute-done.12.refs_5_) | copy-start | bytes 393220
  62.0 4.1 %collective-permute-start.13 = (bf16[32,512]{1,0:T(8,128)(2,1)}, bf16[32,512]{1,0:T(8,128)(2,1)S(1)}, u32[]{:S(2)}, u32[]{:S(2)}) collective-permute-start(bf16[32,512]{1,0:T(8,128)(2,1)} %get-tuple-element.31), channel_id=1, source_target_pairs={{0,4},{2,6},{4,0},{6,2},{8,12},{10,14},{12,8},{14,10},{16,20},{18,... | collective-permute-start | bytes 98312 | tf_op jit(solution)/shard_map/ppermute | solution.py:17
  63.5 4.1 %collective-permute-start.14 = (bf16[32,512]{1,0:T(8,128)(2,1)}, bf16[32,512]{1,0:T(8,128)(2,1)S(1)}, u32[]{:S(2)}, u32[]{:S(2)}) collective-permute-start(bf16[32,512]{1,0:T(8,128)(2,1)} %get-tuple-element.32), channel_id=1, source_target_pairs={{0,8},{2,10},{4,12},{6,14},{8,0},{10,2},{12,4},{14,6},{16,24},{18,... | collective-permute-start | bytes 98312 | tf_op jit(solution)/shard_map/ppermute | solution.py:17
  63.5 5.0 %collective-permute-start.15 = (bf16[32,512]{1,0:T(8,128)(2,1)}, bf16[32,512]{1,0:T(8,128)(2,1)S(1)}, u32[]{:S(2)}, u32[]{:S(2)}) collective-permute-start(bf16[32,512]{1,0:T(8,128)(2,1)} %get-tuple-element.33), channel_id=1, source_target_pairs={{0,12},{2,14},{4,8},{6,10},{8,4},{10,6},{12,0},{14,2},{16,28},{18,... | collective-permute-start | bytes 98312 | tf_op jit(solution)/shard_map/ppermute | solution.py:17

commit v3 on v2

--- a/solution.py
+++ b/solution.py
@@ -7,12 +7,17 @@
 from jax.experimental.pallas import tpu as pltpu
 from jax.sharding import PartitionSpec as P
 
+
 SHARE = 0.1
 BETA_SCALE = 0.5
 BF16 = jnp.bfloat16
 F32 = jnp.float32
 
 
+def vmem_of(layers):
+    return min(60, 14 + 6 * layers) << 20
+
+
 def swapped(x, mask):
     return lax.ppermute(x, "dom", [(i, i ^ mask) for i in range(lax.axis_size("dom"))])
 
@@ -42,7 +47,7 @@
     return lax.rem(seg - k + n, n)
 
 
-def forward_call(scalars, feats, adj, couple, send_rows, got, w_pieces):
+def first_layer_call(scalars, feats, adj, couple, send_rows, got, w_pieces):
     layers = len(w_pieces)
     rows, width = feats.shape
     piece = rows // layers
@@ -51,13 +56,13 @@
     def body(sc, feats_r, adj_r, couple_r, sr_r, *refs):
         got_r = [refs[g * layers : (g + 1) * layers] for g in range(3)]
         w_r = refs[3 * layers : 4 * layers]
-        acts_o, mix_o, slope_o, blocks_o, w_o, x_s, ac_s = refs[4 * layers :]
+        x0_o, x1_o, mix_o, slope_o, blocks_o, w_o, ac_s = refs[4 * layers :]
         seg = sc[0]
-        x_s[0] = feats_r[...]
+        x0_o[0] = feats_r[...]
         for g in range(3):
             for k in range(layers):
                 at = pl.multiple_of(place_of(seg, k, layers) * piece, piece)
-                x_s[g + 1, pl.ds(at, piece), :] = got_r[g][k][:piece, :]
+                x0_o[g + 1, pl.ds(at, piece), :] = got_r[g][k][:piece, :]
                 ac_s[g, pl.ds(at, piece), :] = got_r[g][k][piece : 2 * piece, :]
         for k in range(layers):
             w_o[place_of(seg, k, layers)] = w_r[k][...]
@@ -72,49 +77,91 @@
             blocks_o[g, :, :rows] = own
             blocks_o[g, :, rows : 2 * rows] = mm_nt(cp[:, :bound], picks[g ^ 1][:, :bound]).astype(BF16)
             blocks_o[g, :, 2 * rows :] = mm_nt(cp[:, bound:], picks[g ^ 2][:, bound:]).astype(BF16)
-        for k in range(layers):
-            beta = beta_of(k)
-            src = 0 if k == 0 else 4 + 4 * (k % 2)
-            dst = 4 + 4 * ((k + 1) % 2)
-            for g in range(4):
-                agg = (
-                    mm(blocks_o[g, :, :rows], x_s[src + g])
-                    + mm(blocks_o[g, :, rows : 2 * rows], x_s[src + (g ^ 1)])
-                    + mm(blocks_o[g, :, 2 * rows :], x_s[src + (g ^ 2)])
-                )
-                mixed = ((1.0 - SHARE) * agg + SHARE * x_s[g].astype(F32)).astype(BF16)
-                mix_o[k, g] = mixed
-                pre = (1.0 - beta) * mixed.astype(F32) + beta * mm(mixed, w_o[k])
-                sig = 1.0 / (1.0 + jnp.exp(-pre))
-                slope_o[k, g] = sig * (1.0 + pre * (1.0 - sig))
-                out = (pre * sig).astype(BF16)
-                if k + 1 < layers:
-                    x_s[dst + g] = out
-                if g == 0:
-
-                    @pl.when(seg == k)
-                    def _():
-                        acts_o[...] = out
+        for g in range(4):
+            mixed, slope, out = layer_of(0, g, blocks_o, x0_o, x0_o, w_o)
+            mix_o[g] = mixed
+            slope_o[g] = slope
+            x1_o[g] = out
 
     n_in = 4 + 4 * layers
     vm = pl.BlockSpec(memory_space=pltpu.VMEM)
     return pl.pallas_call(
         body,
         out_shape=(
-            jax.ShapeDtypeStruct((rows, width), BF16),
-            jax.ShapeDtypeStruct((layers, 4, rows, width), BF16),
-            jax.ShapeDtypeStruct((layers, 4, rows, width), F32),
+            jax.ShapeDtypeStruct((4, rows, width), BF16),
+            jax.ShapeDtypeStruct((4, rows, width), BF16),
+            jax.ShapeDtypeStruct((4, rows, width), BF16),
+            jax.ShapeDtypeStruct((4, rows, width), F32),
             jax.ShapeDtypeStruct((4, rows, 3 * rows), BF16),
             jax.ShapeDtypeStruct((layers, width, width), BF16),
         ),
         in_specs=[pl.BlockSpec(memory_space=pltpu.SMEM)] + [vm] * n_in,
-        out_specs=(vm,) * 5,
-        scratch_shapes=[pltpu.VMEM((12, rows, width), BF16), pltpu.VMEM((3, rows, 2 * rows), BF16)],
-        name="forward",
+        out_specs=(vm,) * 6,
+        scratch_shapes=[pltpu.VMEM((3, rows, 2 * rows), BF16)],
+        compiler_params=pltpu.CompilerParams(vmem_limit_bytes=vmem_of(layers)),
+        name="first_layer",
     )(scalars, feats, adj, couple, send_rows, *[p for g in got for p in g], *w_pieces)
 
 
-def backward_call(scalars, cot, got, mix, slope, blocks, w):
+def layer_of(k, g, blocks, x_in, x0, w):
+    rows = x_in.shape[1]
+    beta = beta_of(k)
+    agg = (
+        mm(blocks[g, :, :rows], x_in[g])
+        + mm(blocks[g, :, rows : 2 * rows], x_in[g ^ 1])
+        + mm(blocks[g, :, 2 * rows :], x_in[g ^ 2])
+    )
+    mixed = ((1.0 - SHARE) * agg + SHARE * x0[g].astype(F32)).astype(BF16)
+    pre = (1.0 - beta) * mixed.astype(F32) + beta * mm(mixed, w[k])
+    sig = 1.0 / (1.0 + jnp.exp(-pre))
+    return mixed, sig * (1.0 + pre * (1.0 - sig)), (pre * sig).astype(BF16)
+
+
+def later_layers_call(scalars, x0, x1, blocks, w):
+    layers = w.shape[0]
+    rows, width = x0.shape[1:]
+
+    def body(sc, x0_r, x1_r, blocks_r, w_r, acts_o, mix_o, slope_o, xa_s, xb_s):
+        seg = sc[0]
+
+        @pl.when(seg == 0)
+        def _():
+            acts_o[...] = x1_r[0]
+
+        src = x1_r
+        for k in range(1, layers):
+            dst = (xa_s, xb_s)[k % 2]
+            for g in range(4):
+                mixed, slope, out = layer_of(k, g, blocks_r, src, x0_r, w_r)
+                mix_o[k - 1, g] = mixed
+                slope_o[k - 1, g] = slope
+                if k + 1 < layers:
+                    dst[g] = out
+                if g == 0:
+
+                    @pl.when(seg == k)
+                    def _():
+                        acts_o[...] = out
+
+            src = dst
+
+    vm = pl.BlockSpec(memory_space=pltpu.VMEM)
+    return pl.pallas_call(
+        body,
+        out_shape=(
+            jax.ShapeDtypeStruct((rows, width), BF16),
+            jax.ShapeDtypeStruct((layers - 1, 4, rows, width), BF16),
+            jax.ShapeDtypeStruct((layers - 1, 4, rows, width), F32),
+        ),
+        in_specs=[pl.BlockSpec(memory_space=pltpu.SMEM)] + [vm] * 4,
+        out_specs=(vm,) * 3,
+        scratch_shapes=[pltpu.VMEM((4, rows, width), BF16)] * 2,
+        compiler_params=pltpu.CompilerParams(vmem_limit_bytes=vmem_of(layers)),
+        name="later_layers",
+    )(scalars, x0, x1, blocks, w)
+
+
+def backward_call(scalars, cot, got, mix, slope, later_mix, later_slope, blocks, w):
     layers = w.shape[0]
     rows, width = cot.shape
     piece = rows // layers
@@ -126,8 +173,8 @@
 
     def body(sc, cot_r, *refs):
         got_r = [refs[g * layers : (g + 1) * layers] for g in range(3)]
-        mix_r, slope_r, blocks_r, w_r = refs[3 * layers : 3 * layers + 4]
-        outs = refs[3 * layers + 4 :]
+        mix_r, slope_r, later_mix_r, later_slope_r, blocks_r, w_r = refs[3 * layers : 3 * layers + 6]
+        outs = refs[3 * layers + 6 :]
         feat_o, own_o = outs[:2]
         send_o = outs[2 : 1 + others]
         up_s, dpre_s, dmix_s, carry_s, part_s = outs[1 + others :]
@@ -143,7 +190,7 @@
                 up = up_s[g]
                 if k + 1 < layers:
                     up = up.astype(BF16).astype(F32)
-                dpre = (up * slope_r[k, g]).astype(BF16)
+                dpre = (up * (later_slope_r[k - 1, g] if k else slope_r[g])).astype(BF16)
                 dpre_s[pl.ds(g * rows, rows), :] = dpre
                 if k or g < 3:
                     dmix = ((1.0 - beta) * dpre.astype(F32) + beta * mm_nt(dpre, w_r[k])).astype(BF16)
@@ -155,7 +202,8 @@
             def _():
                 part = jnp.zeros((half, width), F32)
                 for g in range(4):
-                    chosen = mix_r[k, g, :, pl.ds(pl.multiple_of(high * half, half), half)]
+                    at = pl.ds(pl.multiple_of(high * half, half), half)
+                    chosen = later_mix_r[k - 1, g, :, at] if k else mix_r[g, :, at]
                     part = part + mm_tn(chosen, dpre_s[pl.ds(g * rows, rows), :])
                 part_s[...] = beta * part
 
@@ -192,7 +240,7 @@
                 + mm_tn(blocks_r[2, :, 2 * rows :], dmix_s[2])
             ) + carry_s[...]
 
-    n_in = 1 + 3 * layers + 4
+    n_in = 1 + 3 * layers + 6
     vm = pl.BlockSpec(memory_space=pltpu.VMEM)
     feat_cols = cols if cols % 128 == 0 else width
     got_out = pl.pallas_call(
@@ -208,15 +256,16 @@
             pltpu.VMEM((rows, width), F32),
             pltpu.VMEM((half, width), F32),
         ],
+        compiler_params=pltpu.CompilerParams(vmem_limit_bytes=vmem_of(layers)),
         name="backward",
-    )(scalars, cot, *[p for g in got for p in g], mix, slope, blocks, w)
+    )(scalars, cot, *[p for g in got for p in g], mix, slope, later_mix, later_slope, blocks, w)
     feat, own = got_out[:2]
     if cols % 128:
         feat = lax.dynamic_slice_in_dim(feat, scalars[0] * cols, cols, 1)
     return feat, own, got_out[2:]
 
 
-def on_device(feats, adj, couple, send_rows, weights, cot):
+def step(feats, adj, couple, send_rows, weights, cot):
     seg = lax.axis_index("segment")
     dom = lax.axis_index("dom")
     layers = lax.axis_size("segment")
@@ -240,17 +289,23 @@
     near_fwd = swapped(fwd_mine, 1)
     far_cot = swapped(cot_mine, top)
     near_cot = swapped(cot_mine, 1)
+    w_pieces = every_piece(weights)
+    near_fwd = every_piece(near_fwd)
     diag_fwd = swapped(far_fwd, 1)
+    far_fwd = every_piece(far_fwd)
     diag_cot = swapped(far_cot, 1)
-    w_pieces = every_piece(weights)
-
-    acts, mix, slope, blocks, w = forward_call(
-        scalars, feats, adj, couple, send_rows, [every_piece(x) for x in (near_fwd, far_fwd, diag_fwd)], w_pieces
+    far_cot = every_piece(far_cot)
+    near_cot = every_piece(near_cot)
+    diag_fwd = every_piece(diag_fwd)
+    x0, x1, mix, slope, blocks, w = first_layer_call(
+        scalars, feats, adj, couple, send_rows, [near_fwd, far_fwd, diag_fwd], w_pieces
     )
+    diag_cot = every_piece(diag_cot)
+    acts, later_mix, later_slope = later_layers_call(scalars, x0, x1, blocks, w)
     feat, wgrad, sends = backward_call(
-        scalars, cot, [every_piece(x) for x in (near_cot, far_cot, diag_cot)], mix, slope, blocks, w
+        scalars, cot, [near_cot, far_cot, diag_cot], mix, slope, later_mix, later_slope, blocks, w
     )
-    for m in range(1, others):
+    for m in range(others - 1, 0, -1):
         wgrad = wgrad + swapped(sends[m - 1], 2 * m).astype(F32)
     return (acts[None], wgrad[None], feat)
 
@@ -265,4 +320,4 @@
         P("dom", None),
     )
     out_specs = (P("segment", "dom", None), P("segment", "dom", None), P("dom", "segment"))
-    return jax.shard_map(on_device, mesh=mesh, in_specs=in_specs, out_specs=out_specs, check_vma=False)
+    return jax.shard_map(step, mesh=mesh, in_specs=in_specs, out_specs=out_specs, check_vma=False)

time: 70.3 us -> 65.5 us (0.932)
  Pallas kernels: 17.4 us -> 11.3 us
  local copies, waits for them, and re-layouts: 2.97 us -> 5.39 us
  other arithmetic: 3.85 us -> 2.42 us
    pallas_call x1, Pallas kernels: 7.98 us -> 4.76 us  [backward_call(): pl.pallas_call(body, out_shape=(jax.ShapeDtypeStruct((rows, feat_cols), F...]
    pallas_call x1 -> x2, Pallas kernels: 9.45 us -> 6.53 us  [the longest x1 3.48 us: first_layer_call(): pl.pallas_call(body, out_shape=(jax.ShapeDtypeStruct((4, rows, width), BF...]
    unnamed x26 -> x12, local copies, waits for them, and re-layouts: 2.06 us -> 4.48 us
    broadcast_in_dim x1, other arithmetic: 1.49 us -> 0.65 us  [step(): return (acts[None], wgrad[None], feat)]
  transfers between devices with their start and end apart: 16 -> 16, of which waited for: 7 -> 7; matrix products, arithmetic and copies ran while one was open for 2% -> 2% of each run, Pallas kernels for 14% -> 10%
where the time goes in v3:
time: 65.5 us; the launch traced here: 65.2 us
  waiting for transfers between devices  32.9 us (50%)
  starting transfers between devices  12.4 us (19%)
  Pallas kernels  11.3 us (17%)
  local copies, waits for them, and re-layouts  5.39 us (8%)
  other arithmetic  2.42 us (4%)
  between operations  0.75 us (1%)
    ppermute x9, waiting for transfers between devices, swapped(): lax.ppermute(x, 'dom', [(i, i ^ mask) for i in range(lax.axis_size('dom'))])  32.9 us
    ppermute x9, starting transfers between devices, swapped(): lax.ppermute(x, 'dom', [(i, i ^ mask) for i in range(lax.axis_size('dom'))])  11.3 us
    pallas_call x1, Pallas kernels, backward_call(): pl.pallas_call(body, out_shape=(jax.ShapeDtypeStruct((rows, feat_cols), F...  4.76 us
    unnamed x12, local copies, waits for them, and re-layouts  4.48 us
    pallas_call x1, Pallas kernels, first_layer_call(): pl.pallas_call(body, out_shape=(jax.ShapeDtypeStruct((4, rows, width), BF...  3.48 us
    pallas_call x1, Pallas kernels, later_layers_call(): pl.pallas_call(body, out_shape=(jax.ShapeDtypeStruct((rows, width), BF16)...  3.05 us
  transfers between devices with their start and end apart: 16, of which 7 were waited for; matrix products, arithmetic and copies ran while one was open for 2% of the time, Pallas kernels for 10%

profile of v3, /device:TPU:0, one launch (start us, length us, event | category | flops | bytes accessed | tf_op | source)
XLA Modules:
  0.0 65.2 jit_solution(15162038379897822279)
XLA Ops:
  0.6 0.7 %convert_element_type.13 = bf16[1,256]{1,0:T(2,128)(2,1)S(1)} convert(s32[1,256]{1,0:T(1,128)} %sr_r.1) | non-fusion elementwise | flops 256 | bytes 1536 | tf_op jit(solution)/shard_map/convert_element_type | solution.py:281
  1.3 1.0 %fusion.2 = (bf16[128,512]{1,0:T(8,128)(2,1)S(1)}, bf16[128,512]{1,0:T(8,128)(2,1)S(1)}) fusion(s32[]{:T(128)S(6)} %select_n.22, bf16[256,256]{1,0:T(8,128)(2,1)} %adj_r.1, bf16[256,256]{1,0:T(8,128)(2,1)} %couple_r.1, bf16[256,512]{1,0:T(8,128)(2,1)} %feats_r.1), kind=kLoop, calls=%fused_computation.5 | loop fusion | flops 262144 | bytes 655364 | tf_op jit(solution)/shard_map/concatenate | solution.py:280
  2.3 4.1 %collective-permute-start.2 = (bf16[272,512]{1,0:T(8,128)(2,1)S(1)}, bf16[272,512]{1,0:T(8,128)(2,1)S(1)}, u32[]{:S(2)}, u32[]{:S(2)}) collective-permute-start(bf16[272,512]{1,0:T(8,128)(2,1)S(1)} %fusion.1), channel_id=1, source_target_pairs={{0,16},{2,18},{4,20},{6,22},{8,24},{10,26},{12,28},{14,30},{16,0},... | collective-permute-start | bytes 835592 | tf_op jit(solution)/shard_map/ppermute | solution.py:22
  6.5 1.5 %collective-permute-start = (bf16[272,512]{1,0:T(8,128)(2,1)S(1)}, bf16[272,512]{1,0:T(8,128)(2,1)S(1)}, u32[]{:S(2)}, u32[]{:S(2)}) collective-permute-start(bf16[272,512]{1,0:T(8,128)(2,1)S(1)} %fusion.1), channel_id=1, source_target_pairs={{0,2},{2,0},{4,6},{6,4},{8,10},{10,8},{12,14},{14,12},{16,18},{18,... | collective-permute-start | bytes 835592 | tf_op jit(solution)/shard_map/ppermute | solution.py:22
  8.0 11.1 %collective-permute-done.2.refs_2_ = bf16[272,512]{1,0:T(8,128)(2,1)S(1)} collective-permute-done((bf16[272,512]{1,0:T(8,128)(2,1)S(1)}, bf16[272,512]{1,0:T(8,128)(2,1)S(1)}, u32[]{:S(2)}, u32[]{:S(2)}) %collective-permute-start.2) | collective-permute-done | bytes 278560 | tf_op jit(solution)/shard_map/ppermute | solution.py:22
  19.1 1.5 %collective-permute-start.4 = (bf16[272,512]{1,0:T(8,128)(2,1)S(1)}, bf16[272,512]{1,0:T(8,128)(2,1)S(1)}, u32[]{:S(2)}, u32[]{:S(2)}) collective-permute-start(bf16[272,512]{1,0:T(8,128)(2,1)S(1)} %collective-permute-done.2.refs_2_), channel_id=1, source_target_pairs={{0,2},{2,0},{4,6},{6,4},{8,10},{10,8},{12,14},{14,12},{16,18},{18,... | collective-permute-start | bytes 835592 | tf_op jit(solution)/shard_map/ppermute | solution.py:22
  20.6 0.9 %constant_dynamic-slice_fusion = bf16[128,512]{1,0:T(8,128)(2,1)S(1)} fusion(bf16[256,512]{1,0:T(8,128)(2,1)} %cot_r.1, s32[]{:T(128)S(6)} %select_n.22), kind=kLoop, calls=%fused_computation.7 | loop fusion | bytes 262148 | tf_op jit(solution)/shard_map/dynamic_slice | solution.py:284
  21.6 0.1 collective-permute-start.9
  21.6 0.1 collective-permute-start.3
  21.7 8.2 %collective-permute-done.9.refs_2_ = bf16[128,512]{1,0:T(8,128)(2,1)S(1)} collective-permute-done((bf16[128,512]{1,0:T(8,128)(2,1)S(1)}, bf16[128,512]{1,0:T(8,128)(2,1)S(1)}, u32[]{:S(2)}, u32[]{:S(2)}) %collective-permute-start.9) | collective-permute-done | bytes 131104 | tf_op jit(solution)/shard_map/ppermute | solution.py:22
  29.9 0.5 collective-permute-start.7
  30.5 0.5 collective-permute-start.5
  31.0 5.2 %collective-permute-done.7.refs_0_ = bf16[128,512]{1,0:T(8,128)(2,1)S(1)} collective-permute-done((bf16[128,512]{1,0:T(8,128)(2,1)S(1)}, bf16[128,512]{1,0:T(8,128)(2,1)S(1)}, u32[]{:S(2)}, u32[]{:S(2)}) %collective-permute-start.7) | collective-permute-done | bytes 131104 | tf_op jit(solution)/shard_map/ppermute | solution.py:22
  36.1 5.0 %collective-permute-done.11.refs_4_ = bf16[128,512]{1,0:T(8,128)(2,1)S(1)} collective-permute-done((bf16[128,512]{1,0:T(8,128)(2,1)S(1)}, bf16[128,512]{1,0:T(8,128)(2,1)S(1)}, u32[]{:S(2)}, u32[]{:S(2)}) %collective-permute-start.11) | collective-permute-done | bytes 131104 | tf_op jit(solution)/shard_map/ppermute | solution.py:22
  41.1 0.5 collective-permute-start.8
  41.6 0.1 collective-permute-start.12
  41.7 0.1 pad_add_fusion.sc
  41.8 0.9 %copy-done.1 = bf16[256,512]{1,0:T(8,128)(2,1)S(1)} copy-done((bf16[256,512]{1,0:T(8,128)(2,1)S(1)}, bf16[256,512]{1,0:T(8,128)(2,1)}, u32[]{:S(2)}) %copy-start.1) | copy-done | bytes 262168
  42.7 1.0 %copy-done.2 = bf16[512,512]{1,0:T(8,128)(2,1)S(1)} copy-done((bf16[512,512]{1,0:T(8,128)(2,1)S(1)}, bf16[512,512]{1,0:T(8,128)(2,1)}, u32[]{:S(2)}) %copy-start.2) | copy-done | bytes 524312
  43.8 0.9 %copy-done.3 = bf16[256,256]{1,0:T(8,128)(2,1)S(1)} copy-done((bf16[256,256]{1,0:T(8,128)(2,1)S(1)}, bf16[256,256]{1,0:T(8,128)(2,1)}, u32[]{:S(2)}) %copy-start.3) | copy-done | bytes 131096
  44.7 0.9 %copy-done.4 = bf16[256,256]{1,0:T(8,128)(2,1)S(1)} copy-done((bf16[256,256]{1,0:T(8,128)(2,1)S(1)}, bf16[256,256]{1,0:T(8,128)(2,1)}, u32[]{:S(2)}) %copy-start.4) | copy-done | bytes 131096
  45.6 0.7 %copy-done.5 = s32[1,256]{1,0:T(1,128)S(1)} copy-done((s32[1,256]{1,0:T(1,128)S(1)}, s32[1,256]{1,0:T(1,128)}, u32[]{:S(2)}) %copy-start.5) | copy-done | bytes 1048
  46.3 3.5 %first_layer.1 = (bf16[4,256,512]{2,1,0:T(8,128)(2,1)S(1)}, bf16[4,256,512]{2,1,0:T(8,128)(2,1)S(1)}, bf16[4,256,512]{2,1,0:T(8,128)(2,1)S(1)}, f32[4,256,512]{2...) custom-call(s32[4]{0:T(128)S(1)} %pad_add_fusion.sc, ...), custom_call_target="tpu_custom_call" | custom-call | tf_op jit(solution)/shard_map/first_layer/pallas_call | solution.py:88
  49.7 0.0 copy-start
  49.8 3.1 %later_layers.1 = (bf16[256,512]{1,0:T(8,128)(2,1)}, bf16[1,4,256,512]{3,2,1,0:T(8,128)(2,1)S(1)}, f32[1,4,256,512]{3,2,1,0:T(8,128)S(1)}) custom-call(s32[4]{0:T(128)S(1)} %pad_add_fusion.sc, bf16[4,256,512]{2,1,0:T(8,128)(2,1)S(1)} %get-tuple-element.29.x0_r, bf16[4,256,512]{2,1,0:T(8,128)(2,1)S(1)} %get-tuple-element.30.x1_r, ...), custom_call_target="tpu_custom_call" | custom-call | tf_op jit(solution)/shard_map/later_layers/pallas_call | solution.py:149
  52.9 4.8 %backward.1 = (f32[256,256]{1,0:T(8,128)}, f32[32,512]{1,0:T(8,128)S(1)}, bf16[32,512]{1,0:T(8,128)(2,1)S(1)}, bf16[32,512]{1,0:T(8,128)(2,1)S(1)}, bf16[32,512]{1,0:T(8,128)(2,1)S(1)}) custom-call(s32[4]{0:T(128)S(1)} %pad_add_fusion.sc, bf16[256,512]{1,0:T(8,128)(2,1)S(1)} %copy-done, bf16[128,512]{1,0:T(8,128)(2,1)S(1)} %collective-permute-done.7.refs_0_, ...), custom_call_target="tpu_custom_call" | custom-call | tf_op jit(solution)/shard_map/backward/pallas_call | solution.py:246
  57.6 3.0 %collective-permute-start.14 = (bf16[32,512]{1,0:T(8,128)(2,1)S(1)}, bf16[32,512]{1,0:T(8,128)(2,1)S(1)}, u32[]{:S(2)}, u32[]{:S(2)}) collective-permute-start(bf16[32,512]{1,0:T(8,128)(2,1)S(1)} %get-tuple-element.40), channel_id=1, source_target_pairs={{0,8},{2,10},{4,12},{6,14},{8,0},{10,2},{12,4},{14,6},{16,24},{18,... | collective-permute-start | bytes 98312 | tf_op jit(solution)/shard_map/ppermute | solution.py:22
  60.6 0.5 collective-permute-start.15
  61.1 1.5 %collective-permute-done.13 = bf16[32,512]{1,0:T(8,128)(2,1)S(1)} collective-permute-done((bf16[32,512]{1,0:T(8,128)(2,1)S(1)}, bf16[32,512]{1,0:T(8,128)(2,1)S(1)}, u32[]{:S(2)}, u32[]{:S(2)}) %collective-permute-start.13) | collective-permute-done | bytes 32800 | tf_op jit(solution)/shard_map/ppermute | solution.py:22
  62.6 0.4 collective-permute-done.14
  63.0 1.5 %collective-permute-done.15 = bf16[32,512]{1,0:T(8,128)(2,1)S(1)} collective-permute-done((bf16[32,512]{1,0:T(8,128)(2,1)S(1)}, bf16[32,512]{1,0:T(8,128)(2,1)S(1)}, u32[]{:S(2)}, u32[]{:S(2)}) %collective-permute-start.15) | collective-permute-done | bytes 32800 | tf_op jit(solution)/shard_map/ppermute | solution.py:22
  64.5 0.6 add_bitcast_fusion
  (21 shorter events, 0.1 us)
Async XLA Ops:
  2.3 16.8 %collective-permute-start.2 = (bf16[272,512]{1,0:T(8,128)(2,1)S(1)}, bf16[272,512]{1,0:T(8,128)(2,1)S(1)}, u32[]{:S(2)}, u32[]{:S(2)}) collective-permute-start(bf16[272,512]{1,0:T(8,128)(2,1)S(1)} %fusion.1), channel_id=1, source_target_pairs={{0,16},{2,18},{4,20},{6,22},{8,24},{10,26},{12,28},{14,30},{16,0},... | collective-permute-start | bytes 835592 | tf_op jit(solution)/shard_map/ppermute | solution.py:22
  6.5 34.6 %collective-permute-start.6 = (bf16[512,512]{1,0:T(8,128)(2,1)}, bf16[512,512]{1,0:T(8,128)(2,1)S(1)}, u32[]{:S(2)}, u32[]{:S(2)}) collective-permute-start(bf16[512,512]{1,0:T(8,128)(2,1)} %refs_6_.1), channel_id=1, source_target_pairs={{0,1},{1,0},{2,3},{3,2},{4,5},{5,4},{6,7},{7,6},{8,9},{9,8},{10,11... | collective-permute-start | bytes 1572872 | tf_op jit(solution)/shard_map/ppermute | solution.py:27
  6.5 24.0 %collective-permute-start = (bf16[272,512]{1,0:T(8,128)(2,1)S(1)}, bf16[272,512]{1,0:T(8,128)(2,1)S(1)}, u32[]{:S(2)}, u32[]{:S(2)}) collective-permute-start(bf16[272,512]{1,0:T(8,128)(2,1)S(1)} %fusion.1), channel_id=1, source_target_pairs={{0,2},{2,0},{4,6},{6,4},{8,10},{10,8},{12,14},{14,12},{16,18},{18,... | collective-permute-start | bytes 835592 | tf_op jit(solution)/shard_map/ppermute | solution.py:22
  19.1 11.4 %collective-permute-start.4 = (bf16[272,512]{1,0:T(8,128)(2,1)S(1)}, bf16[272,512]{1,0:T(8,128)(2,1)S(1)}, u32[]{:S(2)}, u32[]{:S(2)}) collective-permute-start(bf16[272,512]{1,0:T(8,128)(2,1)S(1)} %collective-permute-done.2.refs_2_), channel_id=1, source_target_pairs={{0,2},{2,0},{4,6},{6,4},{8,10},{10,8},{12,14},{14,12},{16,18},{18,... | collective-permute-start | bytes 835592 | tf_op jit(solution)/shard_map/ppermute | solution.py:22
  21.6 8.4 %collective-permute-start.9 = (bf16[128,512]{1,0:T(8,128)(2,1)S(1)}, bf16[128,512]{1,0:T(8,128)(2,1)S(1)}, u32[]{:S(2)}, u32[]{:S(2)}) collective-permute-start(bf16[128,512]{1,0:T(8,128)(2,1)S(1)} %constant_dynamic-slice_fusion), channel_id=1, source_target_pairs={{0,16},{2,18},{4,20},{6,22},{8,24},{10,26},{12,28},{14,30},{16,0},... | collective-permute-start | bytes 393224 | tf_op jit(solution)/shard_map/ppermute | solution.py:22
  21.6 20.0 %collective-permute-start.3 = (bf16[272,512]{1,0:T(8,128)(2,1)S(1)}, bf16[272,512]{1,0:T(8,128)(2,1)S(1)}, u32[]{:S(2)}, u32[]{:S(2)}) collective-permute-start(bf16[272,512]{1,0:T(8,128)(2,1)S(1)} %collective-permute-done.2.refs_2_), channel_id=1, source_target_pairs={{0,1},{1,0},{2,3},{3,2},{4,5},{5,4},{6,7},{7,6},{8,9},{9,8},{10,11... | collective-permute-start | bytes 835592 | tf_op jit(solution)/shard_map/ppermute | solution.py:27
  29.9 6.2 %collective-permute-start.7 = (bf16[128,512]{1,0:T(8,128)(2,1)S(1)}, bf16[128,512]{1,0:T(8,128)(2,1)S(1)}, u32[]{:S(2)}, u32[]{:S(2)}) collective-permute-start(bf16[128,512]{1,0:T(8,128)(2,1)S(1)} %constant_dynamic-slice_fusion), channel_id=1, source_target_pairs={{0,2},{2,0},{4,6},{6,4},{8,10},{10,8},{12,14},{14,12},{16,18},{18,... | collective-permute-start | bytes 393224 | tf_op jit(solution)/shard_map/ppermute | solution.py:22
  30.5 11.3 %collective-permute-start.1 = (bf16[272,512]{1,0:T(8,128)(2,1)S(1)}, bf16[272,512]{1,0:T(8,128)(2,1)S(1)}, u32[]{:S(2)}, u32[]{:S(2)}) collective-permute-start(bf16[272,512]{1,0:T(8,128)(2,1)S(1)} %collective-permute-done.refs_0_), channel_id=1, source_target_pairs={{0,1},{1,0},{2,3},{3,2},{4,5},{5,4},{6,7},{7,6},{8,9},{9,8},{10,11... | collective-permute-start | bytes 835592 | tf_op jit(solution)/shard_map/ppermute | solution.py:27
  30.5 11.3 %collective-permute-start.5 = (bf16[272,512]{1,0:T(8,128)(2,1)S(1)}, bf16[272,512]{1,0:T(8,128)(2,1)S(1)}, u32[]{:S(2)}, u32[]{:S(2)}) collective-permute-start(bf16[272,512]{1,0:T(8,128)(2,1)S(1)} %collective-permute-done.4.refs_4_), channel_id=1, source_target_pairs={{0,1},{1,0},{2,3},{3,2},{4,5},{5,4},{6,7},{7,6},{8,9},{9,8},{10,11... | collective-permute-start | bytes 835592 | tf_op jit(solution)/shard_map/ppermute | solution.py:27
  36.1 5.0 %collective-permute-start.11 = (bf16[128,512]{1,0:T(8,128)(2,1)S(1)}, bf16[128,512]{1,0:T(8,128)(2,1)S(1)}, u32[]{:S(2)}, u32[]{:S(2)}) collective-permute-start(bf16[128,512]{1,0:T(8,128)(2,1)S(1)} %collective-permute-done.9.refs_2_), channel_id=1, source_target_pairs={{0,2},{2,0},{4,6},{6,4},{8,10},{10,8},{12,14},{14,12},{16,18},{18,... | collective-permute-start | bytes 393224 | tf_op jit(solution)/shard_map/ppermute | solution.py:22
  41.1 11.7 %collective-permute-start.10 = (bf16[128,512]{1,0:T(8,128)(2,1)S(1)}, bf16[128,512]{1,0:T(8,128)(2,1)S(1)}, u32[]{:S(2)}, u32[]{:S(2)}) collective-permute-start(bf16[128,512]{1,0:T(8,128)(2,1)S(1)} %collective-permute-done.9.refs_2_), channel_id=1, source_target_pairs={{0,1},{1,0},{2,3},{3,2},{4,5},{5,4},{6,7},{7,6},{8,9},{9,8},{10,11... | collective-permute-start | bytes 393224 | tf_op jit(solution)/shard_map/ppermute | solution.py:27
  41.1 11.7 %collective-permute-start.8 = (bf16[128,512]{1,0:T(8,128)(2,1)S(1)}, bf16[128,512]{1,0:T(8,128)(2,1)S(1)}, u32[]{:S(2)}, u32[]{:S(2)}) collective-permute-start(bf16[128,512]{1,0:T(8,128)(2,1)S(1)} %collective-permute-done.7.refs_0_), channel_id=1, source_target_pairs={{0,1},{1,0},{2,3},{3,2},{4,5},{5,4},{6,7},{7,6},{8,9},{9,8},{10,11... | collective-permute-start | bytes 393224 | tf_op jit(solution)/shard_map/ppermute | solution.py:27
  41.6 11.2 %collective-permute-start.12 = (bf16[128,512]{1,0:T(8,128)(2,1)S(1)}, bf16[128,512]{1,0:T(8,128)(2,1)S(1)}, u32[]{:S(2)}, u32[]{:S(2)}) collective-permute-start(bf16[128,512]{1,0:T(8,128)(2,1)S(1)} %collective-permute-done.11.refs_4_), channel_id=1, source_target_pairs={{0,1},{1,0},{2,3},{3,2},{4,5},{5,4},{6,7},{7,6},{8,9},{9,8},{10,11... | collective-permute-start | bytes 393224 | tf_op jit(solution)/shard_map/ppermute | solution.py:27
  41.8 1.0 %copy-start.1 = (bf16[256,512]{1,0:T(8,128)(2,1)S(1)}, bf16[256,512]{1,0:T(8,128)(2,1)}, u32[]{:S(2)}) copy-start(bf16[256,512]{1,0:T(8,128)(2,1)} %feats_r.1) | copy-start | bytes 786436
  42.7 1.0 %copy-start.2 = (bf16[512,512]{1,0:T(8,128)(2,1)S(1)}, bf16[512,512]{1,0:T(8,128)(2,1)}, u32[]{:S(2)}) copy-start(bf16[512,512]{1,0:T(8,128)(2,1)} %refs_6_.1) | copy-start | bytes 1572868
  43.8 0.9 %copy-start.3 = (bf16[256,256]{1,0:T(8,128)(2,1)S(1)}, bf16[256,256]{1,0:T(8,128)(2,1)}, u32[]{:S(2)}) copy-start(bf16[256,256]{1,0:T(8,128)(2,1)} %adj_r.1) | copy-start | bytes 393220
  44.7 0.9 %copy-start.4 = (bf16[256,256]{1,0:T(8,128)(2,1)S(1)}, bf16[256,256]{1,0:T(8,128)(2,1)}, u32[]{:S(2)}) copy-start(bf16[256,256]{1,0:T(8,128)(2,1)} %couple_r.1) | copy-start | bytes 393220
  45.6 0.7 %copy-start.5 = (s32[1,256]{1,0:T(1,128)S(1)}, s32[1,256]{1,0:T(1,128)}, u32[]{:S(2)}) copy-start(s32[1,256]{1,0:T(1,128)} %sr_r.1) | copy-start | bytes 3076
  49.7 3.1 %copy-start = (bf16[256,512]{1,0:T(8,128)(2,1)S(1)}, bf16[256,512]{1,0:T(8,128)(2,1)}, u32[]{:S(2)}) copy-start(bf16[256,512]{1,0:T(8,128)(2,1)} %cot_r.1) | copy-start | bytes 786436
  57.6 5.0 %collective-permute-start.13 = (bf16[32,512]{1,0:T(8,128)(2,1)S(1)}, bf16[32,512]{1,0:T(8,128)(2,1)S(1)}, u32[]{:S(2)}, u32[]{:S(2)}) collective-permute-start(bf16[32,512]{1,0:T(8,128)(2,1)S(1)} %get-tuple-element.39), channel_id=1, source_target_pairs={{0,12},{2,14},{4,8},{6,10},{8,4},{10,6},{12,0},{14,2},{16,28},{18,... | collective-permute-start | bytes 98312 | tf_op jit(solution)/shard_map/ppermute | solution.py:22
  57.6 5.4 %collective-permute-start.14 = (bf16[32,512]{1,0:T(8,128)(2,1)S(1)}, bf16[32,512]{1,0:T(8,128)(2,1)S(1)}, u32[]{:S(2)}, u32[]{:S(2)}) collective-permute-start(bf16[32,512]{1,0:T(8,128)(2,1)S(1)} %get-tuple-element.40), channel_id=1, source_target_pairs={{0,8},{2,10},{4,12},{6,14},{8,0},{10,2},{12,4},{14,6},{16,24},{18,... | collective-permute-start | bytes 98312 | tf_op jit(solution)/shard_map/ppermute | solution.py:22
  60.6 3.9 %collective-permute-start.15 = (bf16[32,512]{1,0:T(8,128)(2,1)S(1)}, bf16[32,512]{1,0:T(8,128)(2,1)S(1)}, u32[]{:S(2)}, u32[]{:S(2)}) collective-permute-start(bf16[32,512]{1,0:T(8,128)(2,1)S(1)} %get-tuple-element.41), channel_id=1, source_target_pairs={{0,4},{2,6},{4,0},{6,2},{8,12},{10,14},{12,8},{14,10},{16,20},{18,... | collective-permute-start | bytes 98312 | tf_op jit(solution)/shard_map/ppermute | solution.py:22

commit v4 on v3

v4 whole, which is shorter than its diff:
```python
import math

import jax
import jax.numpy as jnp
from jax import lax
from jax.experimental import pallas as pl
from jax.experimental.pallas import tpu as pltpu
from jax.sharding import PartitionSpec as P


SHARE = 0.1
BETA_SCALE = 0.5
BF16 = jnp.bfloat16
F32 = jnp.float32


def vmem_of(layers):
    return min(60, 14 + 6 * layers) << 20


def swapped(x, mask):
    return lax.ppermute(x, "dom", [(i, i ^ mask) for i in range(lax.axis_size("dom"))])


def every_piece(x):
    n = lax.axis_size("segment")
    return [x] + [lax.ppermute(x, "segment", [(i, (i + k) % n) for i in range(n)]) for k in range(1, n)]


def beta_of(k):
    return math.log(BETA_SCALE / (k + 1.0) + 1.0)


def mm(a, b):
    return jnp.dot(a, b, preferred_element_type=F32)


def mm_nt(a, b):
    return lax.dot_general(a, b, (((1,), (1,)), ((), ())), preferred_element_type=F32)


def mm_tn(a, b):
    return lax.dot_general(a, b, (((0,), (0,)), ((), ())), preferred_element_type=F32)


def place_of(seg, k, n):
    return lax.rem(seg - k + n, n)


def pack_call(scalars, feats, adj, couple, send_rows, cot, layers):
    rows, width = feats.shape
    piece = rows // layers
    picked = send_rows.shape[1]

    def body(sc, feats_r, adj_r, couple_r, sr_r, cot_r, fwd_o, cot_o, sr_s, sems):
        at = pl.ds(pl.multiple_of(sc[0] * piece, piece), piece)
        split = adj_r.shape[1]
        copies = [
            pltpu.make_async_copy(feats_r.at[at, :], fwd_o.at[:piece, :], sems.at[0]),
            pltpu.make_async_copy(adj_r.at[at, :], fwd_o.at[piece : 2 * piece, :split], sems.at[1]),
            pltpu.make_async_copy(couple_r.at[at, :], fwd_o.at[piece : 2 * piece, split:], sems.at[2]),
            pltpu.make_async_copy(cot_r.at[at, :], cot_o, sems.at[3]),
        ]
        sr_copy = pltpu.make_async_copy(sr_r, sr_s, sems.at[4])
        sr_copy.start()
        for c in copies:
            c.start()
        fwd_o[2 * piece :, picked:] = jnp.zeros((16, width - picked), BF16)
        sr_copy.wait()
        fwd_o[2 * piece :, :picked] = jnp.broadcast_to(sr_s[...].astype(F32), (16, picked)).astype(BF16)
        for c in copies:
            c.wait()

    vm = pl.BlockSpec(memory_space=pltpu.VMEM)
    hbm = pl.BlockSpec(memory_space=pltpu.HBM)
    return pl.pallas_call(
        body,
        out_shape=(
            jax.ShapeDtypeStruct((2 * piece + 16, width), BF16),
            jax.ShapeDtypeStruct((piece, width), BF16),
        ),
        in_specs=[pl.BlockSpec(memory_space=pltpu.SMEM), hbm, hbm, hbm, hbm, hbm],
        out_specs=(vm, vm),
        scratch_shapes=[pltpu.VMEM(send_rows.shape, jnp.int32), pltpu.SemaphoreType.DMA((5,))],
        compiler_params=pltpu.CompilerParams(vmem_limit_bytes=4 << 20),
        name="pack",
    )(scalars, feats, adj, couple, send_rows, cot)


def picks_of(sr, rows):
    ids = lax.broadcasted_iota(jnp.int32, (rows, sr.shape[1]), 0).astype(F32)
    return (ids == sr).astype(F32).astype(BF16)


def mixed_of(agg, first):
    return ((1.0 - SHARE) * agg + SHARE * first.astype(F32)).astype(BF16)


def activate(mixed, w, k):
    beta = beta_of(k)
    pre = (1.0 - beta) * mixed.astype(F32) + beta * mm(mixed, w)
    sig = 1.0 / (1.0 + jnp.exp(-pre))
    out = pre * sig
    return sig + out * (1.0 - sig), out.astype(BF16)


def own_part_call(scalars, feats, adj, couple, send_rows, near, far, w_pieces):
    layers = len(w_pieces)
    rows, width = feats.shape
    piece = rows // layers
    bound = couple.shape[1] // 2

    def body(sc, feats_r, adj_r, couple_r, sr_r, *refs):
        got_r = [refs[g * layers : (g + 1) * layers] for g in range(2)]
        w_r = refs[2 * layers : 3 * layers]
        outs = refs[3 * layers :]
        x_o, own_o, near_o, far_o, cp_o, pick_o, agg_o, mix_o, slope_o, x1_o, w_o = outs[:11]
        ac_s, couple_s, sr_s, sems = outs[11:]
        seg = sc[0]
        copies = [
            pltpu.make_async_copy(sr_r, sr_s, sems.at[0]),
            pltpu.make_async_copy(couple_r, couple_s, sems.at[1]),
            pltpu.make_async_copy(feats_r, x_o.at[0], sems.at[2]),
            pltpu.make_async_copy(adj_r, own_o.at[0], sems.at[3]),
            pltpu.make_async_copy(w_r[0], w_o.at[seg], sems.at[4]),
        ]
        for c in copies:
            c.start()
        for g in range(2):
            for k in range(layers):
                at = pl.ds(pl.multiple_of(place_of(seg, k, layers) * piece, piece), piece)
                x_o[g + 1, at, :] = got_r[g][k][:piece, :]
                own_o[g + 1, at, :] = got_r[g][k][piece : 2 * piece, :rows]
                ac_s[g, at, :] = got_r[g][k][piece : 2 * piece, rows:]
        for k in range(1, layers):
            w_o[place_of(seg, k, layers)] = w_r[k][...]
        for c in copies:
            c.wait()
        picks = [picks_of(sr_s[...].astype(F32), rows)]
        for g in range(2):
            picks.append(picks_of(got_r[g][0][2 * piece : 2 * piece + 1, : 2 * bound].astype(F32), rows))
        near_o[0] = mm_nt(couple_s[:, :bound], picks[1][:, :bound]).astype(BF16)
        far_o[0] = mm_nt(couple_s[:, bound:], picks[2][:, bound:]).astype(BF16)
        near_o[1] = mm_nt(ac_s[0, :, :bound], picks[0][:, :bound]).astype(BF16)
        far_o[1] = mm_nt(ac_s[1, :, bound:], picks[0][:, bound:]).astype(BF16)
        cp_o[0] = ac_s[0, :, bound:]
        cp_o[1] = ac_s[1, :, :bound]
        pick_o[0] = picks[1][:, bound:]
        pick_o[1] = picks[2][:, :bound]
        agg_o[0] = mm(own_o[1], x_o[1]) + mm(near_o[1], x_o[0])
        agg_o[1] = mm(own_o[2], x_o[2]) + mm(far_o[1], x_o[0])
        agg = mm(own_o[0], x_o[0]) + mm(near_o[0], x_o[1]) + mm(far_o[0], x_o[2])
        mixed = mixed_of(agg, x_o[0])
        mix_o[...] = mixed
        slope_o[...], x1_o[...] = activate(mixed, w_o[0], 0)

    hbm = pl.BlockSpec(memory_space=pltpu.HBM)
    vm = pl.BlockSpec(memory_space=pltpu.VMEM)
    sds = jax.ShapeDtypeStruct
    return pl.pallas_call(
        body,
        out_shape=(
            sds((3, rows, width), BF16),
            sds((3, rows, rows), BF16),
            sds((2, rows, rows), BF16),
            sds((2, rows, rows), BF16),
            sds((2, rows, bound), BF16),
            sds((2, rows, bound), BF16),
            sds((2, rows, width), F32),
            sds((rows, width), BF16),
            sds((rows, width), F32),
            sds((rows, width), BF16),
            sds((layers, width, width), BF16),
        ),
        in_specs=[pl.BlockSpec(memory_space=pltpu.SMEM)] + [hbm] * 4 + [vm] * (2 * layers) + [hbm] + [vm] * (layers - 1),
        out_specs=(vm,) * 11,
        scratch_shapes=[
            pltpu.VMEM((2, rows, 2 * bound), BF16),
            pltpu.VMEM((rows, 2 * bound), BF16),
            pltpu.VMEM(send_rows.shape, jnp.int32),
            pltpu.SemaphoreType.DMA((5,)),
        ],
        compiler_params=pltpu.CompilerParams(vmem_limit_bytes=vmem_of(layers)),
        name="own_part",
    )(scalars, feats, adj, couple, send_rows, *near, *far, *w_pieces)


def rest_part_call(scalars, diag, part):
    x, _, _, _, cp, pick, agg, _, _, _, w = part
    layers = w.shape[0]
    _, rows, width = x.shape
    piece = rows // layers
    bound = cp.shape[2]

    def body(sc, *refs):
        got_r = refs[:layers]
        x_r, cp_r, pick_r, agg_r, w_r, x3_o, own3_o, near_o, far_o, mix_o, slope_o, x1_o, ac_s = refs[layers:]
        seg = sc[0]
        for k in range(layers):
            at = pl.ds(pl.multiple_of(place_of(seg, k, layers) * piece, piece), piece)
            x3_o[at, :] = got_r[k][:piece, :]
            own3_o[at, :] = got_r[k][piece : 2 * piece, :rows]
            ac_s[at, :] = got_r[k][piece : 2 * piece, rows:]
        picks = picks_of(got_r[0][2 * piece : 2 * piece + 1, : 2 * bound].astype(F32), rows)
        far_o[0] = mm_nt(cp_r[0], picks[:, bound:]).astype(BF16)
        near_o[0] = mm_nt(cp_r[1], picks[:, :bound]).astype(BF16)
        near_o[1] = mm_nt(ac_s[:, :bound], pick_r[1]).astype(BF16)
        far_o[1] = mm_nt(ac_s[:, bound:], pick_r[0]).astype(BF16)
        for g in range(3):
            if g == 0:
                sums = agg_r[0] + mm(far_o[0], x3_o[...])
            elif g == 1:
                sums = agg_r[1] + mm(near_o[0], x3_o[...])
            else:
                sums = mm(own3_o[...], x3_o[...]) + mm(near_o[1], x_r[2]) + mm(far_o[1], x_r[1])
            mixed = mixed_of(sums, x_r[g + 1] if g < 2 else x3_o[...])
            mix_o[g] = mixed
            slope_o[g], x1_o[g] = activate(mixed, w_r[0], 0)

    vm = pl.BlockSpec(memory_space=pltpu.VMEM)
    sds = jax.ShapeDtypeStruct
    return pl.pallas_call(
        body,
        out_shape=(
            sds((rows, width), BF16),
            sds((rows, rows), BF16),
            sds((2, rows, rows), BF16),
            sds((2, rows, rows), BF16),
            sds((3, rows, width), BF16),
            sds((3, rows, width), F32),
            sds((3, rows, width), BF16),
        ),
        in_specs=[pl.BlockSpec(memory_space=pltpu.SMEM)] + [vm] * (5 + layers),
        out_specs=(vm,) * 7,
        scratch_shapes=[pltpu.VMEM((rows, 2 * bound), BF16)],
        compiler_params=pltpu.CompilerParams(vmem_limit_bytes=vmem_of(layers)),
        name="rest_part",
    )(scalars, *diag, x, cp, pick, agg, w)


def blocks_at(own, near, far, own3, near3, far3):
    return (
        lambda g: own[g] if g < 3 else own3[...],
        lambda g: (near[0], near[1], near3[0], near3[1])[g],
        lambda g: (far[0], far3[0], far[1], far3[1])[g],
    )


def later_layers_call(scalars, part, rest):
    x, own, near, far, _, _, _, _, _, x1, w = part
    x3, own3, near3, far3, _, _, x1_rest = rest
    layers = w.shape[0]
    rows, width = x.shape[1:]

    def body(sc, x_r, own_r, near_r, far_r, x1_r, w_r, x3_r, own3_r, near3_r, far3_r, x1n_r, acts_o, mix_o, slope_o, xa_s, xb_s):
        seg = sc[0]
        own_at, near_at, far_at = blocks_at(own_r, near_r, far_r, own3_r, near3_r, far3_r)

        @pl.when(seg == 0)
        def _():
            acts_o[...] = x1_r[...]

        def src(g):
            return x1n_r[g - 1] if g else x1_r[...]

        for k in range(1, layers):
            dst = (xa_s, xb_s)[k % 2]
            for g in range(4):
                agg = mm(own_at(g), src(g)) + mm(near_at(g), src(g ^ 1)) + mm(far_at(g), src(g ^ 2))
                mixed = mixed_of(agg, x_r[g] if g < 3 else x3_r[...])
                mix_o[k - 1, g] = mixed
                slope_o[k - 1, g], out = activate(mixed, w_r[k], k)
                if k + 1 < layers:
                    dst[g] = out
                if g == 0:

                    @pl.when(seg == k)
                    def _():
                        acts_o[...] = out

            def src(g, dst=dst):
                return dst[g]

    vm = pl.BlockSpec(memory_space=pltpu.VMEM)
    return pl.pallas_call(
        body,
        out_shape=(
            jax.ShapeDtypeStruct((rows, width), BF16),
            jax.ShapeDtypeStruct((layers - 1, 4, rows, width), BF16),
            jax.ShapeDtypeStruct((layers - 1, 4, rows, width), F32),
        ),
        in_specs=[pl.BlockSpec(memory_space=pltpu.SMEM)] + [vm] * 11,
        out_specs=(vm,) * 3,
        scratch_shapes=[pltpu.VMEM((4, rows, width), BF16)] * 2,
        compiler_params=pltpu.CompilerParams(vmem_limit_bytes=vmem_of(layers)),
        name="later_layers",
    )(scalars, x, own, near, far, x1, w, x3, own3, near3, far3, x1_rest)


def backward_call(scalars, cot, got, part, rest, later_mix, later_slope):
    _, own, near, far, _, _, _, mix, slope, _, w = part
    _, own3, near3, far3, mix_rest, slope_rest, _ = rest
    layers = w.shape[0]
    rows, width = cot.shape
    piece = rows // layers
    n_dom = lax.axis_size("dom")
    others = n_dom // 4
    out_rows = width // n_dom
    half = width // 2

    def body(sc, cot_r, *refs):
        got_r = [refs[g * layers : (g + 1) * layers] for g in range(3)]
        own_r, near_r, far_r, mix_r, slope_r, w_r, own3_r, near3_r, far3_r, mixn_r, slopen_r, later_mix_r, later_slope_r = refs[
            3 * layers : 3 * layers + 13
        ]
        outs = refs[3 * layers + 13 :]
        dpre_o, carry_o, mine_o = outs[:3]
        send_o = outs[3 : 2 + others]
        up_s, dmix_s, part_s = outs[2 + others :]
        seg, low, high, place = sc[0], sc[1], sc[2], sc[3]
        own_at, near_at, far_at = blocks_at(own_r, near_r, far_r, own3_r, near3_r, far3_r)
        for g in range(3):
            for k in range(layers):
                at = pl.ds(pl.multiple_of(place_of(seg, k, layers) * piece, piece), piece)
                up_s[g + 1, at, :] = got_r[g][k][...]
        up_s[0] = cot_r[...]
        if layers == 1:
            carry_o[...] = jnp.zeros((rows, width), F32)
        for k in range(layers - 1, -1, -1):
            beta = beta_of(k)
            for g in range(4):
                slope_now = later_slope_r[k - 1, g] if k else (slopen_r[g - 1] if g else slope_r[...])
                dpre = (up_s[g].astype(F32) * slope_now).astype(BF16)
                dpre_o[pl.ds(g * rows, rows), :] = dpre
                if k:
                    dmix = ((1.0 - beta) * dpre.astype(F32) + beta * mm_nt(dpre, w_r[k])).astype(BF16)
                    dmix_s[g] = dmix
                    if g == 0:
                        carry_o[...] = SHARE * dmix.astype(F32) + (carry_o[...] if k + 1 < layers else 0.0)

            @pl.when(seg == k)
            def _():
                at = pl.ds(pl.multiple_of(high * half, half), half)
                part = jnp.zeros((half, width), F32)
                for g in range(4):
                    chosen = later_mix_r[k - 1, g, :, at] if k else (mixn_r[g - 1, :, at] if g else mix_r[:, at])
                    part = part + mm_tn(chosen, dpre_o[pl.ds(g * rows, rows), :])
                part_s[...] = beta * part

            if k:
                for g in range(4):
                    up_s[g] = (
                        (1.0 - SHARE)
                        * (
                            mm_tn(own_at(g), dmix_s[g])
                            + mm_tn(near_at(g ^ 1), dmix_s[g ^ 1])
                            + mm_tn(far_at(g ^ 2), dmix_s[g ^ 2])
                        )
                    ).astype(BF16)

        def block(m):
            at = (place ^ m) * (2 * out_rows) + low * out_rows
            return part_s[pl.ds(pl.multiple_of(at, out_rows), out_rows), :]

        mine_o[...] = block(0)
        for m in range(1, others):
            send_o[m - 1][...] = block(m).astype(BF16)

    vm = pl.BlockSpec(memory_space=pltpu.VMEM)
    sds = jax.ShapeDtypeStruct
    got_out = pl.pallas_call(
        body,
        out_shape=(sds((4 * rows, width), BF16), sds((rows, width), F32), sds((out_rows, width), F32))
        + tuple(sds((out_rows, width), BF16) for _ in range(1, others)),
        in_specs=[pl.BlockSpec(memory_space=pltpu.SMEM)] + [vm] * (1 + 3 * layers + 13),
        out_specs=(vm,) * (2 + others),
        scratch_shapes=[
            pltpu.VMEM((4, rows, width), BF16),
            pltpu.VMEM((4, rows, width), BF16),
            pltpu.VMEM((half, width), F32),
        ],
        compiler_params=pltpu.CompilerParams(vmem_limit_bytes=vmem_of(layers)),
        name="backward",
    )(
        scalars,
        cot,
        *[p for g in got for p in g],
        own,
        near,
        far,
        mix,
        slope,
        w,
        own3,
        near3,
        far3,
        mix_rest,
        slope_rest,
        later_mix,
        later_slope,
    )
    return got_out[0], got_out[1], got_out[2], got_out[3:]


def feat_call(scalars, dpre, carry, part):
    _, own, near, far, _, _, _, _, _, _, w = part
    layers = w.shape[0]
    rows, width = carry.shape
    cols = width // layers
    beta = beta_of(0)
    sliced = cols % 128 == 0
    kept = cols if sliced else width

    def body(sc, dpre_r, carry_r, own_r, near_r, far_r, w_r, feat_o):
        at = pl.ds(pl.multiple_of(sc[0] * cols, cols), cols) if sliced else slice(None)
        w_rows = w_r[0, at, :]
        dmix = []
        for g in range(3):
            d_at = pl.ds(g * rows, rows)
            through = mm_nt(dpre_r[d_at, :], w_rows)
            dmix.append(((1.0 - beta) * dpre_r[d_at, at].astype(F32) + beta * through).astype(BF16))
        sums = mm_tn(own_r[0], dmix[0]) + mm_tn(near_r[1], dmix[1]) + mm_tn(far_r[1], dmix[2])
        feat_o[...] = (1.0 - SHARE) * sums + (carry_r[:, at] + SHARE * dmix[0].astype(F32))

    vm = pl.BlockSpec(memory_space=pltpu.VMEM)
    feat = pl.pallas_call(
        body,
        out_shape=jax.ShapeDtypeStruct((rows, kept), F32),
        in_specs=[pl.BlockSpec(memory_space=pltpu.SMEM)] + [vm] * 6,
        out_specs=vm,
        compiler_params=pltpu.CompilerParams(vmem_limit_bytes=vmem_of(layers)),
        name="feat",
    )(scalars, dpre, carry, own, near, far, w)
    return feat if sliced else lax.dynamic_slice_in_dim(feat, scalars[0] * cols, cols, 1)


def step(feats, adj, couple, send_rows, weights, cot):
    seg = lax.axis_index("segment")
    dom = lax.axis_index("dom")
    layers = lax.axis_size("segment")
    n_dom = lax.axis_size("dom")
    top = n_dom // 2
    others = n_dom // 4
    place = (dom // 2) % others
    scalars = jnp.stack([seg, dom & 1, dom // top, place]).astype(jnp.int32)

    fwd_mine, cot_mine = pack_call(scalars, feats, adj, couple, send_rows, cot, layers)
    far_fwd = swapped(fwd_mine, top)
    near_fwd = swapped(fwd_mine, 1)
    near_cot = swapped(cot_mine, 1)
    w_pieces = every_piece(weights)
    near_fwd = every_piece(near_fwd)
    diag_fwd = swapped(far_fwd, 1)
    far_fwd = every_piece(far_fwd)
    far_cot = swapped(cot_mine, top)
    near_cot = every_piece(near_cot)
    part = own_part_call(scalars, feats, adj, couple, send_rows, near_fwd, far_fwd, w_pieces)
    diag_fwd = every_piece(diag_fwd)
    diag_cot = swapped(far_cot, 1)
    far_cot = every_piece(far_cot)
    rest = rest_part_call(scalars, diag_fwd, part)
    diag_cot = every_piece(diag_cot)
    acts, later_mix, later_slope = later_layers_call(scalars, part, rest)
    dpre, carry, wgrad, sends = backward_call(
        scalars, cot, [near_cot, far_cot, diag_cot], part, rest, later_mix, later_slope
    )
    for m in range(others - 1, 0, -1):
        wgrad = wgrad + swapped(sends[m - 1], 2 * m).astype(F32)
    feat = feat_call(scalars, dpre, carry, part)
    return (acts[None], wgrad[None], feat)


def solution(mesh):
    in_specs = (
        P("dom", None),
        P("dom", None),
        P("dom", None),
        P("dom", None),
        P("segment", None),
        P("dom", None),
    )
    out_specs = (P("segment", "dom", None), P("segment", "dom", None), P("dom", "segment"))
    return jax.shard_map(step, mesh=mesh, in_specs=in_specs, out_specs=out_specs, check_vma=False)
```

time: 65.5 us -> 64.5 us (0.985)
  waiting for transfers between devices: 32.9 us -> 26.1 us
  local copies, waits for them, and re-layouts: 5.39 us -> 8.87 us
  Pallas kernels: 11.3 us -> 13.9 us
  other arithmetic: 2.42 us -> 0.72 us
  starting transfers between devices: 12.4 us -> 13.8 us
    ppermute x9, waiting for transfers between devices: 32.9 us -> 26.1 us  [swapped(): lax.ppermute(x, 'dom', [(i, i ^ mask) for i in range(lax.axis_size('dom'))])]
    unnamed x12 -> x22, local copies, waits for them, and re-layouts: 4.48 us -> 8.87 us
    pallas_call x2 -> x5, Pallas kernels: 8.24 us -> 10.6 us  [the longest x1 3.08 us: backward_call(): pl.pallas_call(body, out_shape=(sds((4 * rows, width), BF16), sds((rows,...]
    ppermute x9, starting transfers between devices: 11.3 us -> 12.7 us  [swapped(): lax.ppermute(x, 'dom', [(i, i ^ mask) for i in range(lax.axis_size('dom'))])]
    concatenate x2 -> x0, other arithmetic: 1.01 us -> none  [the longest x1 0.99 us: step(): ac = jnp.concatenate([adj, couple], axis=1)]
    dynamic_slice x1 -> x0, local copies, waits for them, and re-layouts: 0.91 us -> none  [mine(): return lax.dynamic_slice_in_dim(x, seg * piece, piece, 0)]
    convert_element_type x1 -> x0, other arithmetic: 0.68 us -> none  [step(): send_rows[0].astype(BF16)]
  transfers between devices with their start and end apart: 16 -> 16, of which waited for: 7 -> 6; matrix products, arithmetic and copies ran while one was open for 2% -> 0% of each run, Pallas kernels for 10% -> 15%
where the time goes in v4:
time: 64.5 us; the launch traced here: 64.1 us
  waiting for transfers between devices  26.1 us (40%)
  Pallas kernels  13.9 us (22%)
  starting transfers between devices  13.8 us (21%)
  local copies, waits for them, and re-layouts  8.87 us (14%)
  between operations  0.76 us (1%)
  other arithmetic  0.72 us (1%)
    ppermute x9, waiting for transfers between devices, swapped(): lax.ppermute(x, 'dom', [(i, i ^ mask) for i in range(lax.axis_size('dom'))])  26.1 us
    ppermute x9, starting transfers between devices, swapped(): lax.ppermute(x, 'dom', [(i, i ^ mask) for i in range(lax.axis_size('dom'))])  12.7 us
    unnamed x22, local copies, waits for them, and re-layouts  8.87 us
    pallas_call x1, Pallas kernels, later_layers_call(): pl.pallas_call(body, out_shape=(jax.ShapeDtypeStruct((rows, width), BF16)...  3.22 us
    pallas_call x1, Pallas kernels, backward_call(): pl.pallas_call(body, out_shape=(sds((4 * rows, width), BF16), sds((rows,...  3.08 us
    pallas_call x1, Pallas kernels, own_part_call(): pl.pallas_call(body, out_shape=(sds((3, rows, width), BF16), sds((3, rows...  2.4 us
    pallas_call x1, Pallas kernels, rest_part_call(): pl.pallas_call(body, out_shape=(sds((rows, width), BF16), sds((rows, rows...  2.28 us
    pallas_call x1, Pallas kernels, feat_call(): pl.pallas_call(body, out_shape=jax.ShapeDtypeStruct((rows, kept), F32), i...  1.93 us
  transfers between devices with their start and end apart: 16, of which 6 were waited for; matrix products, arithmetic and copies ran while one was open for 0% of the time, Pallas kernels for 15%

profile of v4, /device:TPU:0, one launch (start us, length us, event | category | flops | bytes accessed | tf_op | source)
XLA Modules:
  0.0 64.1 jit_solution(13886759650499945389)
XLA Ops:
  0.7 0.9 %copy-done = bf16[256,512]{1,0:T(8,128)(2,1)S(1)} copy-done((bf16[256,512]{1,0:T(8,128)(2,1)S(1)}, bf16[256,512]{1,0:T(8,128)(2,1)}, u32[]{:S(2)}) %copy-start) | copy-done | bytes 262168
  1.7 0.9 %copy-done.2 = bf16[256,512]{1,0:T(8,128)(2,1)S(1)} copy-done((bf16[256,512]{1,0:T(8,128)(2,1)S(1)}, bf16[256,512]{1,0:T(8,128)(2,1)}, u32[]{:S(2)}) %copy-start.2) | copy-done | bytes 262168
  2.6 0.9 %copy-done.4 = bf16[256,256]{1,0:T(8,128)(2,1)S(1)} copy-done((bf16[256,256]{1,0:T(8,128)(2,1)S(1)}, bf16[256,256]{1,0:T(8,128)(2,1)}, u32[]{:S(2)}) %copy-start.4) | copy-done | bytes 131096
  3.6 0.9 %copy-done.6 = bf16[256,256]{1,0:T(8,128)(2,1)S(1)} copy-done((bf16[256,256]{1,0:T(8,128)(2,1)S(1)}, bf16[256,256]{1,0:T(8,128)(2,1)}, u32[]{:S(2)}) %copy-start.6) | copy-done | bytes 131096
  4.5 0.7 %copy-done.9 = s32[1,256]{1,0:T(1,128)S(1)} copy-done((s32[1,256]{1,0:T(1,128)S(1)}, s32[1,256]{1,0:T(1,128)}, u32[]{:S(2)}) %copy-start.9) | copy-done | bytes 1048
  5.1 1.0 %pack.1 = (bf16[272,512]{1,0:T(8,128)(2,1)S(1)}, bf16[128,512]{1,0:T(8,128)(2,1)S(1)}) custom-call(s32[4]{0:T(128)S(1)} %pad_add_fusion.sc, bf16[256,512]{1,0:T(8,128)(2,1)S(1)} %copy-done.2, bf16[256,256]{1,0:T(8,128)(2,1)S(1)} %copy-done.4, bf16[256,256]{1,0:T(8,128)(2,1)S(1)} %copy-done.6, s32[1,256]{1,0:T(1,128)S(1)} %copy-done.9, ...), custom_call_target="tpu_custom_call" | custom-call | tf_op jit(solution)/shard_map/pack/pallas_call | solution.py:76
  6.1 4.1 %collective-permute-start.2 = (bf16[272,512]{1,0:T(8,128)(2,1)S(1)}, bf16[272,512]{1,0:T(8,128)(2,1)S(1)}, u32[]{:S(2)}, u32[]{:S(2)}) collective-permute-start(bf16[272,512]{1,0:T(8,128)(2,1)S(1)} %get-tuple-element.32), channel_id=1, source_target_pairs={{0,16},{2,18},{4,20},{6,22},{8,24},{10,26},{12,28},{14,30},{16,0},... | collective-permute-start | bytes 835592 | tf_op jit(solution)/shard_map/ppermute | solution.py:22
  10.2 1.5 %collective-permute-start = (bf16[272,512]{1,0:T(8,128)(2,1)S(1)}, bf16[272,512]{1,0:T(8,128)(2,1)S(1)}, u32[]{:S(2)}, u32[]{:S(2)}) collective-permute-start(bf16[272,512]{1,0:T(8,128)(2,1)S(1)} %get-tuple-element.32), channel_id=1, source_target_pairs={{0,2},{2,0},{4,6},{6,4},{8,10},{10,8},{12,14},{14,12},{16,18},{18,... | collective-permute-start | bytes 835592 | tf_op jit(solution)/shard_map/ppermute | solution.py:22
  11.7 11.1 %collective-permute-done.2.refs_2_ = bf16[272,512]{1,0:T(8,128)(2,1)S(1)} collective-permute-done((bf16[272,512]{1,0:T(8,128)(2,1)S(1)}, bf16[272,512]{1,0:T(8,128)(2,1)S(1)}, u32[]{:S(2)}, u32[]{:S(2)}) %collective-permute-start.2) | collective-permute-done | bytes 278560 | tf_op jit(solution)/shard_map/ppermute | solution.py:22
  22.9 1.5 %collective-permute-start.5 = (bf16[272,512]{1,0:T(8,128)(2,1)S(1)}, bf16[272,512]{1,0:T(8,128)(2,1)S(1)}, u32[]{:S(2)}, u32[]{:S(2)}) collective-permute-start(bf16[272,512]{1,0:T(8,128)(2,1)S(1)} %collective-permute-done.2.refs_2_), channel_id=1, source_target_pairs={{0,2},{2,0},{4,6},{6,4},{8,10},{10,8},{12,14},{14,12},{16,18},{18,... | collective-permute-start | bytes 835592 | tf_op jit(solution)/shard_map/ppermute | solution.py:22
  24.4 0.5 collective-permute-start.7
  24.9 8.6 %collective-permute-done.7.refs_0_ = bf16[128,512]{1,0:T(8,128)(2,1)S(1)} collective-permute-done((bf16[128,512]{1,0:T(8,128)(2,1)S(1)}, bf16[128,512]{1,0:T(8,128)(2,1)S(1)}, u32[]{:S(2)}, u32[]{:S(2)}) %collective-permute-start.7) | collective-permute-done | bytes 131104 | tf_op jit(solution)/shard_map/ppermute | solution.py:22
  33.5 0.5 collective-permute-start.6
  34.0 0.5 collective-permute-done.9.refs_2_
  34.5 1.5 %collective-permute-start.11 = (bf16[128,512]{1,0:T(8,128)(2,1)S(1)}, bf16[128,512]{1,0:T(8,128)(2,1)S(1)}, u32[]{:S(2)}, u32[]{:S(2)}) collective-permute-start(bf16[128,512]{1,0:T(8,128)(2,1)S(1)} %collective-permute-done.9.refs_2_), channel_id=1, source_target_pairs={{0,2},{2,0},{4,6},{6,4},{8,10},{10,8},{12,14},{14,12},{16,18},{18,... | collective-permute-start | bytes 393224 | tf_op jit(solution)/shard_map/ppermute | solution.py:22
  36.0 3.5 %collective-permute-done.11.refs_4_ = bf16[128,512]{1,0:T(8,128)(2,1)S(1)} collective-permute-done((bf16[128,512]{1,0:T(8,128)(2,1)S(1)}, bf16[128,512]{1,0:T(8,128)(2,1)S(1)}, u32[]{:S(2)}, u32[]{:S(2)}) %collective-permute-start.11) | collective-permute-done | bytes 131104 | tf_op jit(solution)/shard_map/ppermute | solution.py:22
  39.6 0.5 collective-permute-start.8
  40.1 0.9 %copy-done.3 = bf16[256,512]{1,0:T(8,128)(2,1)S(1)} copy-done((bf16[256,512]{1,0:T(8,128)(2,1)S(1)}, bf16[256,512]{1,0:T(8,128)(2,1)}, u32[]{:S(2)}) %copy-start.3) | copy-done | bytes 262168
  41.1 0.9 %copy-done.5 = bf16[256,256]{1,0:T(8,128)(2,1)S(1)} copy-done((bf16[256,256]{1,0:T(8,128)(2,1)S(1)}, bf16[256,256]{1,0:T(8,128)(2,1)}, u32[]{:S(2)}) %copy-start.5) | copy-done | bytes 131096
  42.0 0.9 %copy-done.7 = bf16[256,256]{1,0:T(8,128)(2,1)S(1)} copy-done((bf16[256,256]{1,0:T(8,128)(2,1)S(1)}, bf16[256,256]{1,0:T(8,128)(2,1)}, u32[]{:S(2)}) %copy-start.7) | copy-done | bytes 131096
  42.9 1.0 %copy-done.8 = bf16[512,512]{1,0:T(8,128)(2,1)S(1)} copy-done((bf16[512,512]{1,0:T(8,128)(2,1)S(1)}, bf16[512,512]{1,0:T(8,128)(2,1)}, u32[]{:S(2)}) %copy-start.8) | copy-done | bytes 524312
  44.0 0.7 %copy-done.10 = s32[1,256]{1,0:T(1,128)S(1)} copy-done((s32[1,256]{1,0:T(1,128)S(1)}, s32[1,256]{1,0:T(1,128)}, u32[]{:S(2)}) %copy-start.10) | copy-done | bytes 1048
  44.6 2.4 %own_part.1 = (bf16[3,256,512]{2,1,0:T(8,128)(2,1)S(1)}, bf16[3,256,256]{2,1,0:T(8,128)(2,1)S(1)}, bf16[2,256,256]{2,1,0:T(8,128)(2,1)S(1)}, bf16[2,256,256]{2,1...) custom-call(s32[4]{0:T(128)S(1)} %pad_add_fusion.sc, ...), custom_call_target="tpu_custom_call" | custom-call | tf_op jit(solution)/shard_map/own_part/pallas_call | solution.py:160
  47.0 2.3 %rest_part.1 = (bf16[256,512]{1,0:T(8,128)(2,1)S(1)}, bf16[256,256]{1,0:T(8,128)(2,1)S(1)}, bf16[2,256,256]{2,1,0:T(8,128)(2,1)S(1)}, bf16[2,256,256]{2,1,0:T(8,...) custom-call(s32[4]{0:T(128)S(1)} %pad_add_fusion.sc, ...), custom_call_target="tpu_custom_call" | custom-call | tf_op jit(solution)/shard_map/rest_part/pallas_call | solution.py:222
  49.4 3.2 %later_layers.1 = (bf16[256,512]{1,0:T(8,128)(2,1)}, bf16[1,4,256,512]{3,2,1,0:T(8,128)(2,1)S(1)}, f32[1,4,256,512]{3,2,1,0:T(8,128)S(1)}) custom-call(s32[4]{0:T(128)S(1)} %pad_add_fusion.sc, bf16[3,256,512]{2,1,0:T(8,128)(2,1)S(1)} %get-tuple-element.33.refs_2_.x_r, bf16[3,256,256]{2,1,0:T(8,128)(2,1)S(1)} %get-tuple-element.34.own_r.refs_6_, ...), custom_call_target="tpu_custom_call" | custom-call | tf_op jit(solution)/shard_map/later_layers/pallas_call | solution.py:285
  52.6 3.1 %backward.1 = (bf16[1024,512]{1,0:T(8,128)(2,1)S(1)}, f32[256,512]{1,0:T(8,128)S(1)}, f32[32,512]{1,0:T(8,128)S(1)}, bf16[32,512]{1,0:T(8,128)(2,1)S(1)}, bf16[3...) custom-call(s32[4]{0:T(128)S(1)} %pad_add_fusion.sc, bf16[256,512]{1,0:T(8,128)(2,1)S(1)} %copy-done.1, ...), custom_call_target="tpu_custom_call" | custom-call | tf_op jit(solution)/shard_map/backward/pallas_call | solution.py:371
  55.7 1.6 %collective-permute-start.15 = (bf16[32,512]{1,0:T(8,128)(2,1)S(1)}, bf16[32,512]{1,0:T(8,128)(2,1)S(1)}, u32[]{:S(2)}, u32[]{:S(2)}) collective-permute-start(bf16[32,512]{1,0:T(8,128)(2,1)S(1)} %get-tuple-element.58), channel_id=1, source_target_pairs={{0,4},{2,6},{4,0},{6,2},{8,12},{10,14},{12,8},{14,10},{16,20},{18,... | collective-permute-start | bytes 98312 | tf_op jit(solution)/shard_map/ppermute | solution.py:22
  57.3 1.4 %collective-permute-start.14 = (bf16[32,512]{1,0:T(8,128)(2,1)S(1)}, bf16[32,512]{1,0:T(8,128)(2,1)S(1)}, u32[]{:S(2)}, u32[]{:S(2)}) collective-permute-start(bf16[32,512]{1,0:T(8,128)(2,1)S(1)} %get-tuple-element.57), channel_id=1, source_target_pairs={{0,8},{2,10},{4,12},{6,14},{8,0},{10,2},{12,4},{14,6},{16,24},{18,... | collective-permute-start | bytes 98312 | tf_op jit(solution)/shard_map/ppermute | solution.py:22
  58.7 0.6 collective-permute-start.13
  59.2 1.9 %feat.1 = f32[256,256]{1,0:T(8,128)} custom-call(s32[4]{0:T(128)S(1)} %pad_add_fusion.sc, bf16[1024,512]{1,0:T(8,128)(2,1)S(1)} %get-tuple-element.59.dpre_r, f32[256,512]{1,0:T(8,128)S(1)} %get-tuple-element.60.carry_r, bf16[3,256,256]{2,1,0:T(8,128)(2,1)S(1)} %get-tuple-element.34.own_r.refs_6_, bf16[2,256,256]{2,1,0:T(8,128)(2,1)S(1)} %get-tuple-element.35.near_r.refs_7_, ...), custom_call_target="tpu_custom_call" | custom-call | tf_op jit(solution)/shard_map/feat/pallas_call | solution.py:426
  61.4 2.1 %collective-permute-done.13 = bf16[32,512]{1,0:T(8,128)(2,1)S(1)} collective-permute-done((bf16[32,512]{1,0:T(8,128)(2,1)S(1)}, bf16[32,512]{1,0:T(8,128)(2,1)S(1)}, u32[]{:S(2)}, u32[]{:S(2)}) %collective-permute-start.13) | collective-permute-done | bytes 32800 | tf_op jit(solution)/shard_map/ppermute | solution.py:22
  63.5 0.6 %add_bitcast_fusion = f32[1,32,512]{2,1,0:T(8,128)} fusion(bf16[32,512]{1,0:T(8,128)(2,1)S(1)} %collective-permute-done.15, bf16[32,512]{1,0:T(8,128)(2,1)S(1)} %collective-permute-done.14, f32[32,512]{1,0:T(8,128)S(1)} %get-tuple-element.55, bf16[32,512]{1,0:T(8,128)(2,1)S(1)} %collective-permute-done.13), kind=kLoop, calls=%fused_computation | loop fusion | flops 98304 | bytes 229376 | tf_op jit(solution)/shard_map/broadcast_in_dim | solution.py:470
  (30 shorter events, 0.4 us)
Async XLA Ops:
  0.7 1.0 %copy-start = (bf16[256,512]{1,0:T(8,128)(2,1)S(1)}, bf16[256,512]{1,0:T(8,128)(2,1)}, u32[]{:S(2)}) copy-start(bf16[256,512]{1,0:T(8,128)(2,1)} %cot_r.3) | copy-start | bytes 786436
  1.7 0.9 %copy-start.2 = (bf16[256,512]{1,0:T(8,128)(2,1)S(1)}, bf16[256,512]{1,0:T(8,128)(2,1)}, u32[]{:S(2)}) copy-start(bf16[256,512]{1,0:T(8,128)(2,1)} %feats_r.3) | copy-start | bytes 786436
  2.6 0.9 %copy-start.4 = (bf16[256,256]{1,0:T(8,128)(2,1)S(1)}, bf16[256,256]{1,0:T(8,128)(2,1)}, u32[]{:S(2)}) copy-start(bf16[256,256]{1,0:T(8,128)(2,1)} %adj_r.3) | copy-start | bytes 393220
  3.6 0.9 %copy-start.6 = (bf16[256,256]{1,0:T(8,128)(2,1)S(1)}, bf16[256,256]{1,0:T(8,128)(2,1)}, u32[]{:S(2)}) copy-start(bf16[256,256]{1,0:T(8,128)(2,1)} %couple_r.3) | copy-start | bytes 393220
  4.5 0.7 %copy-start.9 = (s32[1,256]{1,0:T(1,128)S(1)}, s32[1,256]{1,0:T(1,128)}, u32[]{:S(2)}) copy-start(s32[1,256]{1,0:T(1,128)} %sr_r.3) | copy-start | bytes 3076
  6.1 16.8 %collective-permute-start.2 = (bf16[272,512]{1,0:T(8,128)(2,1)S(1)}, bf16[272,512]{1,0:T(8,128)(2,1)S(1)}, u32[]{:S(2)}, u32[]{:S(2)}) collective-permute-start(bf16[272,512]{1,0:T(8,128)(2,1)S(1)} %get-tuple-element.32), channel_id=1, source_target_pairs={{0,16},{2,18},{4,20},{6,22},{8,24},{10,26},{12,28},{14,30},{16,0},... | collective-permute-start | bytes 835592 | tf_op jit(solution)/shard_map/ppermute | solution.py:22
  10.2 14.7 %collective-permute-start = (bf16[272,512]{1,0:T(8,128)(2,1)S(1)}, bf16[272,512]{1,0:T(8,128)(2,1)S(1)}, u32[]{:S(2)}, u32[]{:S(2)}) collective-permute-start(bf16[272,512]{1,0:T(8,128)(2,1)S(1)} %get-tuple-element.32), channel_id=1, source_target_pairs={{0,2},{2,0},{4,6},{6,4},{8,10},{10,8},{12,14},{14,12},{16,18},{18,... | collective-permute-start | bytes 835592 | tf_op jit(solution)/shard_map/ppermute | solution.py:22
  11.7 27.8 %collective-permute-start.4 = (bf16[512,512]{1,0:T(8,128)(2,1)}, bf16[512,512]{1,0:T(8,128)(2,1)S(1)}, u32[]{:S(2)}, u32[]{:S(2)}) collective-permute-start(bf16[512,512]{1,0:T(8,128)(2,1)} %refs_4_.1), channel_id=1, source_target_pairs={{0,1},{1,0},{2,3},{3,2},{4,5},{5,4},{6,7},{7,6},{8,9},{9,8},{10,11... | collective-permute-start | bytes 1572872 | tf_op jit(solution)/shard_map/ppermute | solution.py:27
  22.9 10.6 %collective-permute-start.5 = (bf16[272,512]{1,0:T(8,128)(2,1)S(1)}, bf16[272,512]{1,0:T(8,128)(2,1)S(1)}, u32[]{:S(2)}, u32[]{:S(2)}) collective-permute-start(bf16[272,512]{1,0:T(8,128)(2,1)S(1)} %collective-permute-done.2.refs_2_), channel_id=1, source_target_pairs={{0,2},{2,0},{4,6},{6,4},{8,10},{10,8},{12,14},{14,12},{16,18},{18,... | collective-permute-start | bytes 835592 | tf_op jit(solution)/shard_map/ppermute | solution.py:22
  24.4 9.1 %collective-permute-start.7 = (bf16[128,512]{1,0:T(8,128)(2,1)S(1)}, bf16[128,512]{1,0:T(8,128)(2,1)S(1)}, u32[]{:S(2)}, u32[]{:S(2)}) collective-permute-start(bf16[128,512]{1,0:T(8,128)(2,1)S(1)} %get-tuple-element.48), channel_id=1, source_target_pairs={{0,2},{2,0},{4,6},{6,4},{8,10},{10,8},{12,14},{14,12},{16,18},{18,... | collective-permute-start | bytes 393224 | tf_op jit(solution)/shard_map/ppermute | solution.py:22
  24.9 15.2 %collective-permute-start.1 = (bf16[272,512]{1,0:T(8,128)(2,1)S(1)}, bf16[272,512]{1,0:T(8,128)(2,1)S(1)}, u32[]{:S(2)}, u32[]{:S(2)}) collective-permute-start(bf16[272,512]{1,0:T(8,128)(2,1)S(1)} %collective-permute-done.refs_0_), channel_id=1, source_target_pairs={{0,1},{1,0},{2,3},{3,2},{4,5},{5,4},{6,7},{7,6},{8,9},{9,8},{10,11... | collective-permute-start | bytes 835592 | tf_op jit(solution)/shard_map/ppermute | solution.py:27
  24.9 9.6 %collective-permute-start.9 = (bf16[128,512]{1,0:T(8,128)(2,1)S(1)}, bf16[128,512]{1,0:T(8,128)(2,1)S(1)}, u32[]{:S(2)}, u32[]{:S(2)}) collective-permute-start(bf16[128,512]{1,0:T(8,128)(2,1)S(1)} %get-tuple-element.48), channel_id=1, source_target_pairs={{0,16},{2,18},{4,20},{6,22},{8,24},{10,26},{12,28},{14,30},{16,0},... | collective-permute-start | bytes 393224 | tf_op jit(solution)/shard_map/ppermute | solution.py:22
  33.5 6.7 %collective-permute-start.3 = (bf16[272,512]{1,0:T(8,128)(2,1)S(1)}, bf16[272,512]{1,0:T(8,128)(2,1)S(1)}, u32[]{:S(2)}, u32[]{:S(2)}) collective-permute-start(bf16[272,512]{1,0:T(8,128)(2,1)S(1)} %collective-permute-done.2.refs_2_), channel_id=1, source_target_pairs={{0,1},{1,0},{2,3},{3,2},{4,5},{5,4},{6,7},{7,6},{8,9},{9,8},{10,11... | collective-permute-start | bytes 835592 | tf_op jit(solution)/shard_map/ppermute | solution.py:27
  33.5 13.6 %collective-permute-start.6 = (bf16[272,512]{1,0:T(8,128)(2,1)S(1)}, bf16[272,512]{1,0:T(8,128)(2,1)S(1)}, u32[]{:S(2)}, u32[]{:S(2)}) collective-permute-start(bf16[272,512]{1,0:T(8,128)(2,1)S(1)} %collective-permute-done.5.refs_0_), channel_id=1, source_target_pairs={{0,1},{1,0},{2,3},{3,2},{4,5},{5,4},{6,7},{7,6},{8,9},{9,8},{10,11... | collective-permute-start | bytes 835592 | tf_op jit(solution)/shard_map/ppermute | solution.py:27
  34.5 5.1 %collective-permute-start.11 = (bf16[128,512]{1,0:T(8,128)(2,1)S(1)}, bf16[128,512]{1,0:T(8,128)(2,1)S(1)}, u32[]{:S(2)}, u32[]{:S(2)}) collective-permute-start(bf16[128,512]{1,0:T(8,128)(2,1)S(1)} %collective-permute-done.9.refs_2_), channel_id=1, source_target_pairs={{0,2},{2,0},{4,6},{6,4},{8,10},{10,8},{12,14},{14,12},{16,18},{18,... | collective-permute-start | bytes 393224 | tf_op jit(solution)/shard_map/ppermute | solution.py:22
  39.6 13.0 %collective-permute-start.10 = (bf16[128,512]{1,0:T(8,128)(2,1)S(1)}, bf16[128,512]{1,0:T(8,128)(2,1)S(1)}, u32[]{:S(2)}, u32[]{:S(2)}) collective-permute-start(bf16[128,512]{1,0:T(8,128)(2,1)S(1)} %collective-permute-done.9.refs_2_), channel_id=1, source_target_pairs={{0,1},{1,0},{2,3},{3,2},{4,5},{5,4},{6,7},{7,6},{8,9},{9,8},{10,11... | collective-permute-start | bytes 393224 | tf_op jit(solution)/shard_map/ppermute | solution.py:27
  39.6 13.0 %collective-permute-start.8 = (bf16[128,512]{1,0:T(8,128)(2,1)S(1)}, bf16[128,512]{1,0:T(8,128)(2,1)S(1)}, u32[]{:S(2)}, u32[]{:S(2)}) collective-permute-start(bf16[128,512]{1,0:T(8,128)(2,1)S(1)} %collective-permute-done.7.refs_0_), channel_id=1, source_target_pairs={{0,1},{1,0},{2,3},{3,2},{4,5},{5,4},{6,7},{7,6},{8,9},{9,8},{10,11... | collective-permute-start | bytes 393224 | tf_op jit(solution)/shard_map/ppermute | solution.py:27
  40.1 12.5 %collective-permute-start.12 = (bf16[128,512]{1,0:T(8,128)(2,1)S(1)}, bf16[128,512]{1,0:T(8,128)(2,1)S(1)}, u32[]{:S(2)}, u32[]{:S(2)}) collective-permute-start(bf16[128,512]{1,0:T(8,128)(2,1)S(1)} %collective-permute-done.11.refs_4_), channel_id=1, source_target_pairs={{0,1},{1,0},{2,3},{3,2},{4,5},{5,4},{6,7},{7,6},{8,9},{9,8},{10,11... | collective-permute-start | bytes 393224 | tf_op jit(solution)/shard_map/ppermute | solution.py:27
  40.1 1.0 %copy-start.3 = (bf16[256,512]{1,0:T(8,128)(2,1)S(1)}, bf16[256,512]{1,0:T(8,128)(2,1)}, u32[]{:S(2)}) copy-start(bf16[256,512]{1,0:T(8,128)(2,1)} %feats_r.3) | copy-start | bytes 786436
  41.1 0.9 %copy-start.5 = (bf16[256,256]{1,0:T(8,128)(2,1)S(1)}, bf16[256,256]{1,0:T(8,128)(2,1)}, u32[]{:S(2)}) copy-start(bf16[256,256]{1,0:T(8,128)(2,1)} %adj_r.3) | copy-start | bytes 393220
  42.0 0.9 %copy-start.7 = (bf16[256,256]{1,0:T(8,128)(2,1)S(1)}, bf16[256,256]{1,0:T(8,128)(2,1)}, u32[]{:S(2)}) copy-start(bf16[256,256]{1,0:T(8,128)(2,1)} %couple_r.3) | copy-start | bytes 393220
  42.9 1.0 %copy-start.8 = (bf16[512,512]{1,0:T(8,128)(2,1)S(1)}, bf16[512,512]{1,0:T(8,128)(2,1)}, u32[]{:S(2)}) copy-start(bf16[512,512]{1,0:T(8,128)(2,1)} %refs_4_.1) | copy-start | bytes 1572868
  43.9 0.7 %copy-start.10 = (s32[1,256]{1,0:T(1,128)S(1)}, s32[1,256]{1,0:T(1,128)}, u32[]{:S(2)}) copy-start(s32[1,256]{1,0:T(1,128)} %sr_r.3) | copy-start | bytes 3076
  49.3 3.2 %copy-start.1 = (bf16[256,512]{1,0:T(8,128)(2,1)S(1)}, bf16[256,512]{1,0:T(8,128)(2,1)}, u32[]{:S(2)}) copy-start(bf16[256,512]{1,0:T(8,128)(2,1)} %cot_r.3) | copy-start | bytes 786436
  55.7 5.5 %collective-permute-start.15 = (bf16[32,512]{1,0:T(8,128)(2,1)S(1)}, bf16[32,512]{1,0:T(8,128)(2,1)S(1)}, u32[]{:S(2)}, u32[]{:S(2)}) collective-permute-start(bf16[32,512]{1,0:T(8,128)(2,1)S(1)} %get-tuple-element.58), channel_id=1, source_target_pairs={{0,4},{2,6},{4,0},{6,2},{8,12},{10,14},{12,8},{14,10},{16,20},{18,... | collective-permute-start | bytes 98312 | tf_op jit(solution)/shard_map/ppermute | solution.py:22
  57.3 4.1 %collective-permute-start.14 = (bf16[32,512]{1,0:T(8,128)(2,1)S(1)}, bf16[32,512]{1,0:T(8,128)(2,1)S(1)}, u32[]{:S(2)}, u32[]{:S(2)}) collective-permute-start(bf16[32,512]{1,0:T(8,128)(2,1)S(1)} %get-tuple-element.57), channel_id=1, source_target_pairs={{0,8},{2,10},{4,12},{6,14},{8,0},{10,2},{12,4},{14,6},{16,24},{18,... | collective-permute-start | bytes 98312 | tf_op jit(solution)/shard_map/ppermute | solution.py:22
  58.7 4.8 %collective-permute-start.13 = (bf16[32,512]{1,0:T(8,128)(2,1)S(1)}, bf16[32,512]{1,0:T(8,128)(2,1)S(1)}, u32[]{:S(2)}, u32[]{:S(2)}) collective-permute-start(bf16[32,512]{1,0:T(8,128)(2,1)S(1)} %get-tuple-element.56), channel_id=1, source_target_pairs={{0,12},{2,14},{4,8},{6,10},{8,4},{10,6},{12,0},{14,2},{16,28},{18,... | collective-permute-start | bytes 98312 | tf_op jit(solution)/shard_map/ppermute | solution.py:22

commit v5 on v4

--- a/solution.py
+++ b/solution.py
@@ -45,6 +45,10 @@
 
 def place_of(seg, k, n):
     return lax.rem(seg - k + n, n)
+
+
+def in_hbm(x):
+    return pltpu.with_memory_space_constraint(x, pltpu.HBM)
 
 
 def pack_call(scalars, feats, adj, couple, send_rows, cot, layers):
@@ -84,7 +88,7 @@
         scratch_shapes=[pltpu.VMEM(send_rows.shape, jnp.int32), pltpu.SemaphoreType.DMA((5,))],
         compiler_params=pltpu.CompilerParams(vmem_limit_bytes=4 << 20),
         name="pack",
-    )(scalars, feats, adj, couple, send_rows, cot)
+    )(scalars, *[in_hbm(a) for a in (feats, adj, couple, send_rows, cot)])
 
 
 def picks_of(sr, rows):
@@ -182,7 +186,14 @@
         ],
         compiler_params=pltpu.CompilerParams(vmem_limit_bytes=vmem_of(layers)),
         name="own_part",
-    )(scalars, feats, adj, couple, send_rows, *near, *far, *w_pieces)
+    )(
+        scalars,
+        *[in_hbm(a) for a in (feats, adj, couple, send_rows)],
+        *near,
+        *far,
+        in_hbm(w_pieces[0]),
+        *w_pieces[1:],
+    )
 
 
 def rest_part_call(scalars, diag, part):

time: 64.5 us -> 56.8 us (0.88)
  local copies, waits for them, and re-layouts: 8.87 us -> 0.01 us
  Pallas kernels: 13.9 us -> 15.3 us
    unnamed x22 -> x2, local copies, waits for them, and re-layouts: 8.87 us -> 0.01 us
    pallas_call x1, Pallas kernels: 2.4 us -> 3.09 us  [own_part_call(): pl.pallas_call(body, out_shape=(sds((3, rows, width), BF16), sds((3, rows...]
    pallas_call x1, Pallas kernels: 0.95 us -> 1.63 us  [pack_call(): pl.pallas_call(body, out_shape=(jax.ShapeDtypeStruct((2 * piece + 16, wid...]
  transfers between devices with their start and end apart: 16 -> 16, of which waited for: 6 -> 6; matrix products, arithmetic and copies ran while one was open for 0% -> 0% of each run, Pallas kernels for 15% -> 19%
where the time goes in v5:
time: 56.8 us; the launch traced here: 56.6 us
  waiting for transfers between devices  26.1 us (46%)
  Pallas kernels  15.3 us (27%)
  starting transfers between devices  13.8 us (24%)
  between operations  0.75 us (1%)
  other arithmetic  0.72 us (1%)
    ppermute x9, waiting for transfers between devices, swapped(): lax.ppermute(x, 'dom', [(i, i ^ mask) for i in range(lax.axis_size('dom'))])  26 us
    ppermute x9, starting transfers between devices, swapped(): lax.ppermute(x, 'dom', [(i, i ^ mask) for i in range(lax.axis_size('dom'))])  12.7 us
    pallas_call x1, Pallas kernels, later_layers_call(): pl.pallas_call(body, out_shape=(jax.ShapeDtypeStruct((rows, width), BF16)...  3.22 us
    pallas_call x1, Pallas kernels, own_part_call(): pl.pallas_call(body, out_shape=(sds((3, rows, width), BF16), sds((3, rows...  3.09 us
    pallas_call x1, Pallas kernels, backward_call(): pl.pallas_call(body, out_shape=(sds((4 * rows, width), BF16), sds((rows,...  3.09 us
    pallas_call x1, Pallas kernels, rest_part_call(): pl.pallas_call(body, out_shape=(sds((rows, width), BF16), sds((rows, rows...  2.3 us
    pallas_call x1, Pallas kernels, feat_call(): pl.pallas_call(body, out_shape=jax.ShapeDtypeStruct((rows, kept), F32), i...  1.93 us
    pallas_call x1, Pallas kernels, pack_call(): pl.pallas_call(body, out_shape=(jax.ShapeDtypeStruct((2 * piece + 16, wid...  1.63 us
  transfers between devices with their start and end apart: 16, of which 6 were waited for; matrix products, arithmetic and copies ran while one was open for 0% of the time, Pallas kernels for 19%

profile of v5, /device:TPU:0, one launch (start us, length us, event | category | flops | bytes accessed | tf_op | source)
XLA Modules:
  0.0 56.6 jit_solution(16419936199410067096)
XLA Ops:
  0.7 0.1 pad_add_fusion.sc
  0.7 1.6 %pack.1 = (bf16[272,512]{1,0:T(8,128)(2,1)S(1)}, bf16[128,512]{1,0:T(8,128)(2,1)S(1)}) custom-call(s32[4]{0:T(128)S(1)} %pad_add_fusion.sc, bf16[256,512]{1,0:T(8,128)(2,1)} %feats_r.3, bf16[256,256]{1,0:T(8,128)(2,1)} %adj_r.3, bf16[256,256]{1,0:T(8,128)(2,1)} %couple_r.3, s32[1,256]{1,0:T(1,128)} %sr_r.3, bf16[256,512]{1,0:T(8,128)(2,1)} %cot_r.3), custom_call_target="tpu_custom_call" | custom-call | tf_op jit(solution)/shard_map/pack/pallas_call | solution.py:80
  2.4 4.1 %collective-permute-start.2 = (bf16[272,512]{1,0:T(8,128)(2,1)S(1)}, bf16[272,512]{1,0:T(8,128)(2,1)S(1)}, u32[]{:S(2)}, u32[]{:S(2)}) collective-permute-start(bf16[272,512]{1,0:T(8,128)(2,1)S(1)} %get-tuple-element.32), channel_id=1, source_target_pairs={{0,16},{2,18},{4,20},{6,22},{8,24},{10,26},{12,28},{14,30},{16,0},... | collective-permute-start | bytes 835592 | tf_op jit(solution)/shard_map/ppermute | solution.py:22
  6.5 1.5 %collective-permute-start = (bf16[272,512]{1,0:T(8,128)(2,1)S(1)}, bf16[272,512]{1,0:T(8,128)(2,1)S(1)}, u32[]{:S(2)}, u32[]{:S(2)}) collective-permute-start(bf16[272,512]{1,0:T(8,128)(2,1)S(1)} %get-tuple-element.32), channel_id=1, source_target_pairs={{0,2},{2,0},{4,6},{6,4},{8,10},{10,8},{12,14},{14,12},{16,18},{18,... | collective-permute-start | bytes 835592 | tf_op jit(solution)/shard_map/ppermute | solution.py:22
  8.0 11.1 %collective-permute-done.2.refs_2_ = bf16[272,512]{1,0:T(8,128)(2,1)S(1)} collective-permute-done((bf16[272,512]{1,0:T(8,128)(2,1)S(1)}, bf16[272,512]{1,0:T(8,128)(2,1)S(1)}, u32[]{:S(2)}, u32[]{:S(2)}) %collective-permute-start.2) | collective-permute-done | bytes 278560 | tf_op jit(solution)/shard_map/ppermute | solution.py:22
  19.1 1.5 %collective-permute-start.5 = (bf16[272,512]{1,0:T(8,128)(2,1)S(1)}, bf16[272,512]{1,0:T(8,128)(2,1)S(1)}, u32[]{:S(2)}, u32[]{:S(2)}) collective-permute-start(bf16[272,512]{1,0:T(8,128)(2,1)S(1)} %collective-permute-done.2.refs_2_), channel_id=1, source_target_pairs={{0,2},{2,0},{4,6},{6,4},{8,10},{10,8},{12,14},{14,12},{16,18},{18,... | collective-permute-start | bytes 835592 | tf_op jit(solution)/shard_map/ppermute | solution.py:22
  20.7 0.5 collective-permute-start.7
  21.2 0.0 collective-permute-done.refs_0_
  21.2 0.0 collective-permute-start.1
  21.2 0.0 collective-permute-start.9
  21.2 8.6 %collective-permute-done.7.refs_0_ = bf16[128,512]{1,0:T(8,128)(2,1)S(1)} collective-permute-done((bf16[128,512]{1,0:T(8,128)(2,1)S(1)}, bf16[128,512]{1,0:T(8,128)(2,1)S(1)}, u32[]{:S(2)}, u32[]{:S(2)}) %collective-permute-start.7) | collective-permute-done | bytes 131104 | tf_op jit(solution)/shard_map/ppermute | solution.py:22
  29.8 0.5 collective-permute-start.6
  30.3 0.5 collective-permute-done.9.refs_2_
  30.8 1.5 %collective-permute-start.11 = (bf16[128,512]{1,0:T(8,128)(2,1)S(1)}, bf16[128,512]{1,0:T(8,128)(2,1)S(1)}, u32[]{:S(2)}, u32[]{:S(2)}) collective-permute-start(bf16[128,512]{1,0:T(8,128)(2,1)S(1)} %collective-permute-done.9.refs_2_), channel_id=1, source_target_pairs={{0,2},{2,0},{4,6},{6,4},{8,10},{10,8},{12,14},{14,12},{16,18},{18,... | collective-permute-start | bytes 393224 | tf_op jit(solution)/shard_map/ppermute | solution.py:22
  32.3 3.5 %collective-permute-done.11.refs_4_ = bf16[128,512]{1,0:T(8,128)(2,1)S(1)} collective-permute-done((bf16[128,512]{1,0:T(8,128)(2,1)S(1)}, bf16[128,512]{1,0:T(8,128)(2,1)S(1)}, u32[]{:S(2)}, u32[]{:S(2)}) %collective-permute-start.11) | collective-permute-done | bytes 131104 | tf_op jit(solution)/shard_map/ppermute | solution.py:22
  35.8 0.0 collective-permute-start.10
  35.8 0.0 collective-permute-done.4.refs_5_
  35.8 0.5 collective-permute-start.8
  36.4 0.0 collective-permute-done.1.refs_1_
  36.4 0.1 collective-permute-start.12
  36.4 3.1 %own_part.1 = (bf16[3,256,512]{2,1,0:T(8,128)(2,1)S(1)}, bf16[3,256,256]{2,1,0:T(8,128)(2,1)S(1)}, bf16[2,256,256]{2,1,0:T(8,128)(2,1)S(1)}, bf16[2,256,256]{2,1...) custom-call(s32[4]{0:T(128)S(1)} %pad_add_fusion.sc, ...), custom_call_target="tpu_custom_call" | custom-call | tf_op jit(solution)/shard_map/own_part/pallas_call | solution.py:164
  39.5 2.3 %rest_part.1 = (bf16[256,512]{1,0:T(8,128)(2,1)S(1)}, bf16[256,256]{1,0:T(8,128)(2,1)S(1)}, bf16[2,256,256]{2,1,0:T(8,128)(2,1)S(1)}, bf16[2,256,256]{2,1,0:T(8,...) custom-call(s32[4]{0:T(128)S(1)} %pad_add_fusion.sc, ...), custom_call_target="tpu_custom_call" | custom-call | tf_op jit(solution)/shard_map/rest_part/pallas_call | solution.py:233
  41.9 0.0 copy-start
  41.9 3.2 %later_layers.1 = (bf16[256,512]{1,0:T(8,128)(2,1)}, bf16[1,4,256,512]{3,2,1,0:T(8,128)(2,1)S(1)}, f32[1,4,256,512]{3,2,1,0:T(8,128)S(1)}) custom-call(s32[4]{0:T(128)S(1)} %pad_add_fusion.sc, bf16[3,256,512]{2,1,0:T(8,128)(2,1)S(1)} %get-tuple-element.33.refs_2_.x_r, bf16[3,256,256]{2,1,0:T(8,128)(2,1)S(1)} %get-tuple-element.34.own_r.refs_6_, ...), custom_call_target="tpu_custom_call" | custom-call | tf_op jit(solution)/shard_map/later_layers/pallas_call | solution.py:296
  45.1 3.1 %backward.1 = (bf16[1024,512]{1,0:T(8,128)(2,1)S(1)}, f32[256,512]{1,0:T(8,128)S(1)}, f32[32,512]{1,0:T(8,128)S(1)}, bf16[32,512]{1,0:T(8,128)(2,1)S(1)}, bf16[3...) custom-call(s32[4]{0:T(128)S(1)} %pad_add_fusion.sc, bf16[256,512]{1,0:T(8,128)(2,1)S(1)} %copy-done, ...), custom_call_target="tpu_custom_call" | custom-call | tf_op jit(solution)/shard_map/backward/pallas_call | solution.py:382
  48.2 1.6 %collective-permute-start.15 = (bf16[32,512]{1,0:T(8,128)(2,1)S(1)}, bf16[32,512]{1,0:T(8,128)(2,1)S(1)}, u32[]{:S(2)}, u32[]{:S(2)}) collective-permute-start(bf16[32,512]{1,0:T(8,128)(2,1)S(1)} %get-tuple-element.58), channel_id=1, source_target_pairs={{0,4},{2,6},{4,0},{6,2},{8,12},{10,14},{12,8},{14,10},{16,20},{18,... | collective-permute-start | bytes 98312 | tf_op jit(solution)/shard_map/ppermute | solution.py:22
  49.8 1.4 %collective-permute-start.14 = (bf16[32,512]{1,0:T(8,128)(2,1)S(1)}, bf16[32,512]{1,0:T(8,128)(2,1)S(1)}, u32[]{:S(2)}, u32[]{:S(2)}) collective-permute-start(bf16[32,512]{1,0:T(8,128)(2,1)S(1)} %get-tuple-element.57), channel_id=1, source_target_pairs={{0,8},{2,10},{4,12},{6,14},{8,0},{10,2},{12,4},{14,6},{16,24},{18,... | collective-permute-start | bytes 98312 | tf_op jit(solution)/shard_map/ppermute | solution.py:22
  51.2 0.6 %collective-permute-start.13 = (bf16[32,512]{1,0:T(8,128)(2,1)S(1)}, bf16[32,512]{1,0:T(8,128)(2,1)S(1)}, u32[]{:S(2)}, u32[]{:S(2)}) collective-permute-start(bf16[32,512]{1,0:T(8,128)(2,1)S(1)} %get-tuple-element.56), channel_id=1, source_target_pairs={{0,12},{2,14},{4,8},{6,10},{8,4},{10,6},{12,0},{14,2},{16,28},{18,... | collective-permute-start | bytes 98312 | tf_op jit(solution)/shard_map/ppermute | solution.py:22
  51.8 1.9 %feat.1 = f32[256,256]{1,0:T(8,128)} custom-call(s32[4]{0:T(128)S(1)} %pad_add_fusion.sc, bf16[1024,512]{1,0:T(8,128)(2,1)S(1)} %get-tuple-element.59.dpre_r, f32[256,512]{1,0:T(8,128)S(1)} %get-tuple-element.60.carry_r, bf16[3,256,256]{2,1,0:T(8,128)(2,1)S(1)} %get-tuple-element.34.own_r.refs_6_, bf16[2,256,256]{2,1,0:T(8,128)(2,1)S(1)} %get-tuple-element.35.near_r.refs_7_, ...), custom_call_target="tpu_custom_call" | custom-call | tf_op jit(solution)/shard_map/feat/pallas_call | solution.py:437
  53.7 0.2 collective-permute-done.14
  53.9 2.1 %collective-permute-done.13 = bf16[32,512]{1,0:T(8,128)(2,1)S(1)} collective-permute-done((bf16[32,512]{1,0:T(8,128)(2,1)S(1)}, bf16[32,512]{1,0:T(8,128)(2,1)S(1)}, u32[]{:S(2)}, u32[]{:S(2)}) %collective-permute-start.13) | collective-permute-done | bytes 32800 | tf_op jit(solution)/shard_map/ppermute | solution.py:22
  56.0 0.6 %add_bitcast_fusion = f32[1,32,512]{2,1,0:T(8,128)} fusion(bf16[32,512]{1,0:T(8,128)(2,1)S(1)} %collective-permute-done.15, bf16[32,512]{1,0:T(8,128)(2,1)S(1)} %collective-permute-done.14, f32[32,512]{1,0:T(8,128)S(1)} %get-tuple-element.55, bf16[32,512]{1,0:T(8,128)(2,1)S(1)} %collective-permute-done.13), kind=kLoop, calls=%fused_computation | loop fusion | flops 98304 | bytes 229376 | tf_op jit(solution)/shard_map/broadcast_in_dim | solution.py:481
  (10 shorter events, 0.0 us)
Async XLA Ops:
  2.4 16.8 %collective-permute-start.2 = (bf16[272,512]{1,0:T(8,128)(2,1)S(1)}, bf16[272,512]{1,0:T(8,128)(2,1)S(1)}, u32[]{:S(2)}, u32[]{:S(2)}) collective-permute-start(bf16[272,512]{1,0:T(8,128)(2,1)S(1)} %get-tuple-element.32), channel_id=1, source_target_pairs={{0,16},{2,18},{4,20},{6,22},{8,24},{10,26},{12,28},{14,30},{16,0},... | collective-permute-start | bytes 835592 | tf_op jit(solution)/shard_map/ppermute | solution.py:22
  6.5 14.7 %collective-permute-start = (bf16[272,512]{1,0:T(8,128)(2,1)S(1)}, bf16[272,512]{1,0:T(8,128)(2,1)S(1)}, u32[]{:S(2)}, u32[]{:S(2)}) collective-permute-start(bf16[272,512]{1,0:T(8,128)(2,1)S(1)} %get-tuple-element.32), channel_id=1, source_target_pairs={{0,2},{2,0},{4,6},{6,4},{8,10},{10,8},{12,14},{14,12},{16,18},{18,... | collective-permute-start | bytes 835592 | tf_op jit(solution)/shard_map/ppermute | solution.py:22
  8.0 27.8 %collective-permute-start.4 = (bf16[512,512]{1,0:T(8,128)(2,1)}, bf16[512,512]{1,0:T(8,128)(2,1)S(1)}, u32[]{:S(2)}, u32[]{:S(2)}) collective-permute-start(bf16[512,512]{1,0:T(8,128)(2,1)} %refs_4_.1), channel_id=1, source_target_pairs={{0,1},{1,0},{2,3},{3,2},{4,5},{5,4},{6,7},{7,6},{8,9},{9,8},{10,11... | collective-permute-start | bytes 1572872 | tf_op jit(solution)/shard_map/ppermute | solution.py:27
  19.1 10.6 %collective-permute-start.5 = (bf16[272,512]{1,0:T(8,128)(2,1)S(1)}, bf16[272,512]{1,0:T(8,128)(2,1)S(1)}, u32[]{:S(2)}, u32[]{:S(2)}) collective-permute-start(bf16[272,512]{1,0:T(8,128)(2,1)S(1)} %collective-permute-done.2.refs_2_), channel_id=1, source_target_pairs={{0,2},{2,0},{4,6},{6,4},{8,10},{10,8},{12,14},{14,12},{16,18},{18,... | collective-permute-start | bytes 835592 | tf_op jit(solution)/shard_map/ppermute | solution.py:22
  20.7 9.1 %collective-permute-start.7 = (bf16[128,512]{1,0:T(8,128)(2,1)S(1)}, bf16[128,512]{1,0:T(8,128)(2,1)S(1)}, u32[]{:S(2)}, u32[]{:S(2)}) collective-permute-start(bf16[128,512]{1,0:T(8,128)(2,1)S(1)} %get-tuple-element.48), channel_id=1, source_target_pairs={{0,2},{2,0},{4,6},{6,4},{8,10},{10,8},{12,14},{14,12},{16,18},{18,... | collective-permute-start | bytes 393224 | tf_op jit(solution)/shard_map/ppermute | solution.py:22
  21.2 15.2 %collective-permute-start.1 = (bf16[272,512]{1,0:T(8,128)(2,1)S(1)}, bf16[272,512]{1,0:T(8,128)(2,1)S(1)}, u32[]{:S(2)}, u32[]{:S(2)}) collective-permute-start(bf16[272,512]{1,0:T(8,128)(2,1)S(1)} %collective-permute-done.refs_0_), channel_id=1, source_target_pairs={{0,1},{1,0},{2,3},{3,2},{4,5},{5,4},{6,7},{7,6},{8,9},{9,8},{10,11... | collective-permute-start | bytes 835592 | tf_op jit(solution)/shard_map/ppermute | solution.py:27
  21.2 9.6 %collective-permute-start.9 = (bf16[128,512]{1,0:T(8,128)(2,1)S(1)}, bf16[128,512]{1,0:T(8,128)(2,1)S(1)}, u32[]{:S(2)}, u32[]{:S(2)}) collective-permute-start(bf16[128,512]{1,0:T(8,128)(2,1)S(1)} %get-tuple-element.48), channel_id=1, source_target_pairs={{0,16},{2,18},{4,20},{6,22},{8,24},{10,26},{12,28},{14,30},{16,0},... | collective-permute-start | bytes 393224 | tf_op jit(solution)/shard_map/ppermute | solution.py:22
  29.8 6.7 %collective-permute-start.3 = (bf16[272,512]{1,0:T(8,128)(2,1)S(1)}, bf16[272,512]{1,0:T(8,128)(2,1)S(1)}, u32[]{:S(2)}, u32[]{:S(2)}) collective-permute-start(bf16[272,512]{1,0:T(8,128)(2,1)S(1)} %collective-permute-done.2.refs_2_), channel_id=1, source_target_pairs={{0,1},{1,0},{2,3},{3,2},{4,5},{5,4},{6,7},{7,6},{8,9},{9,8},{10,11... | collective-permute-start | bytes 835592 | tf_op jit(solution)/shard_map/ppermute | solution.py:27
  29.8 9.8 %collective-permute-start.6 = (bf16[272,512]{1,0:T(8,128)(2,1)S(1)}, bf16[272,512]{1,0:T(8,128)(2,1)S(1)}, u32[]{:S(2)}, u32[]{:S(2)}) collective-permute-start(bf16[272,512]{1,0:T(8,128)(2,1)S(1)} %collective-permute-done.5.refs_0_), channel_id=1, source_target_pairs={{0,1},{1,0},{2,3},{3,2},{4,5},{5,4},{6,7},{7,6},{8,9},{9,8},{10,11... | collective-permute-start | bytes 835592 | tf_op jit(solution)/shard_map/ppermute | solution.py:27
  30.8 5.1 %collective-permute-start.11 = (bf16[128,512]{1,0:T(8,128)(2,1)S(1)}, bf16[128,512]{1,0:T(8,128)(2,1)S(1)}, u32[]{:S(2)}, u32[]{:S(2)}) collective-permute-start(bf16[128,512]{1,0:T(8,128)(2,1)S(1)} %collective-permute-done.9.refs_2_), channel_id=1, source_target_pairs={{0,2},{2,0},{4,6},{6,4},{8,10},{10,8},{12,14},{14,12},{16,18},{18,... | collective-permute-start | bytes 393224 | tf_op jit(solution)/shard_map/ppermute | solution.py:22
  35.8 9.2 %collective-permute-start.10 = (bf16[128,512]{1,0:T(8,128)(2,1)S(1)}, bf16[128,512]{1,0:T(8,128)(2,1)S(1)}, u32[]{:S(2)}, u32[]{:S(2)}) collective-permute-start(bf16[128,512]{1,0:T(8,128)(2,1)S(1)} %collective-permute-done.9.refs_2_), channel_id=1, source_target_pairs={{0,1},{1,0},{2,3},{3,2},{4,5},{5,4},{6,7},{7,6},{8,9},{9,8},{10,11... | collective-permute-start | bytes 393224 | tf_op jit(solution)/shard_map/ppermute | solution.py:27
  35.8 9.2 %collective-permute-start.8 = (bf16[128,512]{1,0:T(8,128)(2,1)S(1)}, bf16[128,512]{1,0:T(8,128)(2,1)S(1)}, u32[]{:S(2)}, u32[]{:S(2)}) collective-permute-start(bf16[128,512]{1,0:T(8,128)(2,1)S(1)} %collective-permute-done.7.refs_0_), channel_id=1, source_target_pairs={{0,1},{1,0},{2,3},{3,2},{4,5},{5,4},{6,7},{7,6},{8,9},{9,8},{10,11... | collective-permute-start | bytes 393224 | tf_op jit(solution)/shard_map/ppermute | solution.py:27
  36.4 8.7 %collective-permute-start.12 = (bf16[128,512]{1,0:T(8,128)(2,1)S(1)}, bf16[128,512]{1,0:T(8,128)(2,1)S(1)}, u32[]{:S(2)}, u32[]{:S(2)}) collective-permute-start(bf16[128,512]{1,0:T(8,128)(2,1)S(1)} %collective-permute-done.11.refs_4_), channel_id=1, source_target_pairs={{0,1},{1,0},{2,3},{3,2},{4,5},{5,4},{6,7},{7,6},{8,9},{9,8},{10,11... | collective-permute-start | bytes 393224 | tf_op jit(solution)/shard_map/ppermute | solution.py:27
  41.9 3.2 %copy-start = (bf16[256,512]{1,0:T(8,128)(2,1)S(1)}, bf16[256,512]{1,0:T(8,128)(2,1)}, u32[]{:S(2)}) copy-start(bf16[256,512]{1,0:T(8,128)(2,1)} %cot_r.3) | copy-start | bytes 786436
  48.2 5.5 %collective-permute-start.15 = (bf16[32,512]{1,0:T(8,128)(2,1)S(1)}, bf16[32,512]{1,0:T(8,128)(2,1)S(1)}, u32[]{:S(2)}, u32[]{:S(2)}) collective-permute-start(bf16[32,512]{1,0:T(8,128)(2,1)S(1)} %get-tuple-element.58), channel_id=1, source_target_pairs={{0,4},{2,6},{4,0},{6,2},{8,12},{10,14},{12,8},{14,10},{16,20},{18,... | collective-permute-start | bytes 98312 | tf_op jit(solution)/shard_map/ppermute | solution.py:22
  49.8 4.1 %collective-permute-start.14 = (bf16[32,512]{1,0:T(8,128)(2,1)S(1)}, bf16[32,512]{1,0:T(8,128)(2,1)S(1)}, u32[]{:S(2)}, u32[]{:S(2)}) collective-permute-start(bf16[32,512]{1,0:T(8,128)(2,1)S(1)} %get-tuple-element.57), channel_id=1, source_target_pairs={{0,8},{2,10},{4,12},{6,14},{8,0},{10,2},{12,4},{14,6},{16,24},{18,... | collective-permute-start | bytes 98312 | tf_op jit(solution)/shard_map/ppermute | solution.py:22
  51.2 4.8 %collective-permute-start.13 = (bf16[32,512]{1,0:T(8,128)(2,1)S(1)}, bf16[32,512]{1,0:T(8,128)(2,1)S(1)}, u32[]{:S(2)}, u32[]{:S(2)}) collective-permute-start(bf16[32,512]{1,0:T(8,128)(2,1)S(1)} %get-tuple-element.56), channel_id=1, source_target_pairs={{0,12},{2,14},{4,8},{6,10},{8,4},{10,6},{12,0},{14,2},{16,28},{18,... | collective-permute-start | bytes 98312 | tf_op jit(solution)/shard_map/ppermute | solution.py:22

commit v6 on v4

v6 whole, which is shorter than its diff:
```python
import math

import jax
import jax.numpy as jnp
from jax import lax
from jax.experimental import pallas as pl
from jax.experimental.pallas import tpu as pltpu
from jax.sharding import PartitionSpec as P


SHARE = 0.1
BETA_SCALE = 0.5
BF16 = jnp.bfloat16
F32 = jnp.float32


def swapped(x, mask):
    return lax.ppermute(x, "dom", [(i, i ^ mask) for i in range(lax.axis_size("dom"))])


def every_piece(x):
    n = lax.axis_size("segment")
    return [x] + [lax.ppermute(x, "segment", [(i, (i + k) % n) for i in range(n)]) for k in range(1, n)]


def beta_of(k):
    return math.log(BETA_SCALE / (k + 1.0) + 1.0)


def mm(a, b):
    return jnp.dot(a, b, preferred_element_type=F32)


def mm_nt(a, b):
    return lax.dot_general(a, b, (((1,), (1,)), ((), ())), preferred_element_type=F32)


def mm_tn(a, b):
    return lax.dot_general(a, b, (((0,), (0,)), ((), ())), preferred_element_type=F32)


def place_of(seg, k, n):
    return lax.rem(seg - k + n, n)


def in_hbm(x):
    return pltpu.with_memory_space_constraint(x, pltpu.HBM)


def call(body, out_shape, ins, scratch=(), vmem=20):
    spaces = {"s": pltpu.SMEM, "h": pltpu.HBM, "v": pltpu.VMEM}
    specs = [pl.BlockSpec(memory_space=spaces[m]) for _, m in ins]
    arrays = [in_hbm(a) if m == "h" else a for a, m in ins]
    return pl.pallas_call(
        body,
        out_shape=tuple(out_shape),
        in_specs=specs,
        out_specs=tuple(pl.BlockSpec(memory_space=pltpu.VMEM) for _ in out_shape),
        scratch_shapes=list(scratch),
        compiler_params=pltpu.CompilerParams(vmem_limit_bytes=vmem << 20),
    )(*arrays)


sds = jax.ShapeDtypeStruct


def pack_call(scalars, feats, adj, couple, send_rows, cot, layers):
    rows, width = feats.shape
    piece = rows // layers
    picked = send_rows.shape[1]

    def body(sc, feats_r, adj_r, couple_r, sr_r, cot_r, ac_o, feats_o, cot_o, sr_s, sems):
        at = pl.ds(pl.multiple_of(sc[0] * piece, piece), piece)
        split = adj_r.shape[1]
        copies = [
            pltpu.make_async_copy(adj_r.at[at, :], ac_o.at[:piece, :split], sems.at[1]),
            pltpu.make_async_copy(couple_r.at[at, :], ac_o.at[:piece, split:], sems.at[2]),
            pltpu.make_async_copy(feats_r.at[at, :], feats_o, sems.at[0]),
            pltpu.make_async_copy(cot_r.at[at, :], cot_o, sems.at[3]),
        ]
        sr_copy = pltpu.make_async_copy(sr_r, sr_s, sems.at[4])
        sr_copy.start()
        for c in copies:
            c.start()
        ac_o[piece:, picked:] = jnp.zeros((8, width - picked), BF16)
        sr_copy.wait()
        ac_o[piece:, :picked] = jnp.broadcast_to(sr_s[...].astype(F32), (8, picked)).astype(BF16)
        for c in copies:
            c.wait()

    return call(
        body,
        (sds((piece + 8, width), BF16), sds((piece, width), BF16), sds((piece, width), BF16)),
        [(scalars, "s"), (feats, "h"), (adj, "h"), (couple, "h"), (send_rows, "h"), (cot, "h")],
        [pltpu.VMEM(send_rows.shape, jnp.int32), pltpu.SemaphoreType.DMA((5,))],
        4,
    )


def picks_of(sr, rows):
    ids = lax.broadcasted_iota(jnp.int32, (rows, sr.shape[1]), 0).astype(F32)
    return (ids == sr).astype(F32).astype(BF16)


def mixed_of(agg, first):
    return ((1.0 - SHARE) * agg + SHARE * first.astype(F32)).astype(BF16)


def activate(mixed, w, k):
    beta = beta_of(k)
    pre = (1.0 - beta) * mixed.astype(F32) + beta * mm(mixed, w)
    sig = 1.0 / (1.0 + jnp.exp(-pre))
    out = pre * sig
    return sig + out * (1.0 - sig), out.astype(BF16)


def piece_slice(seg, k, layers, piece):
    return pl.ds(pl.multiple_of(place_of(seg, k, layers) * piece, piece), piece)


def prep_call(scalars, feats, adj, couple, send_rows, w_pieces):
    layers = len(w_pieces)
    rows, width = feats.shape

    def body(sc, feats_r, adj_r, couple_r, sr_r, *refs):
        w_r = refs[:layers]
        x_o, own_o, couple_o, pick_o, agg_o, w_o, sr_s, sems = refs[layers:]
        seg = sc[0]
        copies = [
            pltpu.make_async_copy(sr_r, sr_s, sems.at[0]),
            pltpu.make_async_copy(couple_r, couple_o, sems.at[1]),
            pltpu.make_async_copy(feats_r, x_o, sems.at[2]),
            pltpu.make_async_copy(adj_r, own_o, sems.at[3]),
            pltpu.make_async_copy(w_r[0], w_o.at[seg], sems.at[4]),
        ]
        for c in copies:
            c.start()
        for k in range(1, layers):
            w_o[place_of(seg, k, layers)] = w_r[k][...]
        for c in copies:
            c.wait()
        pick_o[...] = picks_of(sr_s[...].astype(F32), rows)
        agg_o[...] = mm(own_o[...], x_o[...])

    return call(
        body,
        (
            sds((rows, width), BF16),
            sds((rows, rows), BF16),
            sds(couple.shape[:0] + (rows, couple.shape[1]), BF16),
            sds((rows, send_rows.shape[1]), BF16),
            sds((rows, width), F32),
            sds((layers, width, width), BF16),
        ),
        [(scalars, "s"), (feats, "h"), (adj, "h"), (couple, "h"), (send_rows, "h"), (w_pieces[0], "h")]
        + [(w, "v") for w in w_pieces[1:]],
        [pltpu.VMEM(send_rows.shape, jnp.int32), pltpu.SemaphoreType.DMA((5,))],
        8 + 2 * layers,
    )


def blocks_call(scalars, near, far, couple, pick):
    layers = len(near)
    rows = couple.shape[0]
    piece = rows // layers
    bound = couple.shape[1] // 2

    def body(sc, couple_r, pick_r, *refs):
        got_r = [refs[g * layers : (g + 1) * layers] for g in range(2)]
        own_o, near_o, far_o, cp_o, pick_o, ac_s = refs[2 * layers :]
        seg = sc[0]
        picks = [pick_r[...]]
        for g in range(2):
            for k in range(layers):
                at = piece_slice(seg, k, layers, piece)
                own_o[g, at, :] = got_r[g][k][:piece, :rows]
                ac_s[g, at, :] = got_r[g][k][:piece, rows:]
            picks.append(picks_of(got_r[g][0][piece : piece + 1, : 2 * bound].astype(F32), rows))
        near_o[0] = mm_nt(couple_r[:, :bound], picks[1][:, :bound]).astype(BF16)
        far_o[0] = mm_nt(couple_r[:, bound:], picks[2][:, bound:]).astype(BF16)
        near_o[1] = mm_nt(ac_s[0, :, :bound], picks[0][:, :bound]).astype(BF16)
        far_o[1] = mm_nt(ac_s[1, :, bound:], picks[0][:, bound:]).astype(BF16)
        cp_o[0] = ac_s[0, :, bound:]
        cp_o[1] = ac_s[1, :, :bound]
        pick_o[0] = picks[1][:, bound:]
        pick_o[1] = picks[2][:, :bound]

    return call(
        body,
        (sds((2, rows, rows), BF16),) * 3 + (sds((2, rows, bound), BF16),) * 2,
        [(scalars, "s"), (couple, "v"), (pick, "v")] + [(a, "v") for a in (*near, *far)],
        [pltpu.VMEM((2, rows, 2 * bound), BF16)],
        8,
    )


def own_call(scalars, near, far, diag, prep, blocks):
    x, _, _, _, agg, w = prep
    own12, near01, far02, cp, pick = blocks
    layers = len(near)
    rows, width = x.shape
    piece = rows // layers
    bound = cp.shape[2]

    def body(sc, x_r, agg_r, w_r, own12_r, near01_r, far02_r, cp_r, pick_r, *refs):
        got_r = [refs[g * layers : (g + 1) * layers] for g in range(3)]
        x12_o, mix_o, slope_o, x1_o, sums_o, own3_o, near23_o, far13_o, ac_s = refs[3 * layers :]
        seg = sc[0]
        for k in range(layers):
            at = piece_slice(seg, k, layers, piece)
            x12_o[0, at, :] = got_r[0][k][...]
            x12_o[1, at, :] = got_r[1][k][...]
            own3_o[at, :] = got_r[2][k][:piece, :rows]
            ac_s[at, :] = got_r[2][k][:piece, rows:]
        mixed = mixed_of(agg_r[...] + mm(near01_r[0], x12_o[0]) + mm(far02_r[0], x12_o[1]), x_r[...])
        mix_o[...] = mixed
        slope_o[...], x1_o[...] = activate(mixed, w_r[0], 0)
        picks = picks_of(got_r[2][0][piece : piece + 1, : 2 * bound].astype(F32), rows)
        far13_o[0] = mm_nt(cp_r[0], picks[:, bound:]).astype(BF16)
        near23_o[0] = mm_nt(cp_r[1], picks[:, :bound]).astype(BF16)
        near23_o[1] = mm_nt(ac_s[:, :bound], pick_r[1]).astype(BF16)
        far13_o[1] = mm_nt(ac_s[:, bound:], pick_r[0]).astype(BF16)
        sums_o[0] = mm(own12_r[0], x12_o[0]) + mm(near01_r[1], x_r[...])
        sums_o[1] = mm(own12_r[1], x12_o[1]) + mm(far02_r[1], x_r[...])
        sums_o[2] = mm(near23_o[1], x12_o[1]) + mm(far13_o[1], x12_o[0])

    return call(
        body,
        (
            sds((2, rows, width), BF16),
            sds((rows, width), BF16),
            sds((rows, width), F32),
            sds((rows, width), BF16),
            sds((3, rows, width), F32),
            sds((rows, rows), BF16),
            sds((2, rows, rows), BF16),
            sds((2, rows, rows), BF16),
        ),
        [(scalars, "s")]
        + [(a, "v") for a in (x, agg, w, own12, near01, far02, cp, pick, *near, *far, *diag)],
        [pltpu.VMEM((rows, 2 * bound), BF16)],
        16,
    )


def rest_call(scalars, diag, prep, own):
    x12, _, _, _, sums, own3, near23, far13 = own
    w = prep[-1]
    layers = len(diag)
    _, rows, width = x12.shape
    piece = rows // layers

    def body(sc, x12_r, sums_r, own3_r, near23_r, far13_r, w_r, *refs):
        got_r = refs[:layers]
        x3_o, mix_o, slope_o, x1_o = refs[layers:]
        seg = sc[0]
        for k in range(layers):
            x3_o[piece_slice(seg, k, layers, piece), :] = got_r[k][...]
        for g in range(3):
            blk = (far13_r[0], near23_r[0], own3_r[...])[g]
            agg = sums_r[g] + mm(blk, x3_o[...])
            mixed = mixed_of(agg, x12_r[g] if g < 2 else x3_o[...])
            mix_o[g] = mixed
            slope_o[g], x1_o[g] = activate(mixed, w_r[0], 0)

    return call(
        body,
        (
            sds((rows, width), BF16),
            sds((3, rows, width), BF16),
            sds((3, rows, width), F32),
            sds((3, rows, width), BF16),
        ),
        [(scalars, "s")] + [(a, "v") for a in (x12, sums, own3, near23, far13, w, *diag)],
        vmem=16,
    )


def matrix_of(prep, blocks, own):
    arrays = (prep[1], blocks[0], own[5], blocks[1], own[6], blocks[2], own[7])

    def readers(refs):
        own0, own12, own3, near01, near23, far02, far13 = refs
        return (
            lambda g: own0[...] if g == 0 else own3[...] if g == 3 else own12[g - 1],
            lambda g: (near01, near23)[g // 2][g % 2],
            lambda g: (far02, far13)[g % 2][g // 2],
        )

    return arrays, readers


def later_call(scalars, prep, own, rest, matrix):
    arrays, readers = matrix
    x, w = prep[0], prep[-1]
    layers = w.shape[0]
    rows, width = x.shape
    m = len(arrays)

    def body(sc, x_r, x12_r, x3_r, x1_r, x1n_r, w_r, *refs):
        own_at, near_at, far_at = readers(refs[:m])
        acts_o, mix_o, slope_o, xa_s, xb_s = refs[m:]
        seg = sc[0]
        first = (lambda: x_r[...], lambda: x12_r[0], lambda: x12_r[1], lambda: x3_r[...])

        @pl.when(seg == 0)
        def _():
            acts_o[...] = x1_r[...]

        def src(g):
            return x1n_r[g - 1] if g else x1_r[...]

        for k in range(1, layers):
            dst = (xa_s, xb_s)[k % 2]
            for g in range(4):
                agg = mm(own_at(g), src(g)) + mm(near_at(g), src(g ^ 1)) + mm(far_at(g), src(g ^ 2))
                mixed = mixed_of(agg, first[g]())
                mix_o[k - 1, g] = mixed
                slope_o[k - 1, g], out = activate(mixed, w_r[k], k)
                if k + 1 < layers:
                    dst[g] = out
                if g == 0:

                    @pl.when(seg == k)
                    def _():
                        acts_o[...] = out

            def src(g, dst=dst):
                return dst[g]

    return call(
        body,
        (
            sds((rows, width), BF16),
            sds((layers - 1, 4, rows, width), BF16),
            sds((layers - 1, 4, rows, width), F32),
        ),
        [(scalars, "s")] + [(a, "v") for a in (x, own[0], rest[0], own[3], rest[3], w, *arrays)],
        [pltpu.VMEM((4, rows, width), BF16)] * 2,
        min(60, 14 + 6 * layers),
    )


def dmix_of(dpre, w, k):
    beta = beta_of(k)
    return ((1.0 - beta) * dpre.astype(F32) + beta * mm_nt(dpre, w)).astype(BF16)


def back_start_call(scalars, cot, near, far, w, later_slope, matrix):
    arrays, readers = matrix
    layers = w.shape[0]
    rows, width = cot.shape
    piece = rows // layers
    m = len(arrays)
    last = layers - 1

    def body(sc, cot_r, w_r, slope_r, *refs):
        own_at, near_at, far_at = readers(refs[:m])
        got_r = [refs[m + g * layers : m + (g + 1) * layers] for g in range(2)]
        dpre_o, sums_o, carry_o, up_s = refs[m + 2 * layers :]
        seg = sc[0]
        for g in range(2):
            for k in range(layers):
                up_s[g, piece_slice(seg, k, layers, piece), :] = got_r[g][k][...]
        dmix = []
        for g in range(3):
            up = up_s[g - 1] if g else cot_r[...]
            dpre = (up.astype(F32) * slope_r[last - 1, g]).astype(BF16)
            dpre_o[pl.ds(g * rows, rows), :] = dpre
            dmix.append(dmix_of(dpre, w_r[last], last))
        carry_o[...] = SHARE * dmix[0].astype(F32)
        sums_o[0] = mm_tn(own_at(0), dmix[0]) + mm_tn(near_at(1), dmix[1]) + mm_tn(far_at(2), dmix[2])
        sums_o[1] = mm_tn(own_at(1), dmix[1]) + mm_tn(near_at(0), dmix[0])
        sums_o[2] = mm_tn(own_at(2), dmix[2]) + mm_tn(far_at(0), dmix[0])
        sums_o[3] = mm_tn(near_at(2), dmix[2]) + mm_tn(far_at(1), dmix[1])

    return call(
        body,
        (sds((3 * rows, width), BF16), sds((4, rows, width), F32), sds((rows, width), F32)),
        [(scalars, "s")] + [(a, "v") for a in (cot, w, later_slope, *arrays, *near, *far)],
        [pltpu.VMEM((2, rows, width), BF16)],
        min(60, 14 + 6 * layers),
    )


def back_call(scalars, diag, start, prep, own, rest, later_mix, later_slope, matrix):
    arrays, readers = matrix
    dpre_start, sums, carry = start
    mix, slope = own[1], own[2]
    mix_rest, slope_rest = rest[1], rest[2]
    w = prep[-1]
    layers = w.shape[0]
    rows, width = mix.shape
    piece = rows // layers
    n_dom = lax.axis_size("dom")
    others = n_dom // 4
    out_rows = width // n_dom
    half = width // 2
    m = len(arrays)
    last = layers - 1

    def body(sc, dps_r, sums_r, carry_r, mix_r, slope_r, mixn_r, slopen_r, later_mix_r, later_slope_r, w_r, *refs):
        own_at, near_at, far_at = readers(refs[:m])
        got_r = refs[m : m + layers]
        outs = refs[m + layers :]
        dpre_o, carry_o, mine_o = outs[:3]
        send_o = outs[3 : 2 + others]
        up_s, dmix_s, part_s = outs[2 + others :]
        seg, low, high, place = sc[0], sc[1], sc[2], sc[3]
        for k in range(layers):
            up_s[3, piece_slice(seg, k, layers, piece), :] = got_r[k][...]

        def weight_part(k, dpre_at):
            at = pl.ds(pl.multiple_of(high * half, half), half)
            part = None
            for g in range(4):
                chosen = later_mix_r[k - 1, g, :, at] if k else (mixn_r[g - 1, :, at] if g else mix_r[:, at])
                one = mm_tn(chosen, dpre_at(g))
                part = one if part is None else part + one
            part_s[...] = beta_of(k) * part

        dpre = (up_s[3].astype(F32) * later_slope_r[last - 1, 3]).astype(BF16)
        dpre_o[pl.ds(3 * rows, rows), :] = dpre
        dmix = dmix_of(dpre, w_r[last], last)
        extra = (None, mm_tn(far_at(3), dmix), mm_tn(near_at(3), dmix), mm_tn(own_at(3), dmix))
        for g in range(4):
            total = sums_r[g] if g == 0 else sums_r[g] + extra[g]
            up_s[g] = ((1.0 - SHARE) * total).astype(BF16)

        @pl.when(seg == last)
        def _():
            weight_part(last, lambda g: dps_r[pl.ds(g * rows, rows), :] if g < 3 else dpre_o[pl.ds(g * rows, rows), :])

        carry_o[...] = carry_r[...]
        for k in range(last - 1, -1, -1):
            for g in range(4):
                slope_now = later_slope_r[k - 1, g] if k else (slopen_r[g - 1] if g else slope_r[...])
                dpre = (up_s[g].astype(F32) * slope_now).astype(BF16)
                dpre_o[pl.ds(g * rows, rows), :] = dpre
                if k:
                    dmix = dmix_of(dpre, w_r[k], k)
                    dmix_s[g] = dmix
                    if g == 0:
                        carry_o[...] = SHARE * dmix.astype(F32) + carry_o[...]

            @pl.when(seg == k)
            def _():
                weight_part(k, lambda g: dpre_o[pl.ds(g * rows, rows), :])

            if k:
                for g in range(4):
                    total = (
                        mm_tn(own_at(g), dmix_s[g])
                        + mm_tn(near_at(g ^ 1), dmix_s[g ^ 1])
                        + mm_tn(far_at(g ^ 2), dmix_s[g ^ 2])
                    )
                    up_s[g] = ((1.0 - SHARE) * total).astype(BF16)

        def block(b):
            at = (place ^ b) * (2 * out_rows) + low * out_rows
            return part_s[pl.ds(pl.multiple_of(at, out_rows), out_rows), :]

        mine_o[...] = block(0)
        for b in range(1, others):
            send_o[b - 1][...] = block(b).astype(BF16)

    got = call(
        body,
        (sds((4 * rows, width), BF16), sds((rows, width), F32), sds((out_rows, width), F32))
        + tuple(sds((out_rows, width), BF16) for _ in range(1, others)),
        [(scalars, "s")]
        + [
            (a, "v")
            for a in (
                dpre_start,
                sums,
                carry,
                mix,
                slope,
                mix_rest,
                slope_rest,
                later_mix,
                later_slope,
                w,
                *arrays,
                *diag,
            )
        ],
        [
            pltpu.VMEM((4, rows, width), BF16),
            pltpu.VMEM((4, rows, width), BF16),
            pltpu.VMEM((half, width), F32),
        ],
        min(60, 14 + 6 * layers),
    )
    return got[0], got[1], got[2], got[3:]


def feat_call(scalars, dpre, carry, w, matrix):
    arrays, readers = matrix
    layers = w.shape[0]
    rows, width = carry.shape
    cols = width // layers
    sliced = cols % 128 == 0
    kept = cols if sliced else width
    m = len(arrays)
    beta = beta_of(0)

    def body(sc, dpre_r, carry_r, w_r, *refs):
        own_at, near_at, far_at = readers(refs[:m])
        feat_o = refs[m]
        at = pl.ds(pl.multiple_of(sc[0] * cols, cols), cols) if sliced else slice(None)
        w_rows = w_r[0, at, :]
        dmix = []
        for g in range(3):
            d_at = pl.ds(g * rows, rows)
            through = mm_nt(dpre_r[d_at, :], w_rows)
            dmix.append(((1.0 - beta) * dpre_r[d_at, at].astype(F32) + beta * through).astype(BF16))
        sums = mm_tn(own_at(0), dmix[0]) + mm_tn(near_at(1), dmix[1]) + mm_tn(far_at(2), dmix[2])
        feat_o[...] = (1.0 - SHARE) * sums + (carry_r[:, at] + SHARE * dmix[0].astype(F32))

    (feat,) = call(
        body,
        (sds((rows, kept), F32),),
        [(scalars, "s")] + [(a, "v") for a in (dpre, carry, w, *arrays)],
        vmem=12,
    )
    return feat if sliced else lax.dynamic_slice_in_dim(feat, scalars[0] * cols, cols, 1)


def step(feats, adj, couple, send_rows, weights, cot):
    seg = lax.axis_index("segment")
    dom = lax.axis_index("dom")
    layers = lax.axis_size("segment")
    n_dom = lax.axis_size("dom")
    top = n_dom // 2
    others = n_dom // 4
    place = (dom // 2) % others
    scalars = jnp.stack([seg, dom & 1, dom // top, place]).astype(jnp.int32)

    ac_mine, f_mine, cot_mine = pack_call(scalars, feats, adj, couple, send_rows, cot, layers)
    far_ac = swapped(ac_mine, top)
    near_ac = swapped(ac_mine, 1)
    w_pieces = every_piece(weights)
    prep = prep_call(scalars, feats, adj, couple, send_rows, w_pieces)
    far_f = swapped(f_mine, top)
    near_f = swapped(f_mine, 1)
    near_cot = swapped(cot_mine, 1)
    near_acs = every_piece(near_ac)
    diag_ac = swapped(far_ac, 1)
    far_acs = every_piece(far_ac)
    near_fs = every_piece(near_f)
    blocks = blocks_call(scalars, near_acs, far_acs, prep[2], prep[3])
    far_cot = swapped(cot_mine, top)
    diag_acs = every_piece(diag_ac)
    diag_f = swapped(far_f, 1)
    far_fs = every_piece(far_f)
    near_cots = every_piece(near_cot)
    own = own_call(scalars, near_fs, far_fs, diag_acs, prep, blocks)
    diag_fs = every_piece(diag_f)
    diag_cot = swapped(far_cot, 1)
    far_cots = every_piece(far_cot)
    matrix = matrix_of(prep, blocks, own)
    rest = rest_call(scalars, diag_fs, prep, own)
    acts, later_mix, later_slope = later_call(scalars, prep, own, rest, matrix)
    diag_cots = every_piece(diag_cot)
    start = back_start_call(scalars, cot, near_cots, far_cots, prep[-1], later_slope, matrix)
    dpre, carry, wgrad, sends = back_call(
        scalars, diag_cots, start, prep, own, rest, later_mix, later_slope, matrix
    )
    for m in range(others - 1, 0, -1):
        wgrad = wgrad + swapped(sends[m - 1], 2 * m).astype(F32)
    feat = feat_call(scalars, dpre, carry, prep[-1], matrix)
    return (acts[None], wgrad[None], feat)


def solution(mesh):
    in_specs = (
        P("dom", None),
        P("dom", None),
        P("dom", None),
        P("dom", None),
        P("segment", None),
        P("dom", None),
    )
    out_specs = (P("segment", "dom", None), P("segment", "dom", None), P("dom", "segment"))
    return jax.shard_map(step, mesh=mesh, in_specs=in_specs, out_specs=out_specs, check_vma=False)
```

time: 64.5 us -> 59.4 us (0.921)
  local copies, waits for them, and re-layouts: 8.87 us -> 0.01 us
  starting transfers between devices: 13.8 us -> 21.6 us
  waiting for transfers between devices: 26.1 us -> 18.5 us
  Pallas kernels: 13.9 us -> 17.6 us
    unnamed x22 -> x2, local copies, waits for them, and re-layouts: 8.87 us -> 0.01 us
    ppermute x9 -> x12, waiting for transfers between devices: 26.1 us -> 18.5 us  [swapped(): lax.ppermute(x, 'dom', [(i, i ^ mask) for i in range(lax.axis_size('dom'))])]
    ppermute x9 -> x12, starting transfers between devices: 12.7 us -> 19.6 us  [swapped(): lax.ppermute(x, 'dom', [(i, i ^ mask) for i in range(lax.axis_size('dom'))])]
    pallas_call x6 -> x9, Pallas kernels: 13.9 us -> 17.6 us  [call(): pl.pallas_call(body, out_shape=tuple(out_shape), in_specs=specs, out_spec...]
    ppermute x7 -> x10, starting transfers between devices: 1.1 us -> 2.05 us  [every_piece(): lax.ppermute(x, 'segment', [(i, (i + k) % n) for i in range(n)])]
  transfers between devices with their start and end apart: 16 -> 22, of which waited for: 6 -> 6; matrix products, arithmetic and copies ran while one was open for 0% -> 0% of each run, Pallas kernels for 15% -> 23%
where the time goes in v6:
time: 59.4 us; the launch traced here: 59.2 us
  starting transfers between devices  21.6 us (36%)
  waiting for transfers between devices  18.5 us (31%)
  Pallas kernels  17.6 us (30%)
  between operations  0.78 us (1%)
  other arithmetic  0.72 us (1%)
    ppermute x12, starting transfers between devices, swapped(): lax.ppermute(x, 'dom', [(i, i ^ mask) for i in range(lax.axis_size('dom'))])  19.6 us
    ppermute x12, waiting for transfers between devices, swapped(): lax.ppermute(x, 'dom', [(i, i ^ mask) for i in range(lax.axis_size('dom'))])  18.5 us
    pallas_call x9, Pallas kernels, call(): pl.pallas_call(body, out_shape=tuple(out_shape), in_specs=specs, out_spec...  17.6 us
    ppermute x10, starting transfers between devices, every_piece(): lax.ppermute(x, 'segment', [(i, (i + k) % n) for i in range(n)])  2.05 us
  transfers between devices with their start and end apart: 22, of which 6 were waited for; matrix products, arithmetic and copies ran while one was open for 0% of the time, Pallas kernels for 23%

profile of v6, /device:TPU:0, one launch (start us, length us, event | category | flops | bytes accessed | tf_op | source)
XLA Modules:
  0.0 59.2 jit_solution(14875597658740722688)
XLA Ops:
  0.7 1.6 %shard_map.86 = (bf16[136,512]{1,0:T(8,128)(2,1)S(1)}, bf16[128,512]{1,0:T(8,128)(2,1)S(1)}, bf16[128,512]{1,0:T(8,128)(2,1)S(1)}) custom-call(s32[4]{0:T(128)S(1)} %pad_add_fusion.sc, bf16[256,512]{1,0:T(8,128)(2,1)} %feats_r.3, bf16[256,256]{1,0:T(8,128)(2,1)} %adj_r.3, bf16[256,256]{1,0:T(8,128)(2,1)} %couple_r.3, s32[1,256]{1,0:T(1,128)} %sr_r.3, ...), custom_call_target="tpu_custom_call" | custom-call | tf_op jit(solution)/shard_map/pallas_call | solution.py:54
  2.4 4.1 %collective-permute-start.7 = (bf16[128,512]{1,0:T(8,128)(2,1)S(1)}, bf16[128,512]{1,0:T(8,128)(2,1)S(1)}, u32[]{:S(2)}, u32[]{:S(2)}) collective-permute-start(bf16[128,512]{1,0:T(8,128)(2,1)S(1)} %get-tuple-element.52), channel_id=1, source_target_pairs={{0,16},{2,18},{4,20},{6,22},{8,24},{10,26},{12,28},{14,30},{16,0},... | collective-permute-start | bytes 393224 | tf_op jit(solution)/shard_map/ppermute | solution.py:18
  6.5 1.5 %collective-permute-start.5 = (bf16[128,512]{1,0:T(8,128)(2,1)S(1)}, bf16[128,512]{1,0:T(8,128)(2,1)S(1)}, u32[]{:S(2)}, u32[]{:S(2)}) collective-permute-start(bf16[128,512]{1,0:T(8,128)(2,1)S(1)} %get-tuple-element.52), channel_id=1, source_target_pairs={{0,2},{2,0},{4,6},{6,4},{8,10},{10,8},{12,14},{14,12},{16,18},{18,... | collective-permute-start | bytes 393224 | tf_op jit(solution)/shard_map/ppermute | solution.py:18
  8.0 0.3 collective-permute-start.3
  8.3 2.6 %collective-permute-start.15 = (bf16[128,512]{1,0:T(8,128)(2,1)S(1)}, bf16[128,512]{1,0:T(8,128)(2,1)S(1)}, u32[]{:S(2)}, u32[]{:S(2)}) collective-permute-start(bf16[128,512]{1,0:T(8,128)(2,1)S(1)} %get-tuple-element.64), channel_id=1, source_target_pairs={{0,16},{2,18},{4,20},{6,22},{8,24},{10,26},{12,28},{14,30},{16,0},... | collective-permute-start | bytes 393224 | tf_op jit(solution)/shard_map/ppermute | solution.py:18
  10.9 8.5 %collective-permute-done.7.refs_2_ = bf16[128,512]{1,0:T(8,128)(2,1)S(1)} collective-permute-done((bf16[128,512]{1,0:T(8,128)(2,1)S(1)}, bf16[128,512]{1,0:T(8,128)(2,1)S(1)}, u32[]{:S(2)}, u32[]{:S(2)}) %collective-permute-start.7) | collective-permute-done | bytes 131104 | tf_op jit(solution)/shard_map/ppermute | solution.py:18
  19.5 1.8 %collective-permute-start.13 = (bf16[128,512]{1,0:T(8,128)(2,1)S(1)}, bf16[128,512]{1,0:T(8,128)(2,1)S(1)}, u32[]{:S(2)}, u32[]{:S(2)}) collective-permute-start(bf16[128,512]{1,0:T(8,128)(2,1)S(1)} %get-tuple-element.64), channel_id=1, source_target_pairs={{0,2},{2,0},{4,6},{6,4},{8,10},{10,8},{12,14},{14,12},{16,18},{18,... | collective-permute-start | bytes 393224 | tf_op jit(solution)/shard_map/ppermute | solution.py:18
  21.3 0.2 collective-permute-start.1
  21.5 2.9 %collective-permute-done.15.refs_9_ = bf16[128,512]{1,0:T(8,128)(2,1)S(1)} collective-permute-done((bf16[128,512]{1,0:T(8,128)(2,1)S(1)}, bf16[128,512]{1,0:T(8,128)(2,1)S(1)}, u32[]{:S(2)}, u32[]{:S(2)}) %collective-permute-start.15) | collective-permute-done | bytes 131104 | tf_op jit(solution)/shard_map/ppermute | solution.py:18
  24.4 1.5 %collective-permute-start.11 = (bf16[128,512]{1,0:T(8,128)(2,1)S(1)}, bf16[128,512]{1,0:T(8,128)(2,1)S(1)}, u32[]{:S(2)}, u32[]{:S(2)}) collective-permute-start(bf16[128,512]{1,0:T(8,128)(2,1)S(1)} %collective-permute-done.7.refs_2_), channel_id=1, source_target_pairs={{0,2},{2,0},{4,6},{6,4},{8,10},{10,8},{12,14},{14,12},{16,18},{18,... | collective-permute-start | bytes 393224 | tf_op jit(solution)/shard_map/ppermute | solution.py:18
  26.0 0.5 collective-permute-start.6
  26.5 1.4 %collective-permute-start.9 = (bf16[136,512]{1,0:T(8,128)(2,1)S(1)}, bf16[136,512]{1,0:T(8,128)(2,1)S(1)}, u32[]{:S(2)}, u32[]{:S(2)}) collective-permute-start(bf16[136,512]{1,0:T(8,128)(2,1)S(1)} %collective-permute-done.3.refs_2_), channel_id=1, source_target_pairs={{0,2},{2,0},{4,6},{6,4},{8,10},{10,8},{12,14},{14,12},{16,18},{18,... | collective-permute-start | bytes 417800 | tf_op jit(solution)/shard_map/ppermute | solution.py:18
  27.9 1.8 %collective-permute-done.11.refs_0_ = bf16[128,512]{1,0:T(8,128)(2,1)S(1)} collective-permute-done((bf16[128,512]{1,0:T(8,128)(2,1)S(1)}, bf16[128,512]{1,0:T(8,128)(2,1)S(1)}, u32[]{:S(2)}, u32[]{:S(2)}) %collective-permute-start.11) | collective-permute-done | bytes 131104 | tf_op jit(solution)/shard_map/ppermute | solution.py:18
  29.7 0.5 collective-permute-start.2
  30.3 2.5 %collective-permute-start.17 = (bf16[128,512]{1,0:T(8,128)(2,1)S(1)}, bf16[128,512]{1,0:T(8,128)(2,1)S(1)}, u32[]{:S(2)}, u32[]{:S(2)}) collective-permute-start(bf16[128,512]{1,0:T(8,128)(2,1)S(1)} %collective-permute-done.15.refs_9_), channel_id=1, source_target_pairs={{0,2},{2,0},{4,6},{6,4},{8,10},{10,8},{12,14},{14,12},{16,18},{18,... | collective-permute-start | bytes 393224 | tf_op jit(solution)/shard_map/ppermute | solution.py:18
  32.7 3.7 %collective-permute-done.17.refs_7_ = bf16[128,512]{1,0:T(8,128)(2,1)S(1)} collective-permute-done((bf16[128,512]{1,0:T(8,128)(2,1)S(1)}, bf16[128,512]{1,0:T(8,128)(2,1)S(1)}, u32[]{:S(2)}, u32[]{:S(2)}) %collective-permute-start.17) | collective-permute-done | bytes 131104 | tf_op jit(solution)/shard_map/ppermute | solution.py:18
  36.5 0.5 collective-permute-start.16
  37.1 0.4 collective-permute-start.18
  37.5 2.1 %shard_map.85 = (bf16[256,512]{1,0:T(8,128)(2,1)S(1)}, bf16[256,256]{1,0:T(8,128)(2,1)S(1)}, bf16[256,256]{1,0:T(8,128)(2,1)S(1)}, bf16[256,256]{1,0:T(8,128)(2,...) custom-call(s32[4]{0:T(128)S(1)} %pad_add_fusion.sc, bf16[256,512]{1,0:T(8,128)(2,1)} %feats_r.3, ...), custom_call_target="tpu_custom_call" | custom-call | tf_op jit(solution)/shard_map/pallas_call | solution.py:54
  39.6 0.9 %shard_map.87 = (bf16[2,256,256]{2,1,0:T(8,128)(2,1)S(1)}, bf16[2,256,256]{2,1,0:T(8,128)(2,1)S(1)}, bf16[2,256,256]{2,1,0:T(8,128)(2,1)S(1)}, bf16[2,256,128]{2,1,0:T(8,128)(2,1)S(1)}, bf16[2,256,128]{2,1,0:T(8,128)(2,1)S(1)}) custom-call(s32[4]{0:T(128)S(1)} %pad_add_fusion.sc, bf16[256,256]{1,0:T(8,128)(2,1)S(1)} %get-tuple-element.44.couple_r, ...), custom_call_target="tpu_custom_call" | custom-call | tf_op jit(solution)/shard_map/pallas_call | solution.py:54
  40.5 1.8 %shard_map.88 = (bf16[2,256,512]{2,1,0:T(8,128)(2,1)S(1)}, bf16[256,512]{1,0:T(8,128)(2,1)S(1)}, f32[256,512]{1,0:T(8,128)S(1)}, bf16[256,512]{1,0:T(8,128)(2,1)...) custom-call(s32[4]{0:T(128)S(1)} %pad_add_fusion.sc, ...), custom_call_target="tpu_custom_call" | custom-call | tf_op jit(solution)/shard_map/pallas_call | solution.py:54
  42.3 2.0 %shard_map.89 = (bf16[256,512]{1,0:T(8,128)(2,1)S(1)}, bf16[3,256,512]{2,1,0:T(8,128)(2,1)S(1)}, f32[3,256,512]{2,1,0:T(8,128)S(1)}, bf16[3,256,512]{2,1,0:T(8,128)(2,1)S(1)}) custom-call(s32[4]{0:T(128)S(1)} %pad_add_fusion.sc, bf16[2,256,512]{2,1,0:T(8,128)(2,1)S(1)} %get-tuple-element.53.x12_r, f32[3,256,512]{2,1,0:T(8,128)S(1)} %get-tuple-element.54.sums_r, ...), custom_call_target="tpu_custom_call" | custom-call | tf_op jit(solution)/shard_map/pallas_call | solution.py:54
  44.4 3.2 %shard_map.90 = (bf16[256,512]{1,0:T(8,128)(2,1)}, bf16[1,4,256,512]{3,2,1,0:T(8,128)(2,1)S(1)}, f32[1,4,256,512]{3,2,1,0:T(8,128)S(1)}) custom-call(s32[4]{0:T(128)S(1)} %pad_add_fusion.sc, bf16[256,512]{1,0:T(8,128)(2,1)S(1)} %get-tuple-element.41.x_r, bf16[2,256,512]{2,1,0:T(8,128)(2,1)S(1)} %get-tuple-element.53.x12_r, ...), custom_call_target="tpu_custom_call" | custom-call | tf_op jit(solution)/shard_map/pallas_call | solution.py:54
  47.6 2.0 %shard_map.91 = (bf16[768,512]{1,0:T(8,128)(2,1)S(1)}, f32[4,256,512]{2,1,0:T(8,128)S(1)}, f32[256,512]{1,0:T(8,128)S(1)}) custom-call(s32[4]{0:T(128)S(1)} %pad_add_fusion.sc, bf16[256,512]{1,0:T(8,128)(2,1)S(1)} %copy-done, bf16[2,512,512]{2,1,0:T(8,128)(2,1)S(1)} %get-tuple-element.43.w_r, f32[1,4,256,512]{3,2,1,0:T(8,128)S(1)} %get-tuple-element.63.slope_r.later_slope_r, ...), custom_call_target="tpu_custom_call" | custom-call | tf_op jit(solution)/shard_map/pallas_call | solution.py:54
  49.6 2.0 %shard_map.92 = (bf16[1024,512]{1,0:T(8,128)(2,1)S(1)}, f32[256,512]{1,0:T(8,128)S(1)}, f32[32,512]{1,0:T(8,128)S(1)}, bf16[32,512]{1,0:T(8,128)(2,1)S(1)}, bf16...) custom-call(s32[4]{0:T(128)S(1)} %pad_add_fusion.sc, bf16[768,512]{1,0:T(8,128)(2,1)S(1)} %get-tuple-element.65.dps_r, ...), custom_call_target="tpu_custom_call" | custom-call | tf_op jit(solution)/shard_map/pallas_call | solution.py:54
  51.6 1.9 %collective-permute-start.19 = (bf16[32,512]{1,0:T(8,128)(2,1)S(1)}, bf16[32,512]{1,0:T(8,128)(2,1)S(1)}, u32[]{:S(2)}, u32[]{:S(2)}) collective-permute-start(bf16[32,512]{1,0:T(8,128)(2,1)S(1)} %get-tuple-element.74), channel_id=1, source_target_pairs={{0,12},{2,14},{4,8},{6,10},{8,4},{10,6},{12,0},{14,2},{16,28},{18,... | collective-permute-start | bytes 98312 | tf_op jit(solution)/shard_map/ppermute | solution.py:18
  53.5 1.1 %collective-permute-start.20 = (bf16[32,512]{1,0:T(8,128)(2,1)S(1)}, bf16[32,512]{1,0:T(8,128)(2,1)S(1)}, u32[]{:S(2)}, u32[]{:S(2)}) collective-permute-start(bf16[32,512]{1,0:T(8,128)(2,1)S(1)} %get-tuple-element.75), channel_id=1, source_target_pairs={{0,8},{2,10},{4,12},{6,14},{8,0},{10,2},{12,4},{14,6},{16,24},{18,... | collective-permute-start | bytes 98312 | tf_op jit(solution)/shard_map/ppermute | solution.py:18
  54.6 0.6 collective-permute-start.21
  55.2 1.9 %shard_map.93 = f32[256,256]{1,0:T(8,128)} custom-call(s32[4]{0:T(128)S(1)} %pad_add_fusion.sc, bf16[1024,512]{1,0:T(8,128)(2,1)S(1)} %get-tuple-element.77.dpre_r, f32[256,512]{1,0:T(8,128)S(1)} %get-tuple-element.78.carry_r, bf16[2,512,512]{2,1,0:T(8,128)(2,1)S(1)} %get-tuple-element.43.w_r, bf16[256,256]{1,0:T(8,128)(2,1)S(1)} %get-tuple-element.61.refs_0_, ...), custom_call_target="tpu_custom_call" | custom-call | tf_op jit(solution)/shard_map/pallas_call | solution.py:54
  57.1 0.3 collective-permute-done.20
  57.4 1.1 %collective-permute-done.21 = bf16[32,512]{1,0:T(8,128)(2,1)S(1)} collective-permute-done((bf16[32,512]{1,0:T(8,128)(2,1)S(1)}, bf16[32,512]{1,0:T(8,128)(2,1)S(1)}, u32[]{:S(2)}, u32[]{:S(2)}) %collective-permute-start.21) | collective-permute-done | bytes 32800 | tf_op jit(solution)/shard_map/ppermute | solution.py:18
  58.6 0.6 %add_bitcast_fusion = f32[1,32,512]{2,1,0:T(8,128)} fusion(bf16[32,512]{1,0:T(8,128)(2,1)S(1)} %collective-permute-done.21, bf16[32,512]{1,0:T(8,128)(2,1)S(1)} %collective-permute-done.20, f32[32,512]{1,0:T(8,128)S(1)} %get-tuple-element.73, bf16[32,512]{1,0:T(8,128)(2,1)S(1)} %collective-permute-done.19), kind=kLoop, calls=%fused_computation | loop fusion | flops 98304 | bytes 229376 | tf_op jit(solution)/shard_map/broadcast_in_dim | solution.py:574
  (25 shorter events, 0.2 us)
Async XLA Ops:
  2.4 17.1 %collective-permute-start.7 = (bf16[128,512]{1,0:T(8,128)(2,1)S(1)}, bf16[128,512]{1,0:T(8,128)(2,1)S(1)}, u32[]{:S(2)}, u32[]{:S(2)}) collective-permute-start(bf16[128,512]{1,0:T(8,128)(2,1)S(1)} %get-tuple-element.52), channel_id=1, source_target_pairs={{0,16},{2,18},{4,20},{6,22},{8,24},{10,26},{12,28},{14,30},{16,0},... | collective-permute-start | bytes 393224 | tf_op jit(solution)/shard_map/ppermute | solution.py:18
  6.5 30.5 %collective-permute-start = (bf16[512,512]{1,0:T(8,128)(2,1)}, bf16[512,512]{1,0:T(8,128)(2,1)S(1)}, u32[]{:S(2)}, u32[]{:S(2)}) collective-permute-start(bf16[512,512]{1,0:T(8,128)(2,1)} %refs_0_.1), channel_id=1, source_target_pairs={{0,1},{1,0},{2,3},{3,2},{4,5},{5,4},{6,7},{7,6},{8,9},{9,8},{10,11... | collective-permute-start | bytes 1572872 | tf_op jit(solution)/shard_map/ppermute | solution.py:23
  6.5 14.7 %collective-permute-start.5 = (bf16[128,512]{1,0:T(8,128)(2,1)S(1)}, bf16[128,512]{1,0:T(8,128)(2,1)S(1)}, u32[]{:S(2)}, u32[]{:S(2)}) collective-permute-start(bf16[128,512]{1,0:T(8,128)(2,1)S(1)} %get-tuple-element.52), channel_id=1, source_target_pairs={{0,2},{2,0},{4,6},{6,4},{8,10},{10,8},{12,14},{14,12},{16,18},{18,... | collective-permute-start | bytes 393224 | tf_op jit(solution)/shard_map/ppermute | solution.py:18
  8.0 17.9 %collective-permute-start.3 = (bf16[136,512]{1,0:T(8,128)(2,1)S(1)}, bf16[136,512]{1,0:T(8,128)(2,1)S(1)}, u32[]{:S(2)}, u32[]{:S(2)}) collective-permute-start(bf16[136,512]{1,0:T(8,128)(2,1)S(1)} %get-tuple-element.46), channel_id=1, source_target_pairs={{0,16},{2,18},{4,20},{6,22},{8,24},{10,26},{12,28},{14,30},{16,0},... | collective-permute-start | bytes 417800 | tf_op jit(solution)/shard_map/ppermute | solution.py:18
  8.3 16.1 %collective-permute-start.15 = (bf16[128,512]{1,0:T(8,128)(2,1)S(1)}, bf16[128,512]{1,0:T(8,128)(2,1)S(1)}, u32[]{:S(2)}, u32[]{:S(2)}) collective-permute-start(bf16[128,512]{1,0:T(8,128)(2,1)S(1)} %get-tuple-element.64), channel_id=1, source_target_pairs={{0,16},{2,18},{4,20},{6,22},{8,24},{10,26},{12,28},{14,30},{16,0},... | collective-permute-start | bytes 393224 | tf_op jit(solution)/shard_map/ppermute | solution.py:18
  19.5 6.5 %collective-permute-start.13 = (bf16[128,512]{1,0:T(8,128)(2,1)S(1)}, bf16[128,512]{1,0:T(8,128)(2,1)S(1)}, u32[]{:S(2)}, u32[]{:S(2)}) collective-permute-start(bf16[128,512]{1,0:T(8,128)(2,1)S(1)} %get-tuple-element.64), channel_id=1, source_target_pairs={{0,2},{2,0},{4,6},{6,4},{8,10},{10,8},{12,14},{14,12},{16,18},{18,... | collective-permute-start | bytes 393224 | tf_op jit(solution)/shard_map/ppermute | solution.py:18
  21.3 5.2 %collective-permute-start.1 = (bf16[136,512]{1,0:T(8,128)(2,1)S(1)}, bf16[136,512]{1,0:T(8,128)(2,1)S(1)}, u32[]{:S(2)}, u32[]{:S(2)}) collective-permute-start(bf16[136,512]{1,0:T(8,128)(2,1)S(1)} %get-tuple-element.46), channel_id=1, source_target_pairs={{0,2},{2,0},{4,6},{6,4},{8,10},{10,8},{12,14},{14,12},{16,18},{18,... | collective-permute-start | bytes 417800 | tf_op jit(solution)/shard_map/ppermute | solution.py:18
  24.4 5.3 %collective-permute-start.11 = (bf16[128,512]{1,0:T(8,128)(2,1)S(1)}, bf16[128,512]{1,0:T(8,128)(2,1)S(1)}, u32[]{:S(2)}, u32[]{:S(2)}) collective-permute-start(bf16[128,512]{1,0:T(8,128)(2,1)S(1)} %collective-permute-done.7.refs_2_), channel_id=1, source_target_pairs={{0,2},{2,0},{4,6},{6,4},{8,10},{10,8},{12,14},{14,12},{16,18},{18,... | collective-permute-start | bytes 393224 | tf_op jit(solution)/shard_map/ppermute | solution.py:18
  26.0 3.8 %collective-permute-start.8 = (bf16[128,512]{1,0:T(8,128)(2,1)S(1)}, bf16[128,512]{1,0:T(8,128)(2,1)S(1)}, u32[]{:S(2)}, u32[]{:S(2)}) collective-permute-start(bf16[128,512]{1,0:T(8,128)(2,1)S(1)} %collective-permute-done.7.refs_2_), channel_id=1, source_target_pairs={{0,1},{1,0},{2,3},{3,2},{4,5},{5,4},{6,7},{7,6},{8,9},{9,8},{10,11... | collective-permute-start | bytes 393224 | tf_op jit(solution)/shard_map/ppermute | solution.py:23
  26.0 4.3 %collective-permute-start.6 = (bf16[128,512]{1,0:T(8,128)(2,1)S(1)}, bf16[128,512]{1,0:T(8,128)(2,1)S(1)}, u32[]{:S(2)}, u32[]{:S(2)}) collective-permute-start(bf16[128,512]{1,0:T(8,128)(2,1)S(1)} %collective-permute-done.5.refs_0_), channel_id=1, source_target_pairs={{0,1},{1,0},{2,3},{3,2},{4,5},{5,4},{6,7},{7,6},{8,9},{9,8},{10,11... | collective-permute-start | bytes 393224 | tf_op jit(solution)/shard_map/ppermute | solution.py:23
  26.5 6.3 %collective-permute-start.9 = (bf16[136,512]{1,0:T(8,128)(2,1)S(1)}, bf16[136,512]{1,0:T(8,128)(2,1)S(1)}, u32[]{:S(2)}, u32[]{:S(2)}) collective-permute-start(bf16[136,512]{1,0:T(8,128)(2,1)S(1)} %collective-permute-done.3.refs_2_), channel_id=1, source_target_pairs={{0,2},{2,0},{4,6},{6,4},{8,10},{10,8},{12,14},{14,12},{16,18},{18,... | collective-permute-start | bytes 417800 | tf_op jit(solution)/shard_map/ppermute | solution.py:18
  29.7 6.7 %collective-permute-start.4 = (bf16[136,512]{1,0:T(8,128)(2,1)S(1)}, bf16[136,512]{1,0:T(8,128)(2,1)S(1)}, u32[]{:S(2)}, u32[]{:S(2)}) collective-permute-start(bf16[136,512]{1,0:T(8,128)(2,1)S(1)} %collective-permute-done.3.refs_2_), channel_id=1, source_target_pairs={{0,1},{1,0},{2,3},{3,2},{4,5},{5,4},{6,7},{7,6},{8,9},{9,8},{10,11... | collective-permute-start | bytes 417800 | tf_op jit(solution)/shard_map/ppermute | solution.py:23
  29.7 7.2 %collective-permute-start.2 = (bf16[136,512]{1,0:T(8,128)(2,1)S(1)}, bf16[136,512]{1,0:T(8,128)(2,1)S(1)}, u32[]{:S(2)}, u32[]{:S(2)}) collective-permute-start(bf16[136,512]{1,0:T(8,128)(2,1)S(1)} %collective-permute-done.1.refs_0_), channel_id=1, source_target_pairs={{0,1},{1,0},{2,3},{3,2},{4,5},{5,4},{6,7},{7,6},{8,9},{9,8},{10,11... | collective-permute-start | bytes 417800 | tf_op jit(solution)/shard_map/ppermute | solution.py:23
  30.3 6.2 %collective-permute-start.17 = (bf16[128,512]{1,0:T(8,128)(2,1)S(1)}, bf16[128,512]{1,0:T(8,128)(2,1)S(1)}, u32[]{:S(2)}, u32[]{:S(2)}) collective-permute-start(bf16[128,512]{1,0:T(8,128)(2,1)S(1)} %collective-permute-done.15.refs_9_), channel_id=1, source_target_pairs={{0,2},{2,0},{4,6},{6,4},{8,10},{10,8},{12,14},{14,12},{16,18},{18,... | collective-permute-start | bytes 393224 | tf_op jit(solution)/shard_map/ppermute | solution.py:18
  32.7 7.7 %collective-permute-start.10 = (bf16[136,512]{1,0:T(8,128)(2,1)S(1)}, bf16[136,512]{1,0:T(8,128)(2,1)S(1)}, u32[]{:S(2)}, u32[]{:S(2)}) collective-permute-start(bf16[136,512]{1,0:T(8,128)(2,1)S(1)} %collective-permute-done.9.refs_4_), channel_id=1, source_target_pairs={{0,1},{1,0},{2,3},{3,2},{4,5},{5,4},{6,7},{7,6},{8,9},{9,8},{10,11... | collective-permute-start | bytes 417800 | tf_op jit(solution)/shard_map/ppermute | solution.py:23
  36.5 5.8 %collective-permute-start.12 = (bf16[128,512]{1,0:T(8,128)(2,1)S(1)}, bf16[128,512]{1,0:T(8,128)(2,1)S(1)}, u32[]{:S(2)}, u32[]{:S(2)}) collective-permute-start(bf16[128,512]{1,0:T(8,128)(2,1)S(1)} %collective-permute-done.11.refs_0_), channel_id=1, source_target_pairs={{0,1},{1,0},{2,3},{3,2},{4,5},{5,4},{6,7},{7,6},{8,9},{9,8},{10,11... | collective-permute-start | bytes 393224 | tf_op jit(solution)/shard_map/ppermute | solution.py:23
  36.5 11.1 %collective-permute-start.16 = (bf16[128,512]{1,0:T(8,128)(2,1)S(1)}, bf16[128,512]{1,0:T(8,128)(2,1)S(1)}, u32[]{:S(2)}, u32[]{:S(2)}) collective-permute-start(bf16[128,512]{1,0:T(8,128)(2,1)S(1)} %collective-permute-done.15.refs_9_), channel_id=1, source_target_pairs={{0,1},{1,0},{2,3},{3,2},{4,5},{5,4},{6,7},{7,6},{8,9},{9,8},{10,11... | collective-permute-start | bytes 393224 | tf_op jit(solution)/shard_map/ppermute | solution.py:23
  37.0 10.6 %collective-permute-start.14 = (bf16[128,512]{1,0:T(8,128)(2,1)S(1)}, bf16[128,512]{1,0:T(8,128)(2,1)S(1)}, u32[]{:S(2)}, u32[]{:S(2)}) collective-permute-start(bf16[128,512]{1,0:T(8,128)(2,1)S(1)} %collective-permute-done.13.refs_7_), channel_id=1, source_target_pairs={{0,1},{1,0},{2,3},{3,2},{4,5},{5,4},{6,7},{7,6},{8,9},{9,8},{10,11... | collective-permute-start | bytes 393224 | tf_op jit(solution)/shard_map/ppermute | solution.py:23
  37.1 12.5 %collective-permute-start.18 = (bf16[128,512]{1,0:T(8,128)(2,1)S(1)}, bf16[128,512]{1,0:T(8,128)(2,1)S(1)}, u32[]{:S(2)}, u32[]{:S(2)}) collective-permute-start(bf16[128,512]{1,0:T(8,128)(2,1)S(1)} %collective-permute-done.17.refs_7_), channel_id=1, source_target_pairs={{0,1},{1,0},{2,3},{3,2},{4,5},{5,4},{6,7},{7,6},{8,9},{9,8},{10,11... | collective-permute-start | bytes 393224 | tf_op jit(solution)/shard_map/ppermute | solution.py:23
  44.3 3.2 %copy-start = (bf16[256,512]{1,0:T(8,128)(2,1)S(1)}, bf16[256,512]{1,0:T(8,128)(2,1)}, u32[]{:S(2)}) copy-start(bf16[256,512]{1,0:T(8,128)(2,1)} %cot_r.3) | copy-start | bytes 786436
  51.6 5.5 %collective-permute-start.19 = (bf16[32,512]{1,0:T(8,128)(2,1)S(1)}, bf16[32,512]{1,0:T(8,128)(2,1)S(1)}, u32[]{:S(2)}, u32[]{:S(2)}) collective-permute-start(bf16[32,512]{1,0:T(8,128)(2,1)S(1)} %get-tuple-element.74), channel_id=1, source_target_pairs={{0,12},{2,14},{4,8},{6,10},{8,4},{10,6},{12,0},{14,2},{16,28},{18,... | collective-permute-start | bytes 98312 | tf_op jit(solution)/shard_map/ppermute | solution.py:18
  53.5 3.9 %collective-permute-start.20 = (bf16[32,512]{1,0:T(8,128)(2,1)S(1)}, bf16[32,512]{1,0:T(8,128)(2,1)S(1)}, u32[]{:S(2)}, u32[]{:S(2)}) collective-permute-start(bf16[32,512]{1,0:T(8,128)(2,1)S(1)} %get-tuple-element.75), channel_id=1, source_target_pairs={{0,8},{2,10},{4,12},{6,14},{8,0},{10,2},{12,4},{14,6},{16,24},{18,... | collective-permute-start | bytes 98312 | tf_op jit(solution)/shard_map/ppermute | solution.py:18
  54.6 3.9 %collective-permute-start.21 = (bf16[32,512]{1,0:T(8,128)(2,1)S(1)}, bf16[32,512]{1,0:T(8,128)(2,1)S(1)}, u32[]{:S(2)}, u32[]{:S(2)}) collective-permute-start(bf16[32,512]{1,0:T(8,128)(2,1)S(1)} %get-tuple-element.76), channel_id=1, source_target_pairs={{0,4},{2,6},{4,0},{6,2},{8,12},{10,14},{12,8},{14,10},{16,20},{18,... | collective-permute-start | bytes 98312 | tf_op jit(solution)/shard_map/ppermute | solution.py:18
